TPU v7x, 32 devices: a whole 2x2x4 slice. The times are simulated.
32 devices in a mesh: groups: 2 (over y), tx: 4 (over z), ty: 2 (over x), pb: 2 (over core).
Axes of the slice: x: 2, y: 2, z: 4, core: 2. Of those that a mesh axis runs over, the one named last changes fastest.
Arguments:
- displacement: float32 [6, 256, 256], P(None, ('tx', 'pb'), 'ty'), may hold values from -3 to 3
- direction: float32 [6, 256, 256], P(None, ('tx', 'pb'), 'ty'), may hold values from -3 to 3
- load: float32 [6, 256, 256], P(None, ('tx', 'pb'), 'ty'), may hold values from -6 to 6
- w_in: bfloat16 [256, 12], replicated, may hold values from -1.75 to 1.75
- b_in: float32 [256], replicated, may hold values from -3 to 3
- w_mid: bfloat16 [256, 256], replicated, may hold values from -0.375 to 0.375
- b_mid: float32 [256], replicated, may hold values from -3 to 3
- w_out: bfloat16 [12, 256], replicated, may hold values from -0.375 to 0.375
- fitting_disp: float32 [6, 4096], P(None, ('groups', 'tx', 'ty', 'pb')), parts along dimension 1, may hold values from -3 to 3
- fitting_dir: float32 [6, 4096], P(None, ('groups', 'tx', 'ty', 'pb')), parts along dimension 1, may hold values from -3 to 3
- tie_node: int32 [24576], P(('groups', 'tx', 'ty', 'pb')), parts along dimension 0, may hold values from 0 to 4095
- tie_owner: int32 [24576, 1], P(('groups', 'tx', 'ty', 'pb')), parts along dimension 0, may hold values from 0 to 7; in each aligned block of 768 rows (0 to 767, 768 to 1535, ...) at most 288 rows name the same one
- tie_slot: int32 [24576], P(('groups', 'tx', 'ty', 'pb')), parts along dimension 0, may hold values from 0 to 127
Outputs:
- node_residual: float32 [6, 512, 256], P(None, ('groups', 'tx', 'pb'), 'ty'), parts along dimension 1
- node_tangent: float32 [6, 512, 256], P(None, ('groups', 'tx', 'pb'), 'ty'), parts along dimension 1
- fitting_residual: float32 [6, 4096], P(None, ('groups', 'tx', 'ty', 'pb')), parts along dimension 1
- fitting_tangent: float32 [6, 4096], P(None, ('groups', 'tx', 'ty', 'pb')), parts along dimension 1
There are 2 independent parts, one for each index of `groups`. A program takes and returns all parts, laid end to end along the dimension named above; an argument that names none is the same for every part. Nothing has to cross between parts.
Inputs may be any that keep to these rules, and one draw needn't show every extreme that they name: `tie_owner`: in each aligned block of 768 ties (the ties of one device) no owner is named more than 288 times, a bound that some block reaches.
All inputs are finite; a program needn't handle non-finite values.
Results may differ from a plain program's by a relative error of at most 0.0003.
Values sent between devices are 32-bit elements; how exact they have to be, the bound alone decides.
No kernel may reach another device: no remote copies, remote signals or barrier semaphores. Data moves between devices by JAX's collectives and lax.ppermute only.
A program may use at most 64 MiB of HBM per device.

v0:
```python
import math

import jax
import jax.numpy as jnp
from jax import lax
from jax.experimental import pallas as pl
from jax.experimental.pallas import tpu as pltpu
from jax.sharding import PartitionSpec as P

F32 = jnp.float32
BF16 = jnp.bfloat16
GAUSS = (0.5 - 0.5 / math.sqrt(3.0), 0.5 + 0.5 / math.sqrt(3.0))
COMPS = 16
COUNT_ROW = 6
SPARE_ROWS = (6, 7, 14)
GROUP = 3


def dot(a, b, dims=((1,), (0,))):
    return lax.dot_general(a, b, (dims, ((), ())), preferred_element_type=F32)


def split(value, terms):
    parts = []
    for _ in range(terms):
        part = value.astype(BF16)
        parts.append(part)
        value = value - part.astype(F32)
    return parts


def rows_of(value):
    return lax.broadcasted_iota(jnp.int32, value, 0)


def lanes_of(value):
    return lax.broadcasted_iota(jnp.int32, value, 1)


def one_hot(index, size):
    shape = (size, index.shape[1])
    return (rows_of(shape) == index).astype(F32).astype(BF16)


def as_line(ref):
    return jnp.concatenate([ref[row : row + 1, :] for row in range(ref.shape[0])], axis=1)


def paired(top, bottom):
    spare = jnp.zeros((2, top.shape[1]), F32)
    return jnp.concatenate([top, spare, bottom, spare], axis=0)


def strain_tile(f00, f10, f01, f11):
    along_low = f10 - f00
    along_high = f11 - f01
    across_low = f01 - f00
    across_high = f11 - f10
    shape = f00.shape
    row = rows_of(shape)
    ones = ((row == 6) | (row == 7) | (row == 14)).astype(F32)
    groups = []
    for frac in GAUSS:
        groups.append((((1.0 - frac) * along_low + frac * along_high) + ones).astype(BF16))
    for frac in GAUSS:
        groups.append(((1.0 - frac) * across_low + frac * across_high).astype(BF16))
    return jnp.concatenate(groups, axis=0)


def stress_sums(strains, w_first, w_mid, b_mid, w_last):
    hid = w_mid.shape[0]
    tasks = [(tile, point) for tile in range(len(strains)) for point in range(4)]
    totals = [[None, None] for _ in strains]

    def layer_one(task):
        tile, point = task
        start = point * 2 * hid
        return (
            dot(w_first[start : start + hid, :], strains[tile]),
            dot(w_first[start + hid : start + 2 * hid, :], strains[tile]),
        )

    def activate(value, slope):
        act = jnp.tanh(value)
        return (act.astype(BF16), ((1.0 - act * act) * slope).astype(BF16))

    def layer_two(hidden):
        bias = b_mid[...]
        value = dot(w_mid[...], hidden[0])
        slope = dot(w_mid[...], hidden[1])
        bias = jnp.concatenate([bias] * (value.shape[1] // bias.shape[1]), axis=1)
        return (value + bias, slope)

    def layer_three(task, hidden):
        tile, point = task
        last = w_last[point * 32 : (point + 1) * 32, :]
        for side in range(2):
            part = dot(last, hidden[side])
            old = totals[tile][side]
            totals[tile][side] = part if old is None else old + part

    ones = {0: layer_one(tasks[0])}
    twos = {}
    for at in range(len(tasks) + 1):
        if at + 1 < len(tasks):
            ones[at + 1] = layer_one(tasks[at + 1])
        if at < len(tasks):
            hidden = activate(*ones.pop(at))
            twos[at] = layer_two(hidden)
        if at >= 1:
            layer_three(tasks[at - 1], activate(*twos.pop(at - 1)))
    return totals


def corner_forces(primal, tangent):
    def both(group):
        return jnp.concatenate([primal[group * 8 : group * 8 + 8], tangent[group * 8 : group * 8 + 8]], axis=0)

    along = (both(0), both(1))
    across = (both(2), both(3))

    def mix(pair, weights):
        return (0.25 * weights[0]) * pair[0] + (0.25 * weights[1]) * pair[1]

    rest = (1.0 - GAUSS[0], 1.0 - GAUSS[1])
    along_rest = mix(along, rest)
    along_frac = mix(along, GAUSS)
    across_rest = mix(across, rest)
    across_frac = mix(across, GAUSS)
    return (
        -along_rest - across_rest,
        along_rest - across_frac,
        across_rest - along_frac,
        along_frac + across_frac,
    )


def block_of(row_place, across, ty_count, pb_count):
    return (row_place // pb_count * ty_count + across) * pb_count + row_place % pb_count


def prepare(axes, *refs):
    (disp, dirn, fit_disp, fit_dir, node_ref, owner_ref, slot_ref, w_in, b_in, b_mid, w_out) = refs[:11]
    (fields, ties, w_first, w_last, b_cols, col_out, pay) = refs[11:]
    tx_count, ty_count, pb_count = axes
    row_total = fields.shape[0] // COMPS
    cols = fields.shape[1]
    slots = fit_disp.shape[1]
    tie_total = ties.shape[1]
    hid = w_in.shape[1]
    core = lax.axis_index("pb")
    across = lax.axis_index("ty")
    place = lax.axis_index("tx") * pb_count + core

    fields[...] = jnp.zeros(fields.shape, F32)
    for comp in range(6):
        fields[pl.ds(comp, row_total, stride=COMPS), :] = disp[comp * row_total : (comp + 1) * row_total, :]
        fields[pl.ds(8 + comp, row_total, stride=COMPS), :] = dirn[comp * row_total : (comp + 1) * row_total, :]

    lane = lanes_of((COMPS, cols))
    for side, column in enumerate((0, cols - 1)):
        gathered = jnp.zeros((COMPS, cols), F32)
        for row in range(row_total):
            value = fields[row * COMPS : (row + 1) * COMPS, column : column + 1]
            gathered = jnp.where(lane == row, value, gathered)
        col_out[side * COMPS : (side + 1) * COMPS, :] = gathered

    bias_rows = split(b_in[...], 3)
    row = rows_of((8, hid))
    stacked = jnp.zeros((8, hid), F32)
    mid_stacked = jnp.zeros((8, hid), F32)
    for at, (one, two) in enumerate(zip(bias_rows, split(b_mid[...], 3))):
        stacked = jnp.where(row == at, one.astype(F32), stacked)
        mid_stacked = jnp.where(row == at, two.astype(F32), mid_stacked)
    lhs = jnp.concatenate([w_in[...].astype(F32), jnp.zeros((4, hid), F32), stacked], axis=0).astype(BF16)
    sel_shape = (24, 4 * COMPS)
    source = rows_of(sel_shape)
    target = lanes_of(sel_shape)
    for point in range(4):
        a_base = (point // 2) * COMPS
        c_base = (2 + point % 2) * COMPS
        for side in range(2):
            hit = (source < 6) & (target == a_base + 8 * side + source)
            hit = hit | ((source >= 6) & (source < 12) & (target == c_base + 8 * side + source - 6))
            if side == 0:
                for at, spot in enumerate((6, 7, 14)):
                    hit = hit | ((source == 16 + at) & (target == a_base + spot))
            block = dot(lhs, hit.astype(F32).astype(BF16), ((0,), (0,)))
            start = (2 * point + side) * hid
            w_first[start : start + hid, :] = block.astype(BF16)
    ones = (rows_of((8, 128)) < 3).astype(F32).astype(BF16)
    b_cols[...] = dot(mid_stacked.astype(BF16), ones, ((0,), (0,)))
    last_shape = (128, 12)
    target = rows_of(last_shape)
    source = lanes_of(last_shape)
    hit = target < 0
    for point in range(4):
        a_base = point * 32 + (point // 2) * 8
        c_base = point * 32 + 16 + (point % 2) * 8
        hit = hit | ((source < 6) & (target == a_base + source))
        hit = hit | ((source >= 6) & (target == c_base + source - 6))
    w_last[...] = dot(hit.astype(F32).astype(BF16), w_out[...]).astype(BF16)

    node = as_line(node_ref)
    slot = as_line(slot_ref)
    owner = owner_ref[...]
    node_row = lax.shift_right_logical(node, cols.bit_length() - 1)
    node_col = jnp.bitwise_and(node, cols - 1)
    hot_col = one_hot(node_col, cols)
    wide = dot(
        jnp.concatenate(split(fields[...], 3), axis=1), jnp.concatenate([hot_col] * 3, axis=0)
    )
    value = jnp.zeros((COMPS, tie_total), F32)
    for row in range(row_total):
        value = jnp.where(node_row == row, wide[row * COMPS : (row + 1) * COMPS], value)
    value = jnp.where(rows_of(value.shape) == COUNT_ROW, 1.0, value)
    ties[...] = value
    stack = jnp.concatenate(split(value, 3), axis=0)
    hot_slot = one_hot(slot, slots)
    fitting = paired(fit_disp[...], fit_dir[...])

    def bins(first, count):
        lhs = [
            stack * (owner == first + at).astype(F32).astype(BF16) for at in range(count)
        ]
        return dot(jnp.concatenate(lhs, axis=0), hot_slot, ((1,), (1,)))

    def folded(wide_bins, at):
        part = wide_bins[at * 48 : at * 48 + 48]
        return part[0:16] + part[16:32] + part[32:48]

    peers = tx_count * ty_count
    block = math.gcd(peers, 8)

    def fill(first):
        wide_bins = bins(first, block)
        for peer in range(block):
            at = (first + peer) * pb_count + core
            pay[at, 0:COMPS, :] = fitting
            pay[at, COMPS : 2 * COMPS, :] = folded(wide_bins, peer)

    if block == peers:
        fill(0)
    else:
        lax.fori_loop(0, peers // block, lambda at, carry: (fill(at * block), carry)[1], 0)

    for step, edge in ((-1, fields[0:COMPS, :]), (1, fields[(row_total - 1) * COMPS :, :])):
        for side in (-1, 0, 1):
            there, over = place + step, across + side
            valid = (there >= 0) & (there < tx_count * pb_count) & (over >= 0) & (over < ty_count)

            @pl.when(valid)
            def _():
                pay[block_of(there, over, ty_count, pb_count), 0:COMPS, :] = edge

    for side, edge in ((-1, 0), (1, 1)):
        over = across + side
        packed = pack_column(col_out[edge * COMPS : (edge + 1) * COMPS, :], row_total)

        @pl.when((over >= 0) & (over < ty_count))
        def _():
            at = block_of(place, over, ty_count, pb_count)
            for line, row in zip(packed, SPARE_ROWS):
                pay[at, row : row + 1, :] = line


def pack_column(column, width):
    each = column.shape[1] // width
    lines = []
    for first in range(0, 12, each):
        line = None
        for at in range(first, min(first + each, 12)):
            row = at % 6 + at // 6 * 8
            part = column[row : row + 1]
            if at > first:
                part = pltpu.roll(part, (at - first) * width, 1)
            line = part if line is None else line + part
        lines.append(line)
    assert len(lines) <= len(SPARE_ROWS)
    return lines


def unpack_column(block, width):
    shape = (COMPS, block.shape[1])
    each = shape[1] // width
    row = rows_of(shape)
    column = jnp.zeros(shape, F32)
    for at in range(12):
        spare = SPARE_ROWS[at // each]
        line = block[spare : spare + 1]
        if at % each:
            line = pltpu.roll(line, shape[1] - at % each * width, 1)
        column = jnp.where(row == at % 6 + at // 6 * 8, line, column)
    return jnp.where(lanes_of(shape) < width, column, 0.0)


def interior(fields, w_first, w_mid, b_mid, w_last, forces, strain):
    row_total, cols = fields.shape[0] // COMPS, fields.shape[1]
    pairs = (row_total - 1) // 2
    group = next(size for size in (GROUP, 3, 2, 1) if pairs % size == 0)
    keep = lanes_of((COMPS, cols)) < cols - 1

    def row_strain(row):
        base = fields[pl.ds(row * COMPS, COMPS), :]
        right = fields[pl.ds(row * COMPS + COMPS, COMPS), :]
        return strain_tile(base, right, pltpu.roll(base, cols - 1, 1), pltpu.roll(right, cols - 1, 1))

    def build(pair, carry):
        strain[pair] = jnp.concatenate([row_strain(2 * pair), row_strain(2 * pair + 1)], axis=1)
        return carry

    lax.fori_loop(0, pairs, build, 0)
    forces[...] = jnp.zeros(forces.shape, F32)

    def step(pair, carry):
        start = pair * group
        sums = stress_sums([strain[start + at] for at in range(group)], w_first, w_mid, b_mid, w_last)
        for tile, (primal, tangent) in enumerate(sums):
            for half in range(2):
                lanes = slice(half * cols, (half + 1) * cols)
                parts = corner_forces(primal[:, lanes], tangent[:, lanes])
                base, right, upper, corner = (jnp.where(keep, part, 0.0) for part in parts)
                at = (2 * (start + tile) + half) * COMPS
                forces[pl.ds(at, COMPS), :] += base + pltpu.roll(upper, 1, 1)
                forces[pl.ds(at + COMPS, COMPS), :] += right + pltpu.roll(corner, 1, 1)
        return carry

    lax.fori_loop(0, pairs // group, step, 0)


def finish(names, axes, *refs):
    ref = dict(zip(names, refs))
    tx_count, ty_count, pb_count = axes
    fields, ties, forces_in, load = ref["fields"], ref["ties"], ref["forces"], ref["load"]
    scratch, got = ref["scratch"], ref["got"]
    row_total, cols = fields.shape[0] // COMPS, fields.shape[1]
    slots = got.shape[2]
    tie_total = ties.shape[1]
    lane = lanes_of((COMPS, cols))
    core = lax.axis_index("pb")
    across = lax.axis_index("ty")
    place = lax.axis_index("tx") * pb_count + core

    def around(step, side):
        there, over = place + step, across + side
        valid = (there >= 0) & (there < tx_count * pb_count) & (over >= 0) & (over < ty_count)
        at = jnp.where(valid, block_of(there, over, ty_count, pb_count), 0)
        value = got[at, 0:COMPS, :]
        if step == 0:
            value = unpack_column(value, row_total)
        return jnp.where(valid, value, 0.0)

    prev_row = around(-1, 0)
    next_row = around(1, 0)
    next_col = around(0, 1)
    prev_col = around(0, -1)
    next_corner = (around(-1, 1)[:, 0:1], around(1, 1)[:, 0:1])
    prev_corner = (around(-1, -1)[:, cols - 1 : cols], around(1, -1)[:, cols - 1 : cols])

    def column(inner, before, after):
        line = pltpu.roll(inner, 1, 1)
        line = jnp.where(lane == 0, before, line)
        return jnp.where(lane == row_total + 1, after, line)

    own_cols = ref["cols"]
    line_prev = column(prev_col, prev_corner[0], prev_corner[1])
    line_next = column(next_col, next_corner[0], next_corner[1])
    line_first = column(own_cols[0:COMPS, :], prev_row[:, 0:1], next_row[:, 0:1])
    line_final = column(
        own_cols[COMPS : 2 * COMPS, :], prev_row[:, cols - 1 : cols], next_row[:, cols - 1 : cols]
    )

    def shifted(row_value, beyond):
        return jnp.where(lane == cols - 1, beyond, pltpu.roll(row_value, cols - 1, 1))

    first_row = fields[0:COMPS, :]
    last_row = fields[(row_total - 1) * COMPS :, :]
    inner_row = fields[(row_total - 2) * COMPS : (row_total - 1) * COMPS, :]

    tile_inner = strain_tile(
        inner_row, last_row, pltpu.roll(inner_row, cols - 1, 1), pltpu.roll(last_row, cols - 1, 1)
    )
    tile_before = strain_tile(
        prev_row,
        first_row,
        shifted(prev_row, next_corner[0]),
        shifted(first_row, next_col[:, 0:1]),
    )
    tile_after = strain_tile(
        last_row,
        next_row,
        shifted(last_row, next_col[:, row_total - 1 : row_total]),
        shifted(next_row, next_corner[1]),
    )
    half = cols // 2
    low = lane < half
    back = cols - 1

    def two(left, right_line):
        return jnp.where(low, left, pltpu.roll(right_line, half + back, 1))

    left_base = two(line_prev, line_final)
    left_upper = two(line_first, line_next)
    right_base = two(pltpu.roll(line_prev, back, 1), pltpu.roll(line_final, back, 1))
    right_upper = two(pltpu.roll(line_first, back, 1), pltpu.roll(line_next, back, 1))
    tile_side = strain_tile(left_base, right_base, left_upper, right_upper)

    parts = []
    edge_tiles = [jnp.concatenate(pair, axis=1) for pair in ((tile_inner, tile_before), (tile_after, tile_side))]
    edge_sums = stress_sums(edge_tiles, ref["w_first"], ref["w_mid"], ref["b_mid"], ref["w_last"])
    for primal, tangent in edge_sums:
        for at in range(2):
            lanes = slice(at * cols, (at + 1) * cols)
            parts.append(corner_forces(primal[:, lanes], tangent[:, lanes]))
    part_inner, part_before, part_after, part_side = parts

    def mask(value, keep):
        return jnp.where(keep, value, 0.0)

    def moved(value, keep):
        return pltpu.roll(mask(value, keep), 1, 1)

    inside = lane < cols - 1
    i_base, i_right, i_upper, i_corner = part_inner
    _, b_right, _, b_corner = part_before
    a_base, _, a_upper, _ = part_after
    s_base, s_right, s_upper, s_corner = part_side
    has_row = place > 0
    has_col = across > 0
    row_first = mask(mask(b_right, lane < cols) + moved(b_corner, inside), has_row)
    row_inner = mask(i_base, inside) + moved(i_upper, inside)
    row_last = mask(i_right, inside) + moved(i_corner, inside) + a_base + moved(a_upper, inside)
    first_lane = jnp.where(has_row, 0, 1)
    s_corner = mask(s_corner, (lane >= first_lane) & (lane < row_total))
    s_upper = mask(s_upper, (lane >= 1) & (lane <= row_total))
    col_first = mask(pltpu.roll(s_upper, back, 1) + s_corner, has_col)
    s_base = mask(s_base, (lane >= half) & (lane < half + row_total - 1))
    s_right = mask(s_right, (lane >= half) & (lane < half + row_total - 1))
    col_last = pltpu.roll(s_base + pltpu.roll(s_right, 1, 1), cols - half, 1)

    node = as_line(ref["node"])
    slot = as_line(ref["slot"])
    owner = ref["owner"][...]
    hot_slot = one_hot(slot, slots)
    hot_three = jnp.concatenate([hot_slot] * 3, axis=0)
    fit_value = jnp.zeros((COMPS, tie_total), F32)
    bins = jnp.zeros((COMPS, slots), F32)
    peers = tx_count * ty_count
    block = math.gcd(peers, 8)

    def collect(first, carry):
        fit_value, bins = carry
        parts = [got[(first + peer) * pb_count + core] for peer in range(block)]
        fit_all = jnp.concatenate([part[0:COMPS] for part in parts], axis=0)
        wide = dot(jnp.concatenate(split(fit_all, 3), axis=1), hot_three)
        for peer, part in enumerate(parts):
            fit_value = jnp.where(owner == first + peer, wide[peer * COMPS : (peer + 1) * COMPS], fit_value)
            bins = bins + part[COMPS : 2 * COMPS]
        return fit_value, bins

    if block == peers:
        fit_value, bins = collect(0, (fit_value, bins))
    else:
        fit_value, bins = lax.fori_loop(
            0, peers // block, lambda at, carry: collect(at * block, carry), (fit_value, bins)
        )
    count = bins[COUNT_ROW : COUNT_ROW + 1]
    for out, fit, base in (("fit_res", "fit_disp", 0), ("fit_tan", "fit_dir", 8)):
        ref[out][...] = 2.0 * (count * ref[fit][...] - bins[base : base + 6])

    pulled = 2.0 * (ties[...] - fit_value)
    node_row = lax.shift_right_logical(node, cols.bit_length() - 1)
    node_col = jnp.bitwise_and(node, cols - 1)
    hot_col = one_hot(node_col, cols)
    sides = split(pulled, 2)
    lhs = []
    for row in range(row_total):
        hit = (node_row == row).astype(F32).astype(BF16)
        lhs.append(jnp.concatenate([side * hit for side in sides], axis=1))
    tie_forces = dot(
        jnp.concatenate(lhs, axis=0), jnp.concatenate([hot_col] * 2, axis=1), ((1,), (1,))
    )

    for row in range(row_total):
        total = forces_in[row * COMPS : (row + 1) * COMPS, :] + tie_forces[row * COMPS : (row + 1) * COMPS]
        total = total + jnp.where(lane == 0, col_first[:, row : row + 1], 0.0)
        total = total + jnp.where(lane == cols - 1, col_last[:, row : row + 1], 0.0)
        if row == 0:
            total = total + row_first
        if row == row_total - 2:
            total = total + row_inner
        if row == row_total - 1:
            total = total + row_last
        scratch[row * COMPS : (row + 1) * COMPS, :] = total
    for comp in range(6):
        rows = slice(comp * row_total, (comp + 1) * row_total)
        ref["res"][rows, :] = scratch[pl.ds(comp, row_total, stride=COMPS), :] - load[rows, :]
        ref["tan"][rows, :] = scratch[pl.ds(8 + comp, row_total, stride=COMPS), :]


def per_device(
    displacement,
    direction,
    load,
    w_in,
    b_in,
    w_mid,
    b_mid,
    w_out,
    fitting_disp,
    fitting_dir,
    tie_node,
    tie_owner,
    tie_slot,
):
    tx_count = lax.axis_size("tx")
    ty_count = lax.axis_size("ty")
    pb_count = lax.axis_size("pb")
    peers = tx_count * ty_count
    axes = (tx_count, ty_count, pb_count)
    _, row_total, cols = displacement.shape
    slots = fitting_disp.shape[1]
    tie_total = tie_node.shape[0]
    hid = w_mid.shape[0]
    flat = (6 * row_total, cols)
    disp2 = displacement.reshape(flat)
    dir2 = direction.reshape(flat)
    load2 = load.reshape(flat)
    node2 = tie_node.reshape(tie_total // 128, 128)
    slot2 = tie_slot.reshape(tie_total // 128, 128)
    owner2 = tie_owner.reshape(1, tie_total)

    def shape(*dims, dtype=F32):
        return jax.ShapeDtypeStruct(dims, dtype)

    outs = pl.pallas_call(
        lambda *refs: prepare(axes, *refs),
        out_shape=[
            shape(row_total * COMPS, cols),
            shape(COMPS, tie_total),
            shape(8 * hid, 4 * COMPS, dtype=BF16),
            shape(128, hid, dtype=BF16),
            shape(hid, 128),
            shape(2 * COMPS, cols),
            shape(peers * pb_count, 2 * COMPS, slots),
        ],
        name="prepare",
    )(
        disp2,
        dir2,
        fitting_disp,
        fitting_dir,
        node2,
        owner2,
        slot2,
        w_in.T,
        b_in.reshape(1, hid),
        b_mid.reshape(1, hid),
        w_out,
    )
    fields, ties, w_first, w_last, b_cols, cols_out, pay = outs
    got = lax.all_to_all(pay, ("tx", "ty", "pb"), split_axis=0, concat_axis=0, tiled=True)

    forces = pl.pallas_call(
        interior,
        out_shape=shape(row_total * COMPS, cols),
        scratch_shapes=[pltpu.VMEM(((row_total - 1) // 2, 4 * COMPS, 2 * cols), BF16)],
        name="interior",
    )(fields, w_first, w_mid, b_cols, w_last)

    named = dict(
        got=got,
        fields=fields,
        ties=ties,
        forces=forces,
        load=load2,
        cols=cols_out,
        w_first=w_first,
        w_mid=w_mid,
        b_mid=b_cols,
        w_last=w_last,
        node=node2,
        slot=slot2,
        owner=owner2,
        fit_disp=fitting_disp,
        fit_dir=fitting_dir,
    )
    names = list(named)
    res, tan, fit_res, fit_tan = pl.pallas_call(
        lambda *refs: finish(names + ["res", "tan", "fit_res", "fit_tan", "scratch"], axes, *refs),
        out_shape=[shape(*flat), shape(*flat), shape(6, slots), shape(6, slots)],
        scratch_shapes=[pltpu.VMEM((row_total * COMPS, cols), F32)],
        name="finish",
    )(*named.values())
    cube = displacement.shape
    return (res.reshape(cube), tan.reshape(cube), fit_res, fit_tan)


def solution(mesh):
    in_specs = (
        P(None, ("tx", "pb"), "ty"),
        P(None, ("tx", "pb"), "ty"),
        P(None, ("tx", "pb"), "ty"),
        P(),
        P(),
        P(),
        P(),
        P(),
        P(None, ("groups", "tx", "ty", "pb")),
        P(None, ("groups", "tx", "ty", "pb")),
        P(("groups", "tx", "ty", "pb")),
        P(("groups", "tx", "ty", "pb"), None),
        P(("groups", "tx", "ty", "pb")),
    )
    out_specs = (
        P(None, ("groups", "tx", "pb"), "ty"),
        P(None, ("groups", "tx", "pb"), "ty"),
        P(None, ("groups", "tx", "ty", "pb")),
        P(None, ("groups", "tx", "ty", "pb")),
    )
    return jax.shard_map(
        per_device, mesh=mesh, in_specs=in_specs, out_specs=out_specs, check_vma=False
    )
```

profile of v0, /device:TPU:0, one launch (start us, length us, event | category | flops | bytes accessed | tf_op | source)
XLA Modules:
  0.0 31.9 jit_solution(7932786497754085943)
XLA Ops:
  0.6 3.7 %prepare.1 = (f32[512,128]{1,0:T(8,128)}, f32[16,768]{1,0:T(8,128)}, bf16[2048,64]{1,0:T(8,128)(2,1)}, bf16[128,256]{1,0:T(8,128)(2,1)}, f32[256,128]{1,0:T(8,12...) custom-call(f32[192,128]{1,0:T(8,128)} %bitcast.11, f32[192,128]{1,0:T(8,128)} %bitcast.12, f32[6,128]{1,0:T(8,128)} %refs_13_.1, ...), custom_call_target="tpu_custom_call" | custom-call | tf_op jit(solution)/shard_map/prepare/pallas_call | solution.py:536
  4.3 7.4 %all-to-all-start = ((f32[16,32,128]{2,1,0:T(8,128)}), f32[16,32,128]{2,1,0:T(8,128)S(1)}, u32[]{:S(2)}, u32[]{:S(2)}) async-start(f32[16,32,128]{2,1,0:T(8,128)} %get-tuple-element.15), calls=%async_computation | async-start | bytes 524288 | tf_op jit(solution)/shard_map/all_to_all | solution.py:562
  11.7 14.9 %interior.1.refs_3_ = f32[512,128]{1,0:T(8,128)} custom-call(f32[512,128]{1,0:T(8,128)} %get-tuple-element.16.fields.refs_1_, bf16[2048,64]{1,0:T(8,128)(2,1)} %get-tuple-element.18.w_first.refs_6_, bf16[256,256]{1,0:T(8,128)(2,1)} %refs_7_.1, f32[256,128]{1,0:T(8,128)} %get-tuple-element.19.b_mid.refs_8_, bf16[128,256]{1,0:T(8,128)(2,1)} %get-tuple-element.20.w_last.refs_9_), custom_call_target="tpu_custom_call" | custom-call | tf_op jit(solution)/shard_map/interior/pallas_call | solution.py:564
  26.6 0.0 all-to-all-done.refs_0_
  26.6 0.0 copy-start
  26.6 0.7 %copy-done = f32[16,32,128]{2,1,0:T(8,128)} copy-done((f32[16,32,128]{2,1,0:T(8,128)}, f32[16,32,128]{2,1,0:T(8,128)S(1)}, u32[]{:S(2)}) %copy-start) | copy-done | bytes 262168
  27.3 4.6 %finish.1 = (f32[192,128]{1,0:T(8,128)}, f32[192,128]{1,0:T(8,128)}, f32[6,128]{1,0:T(8,128)}, f32[6,128]{1,0:T(8,128)}) custom-call(f32[16,32,128]{2,1,0:T(8,128)} %copy-done, f32[512,128]{1,0:T(8,128)} %get-tuple-element.16.fields.refs_1_, f32[16,768]{1,0:T(8,128)} %get-tuple-element.17.refs_2_, f32[512,128]{1,0:T(8,128)} %interior.1.refs_3_, ...), custom_call_target="tpu_custom_call" | custom-call | tf_op jit(solution)/shard_map/finish/pallas_call | solution.py:589
Async XLA Ops:
  4.3 22.3 %all-to-all-start = ((f32[16,32,128]{2,1,0:T(8,128)}), f32[16,32,128]{2,1,0:T(8,128)S(1)}, u32[]{:S(2)}, u32[]{:S(2)}) async-start(f32[16,32,128]{2,1,0:T(8,128)} %get-tuple-element.15), calls=%async_computation | async-start | bytes 524288 | tf_op jit(solution)/shard_map/all_to_all | solution.py:562
  26.6 0.7 %copy-start = (f32[16,32,128]{2,1,0:T(8,128)}, f32[16,32,128]{2,1,0:T(8,128)S(1)}, u32[]{:S(2)}) copy-start(f32[16,32,128]{2,1,0:T(8,128)S(1)} %all-to-all-done.refs_0_) | copy-start | bytes 786436
where the time goes:
time: 32.2 us; the launch traced here: 31.9 us
  Pallas kernels  23.2 us (72%)
  starting transfers between devices  7.39 us (23%)
  local copies, waits for them, and re-layouts  0.7 us (2%)
  between operations  0.64 us (2%)
    pallas_call x1, Pallas kernels, per_device(): pl.pallas_call(interior, out_shape=shape(row_total * COMPS, cols), scratc...  14.9 us
    all_to_all x1, starting transfers between devices, per_device(): lax.all_to_all(pay, ('tx', 'ty', 'pb'), split_axis=0, concat_axis=0, tile...  7.39 us
    pallas_call x1, Pallas kernels, per_device(): pl.pallas_call(lambda *refs: finish(names + ['res', 'tan', 'fit_res', 'fi...  4.61 us
    pallas_call x1, Pallas kernels, per_device(): pl.pallas_call(lambda *refs: prepare(axes, *refs), out_shape=[shape(row_t...  3.65 us
    unnamed x2, local copies, waits for them, and re-layouts  0.7 us
  transfers between devices with their start and end apart: 1, of which 0 were waited for; matrix products, arithmetic and copies ran while one was open for 0% of the time, Pallas kernels for 47%

commit v1 on v0

--- a/solution.py
+++ b/solution.py
@@ -13,7 +13,11 @@
 COMPS = 16
 COUNT_ROW = 6
 SPARE_ROWS = (6, 7, 14)
-GROUP = 3
+GROUP = 5
+
+
+def local(count):
+    return [pl.BlockSpec(memory_space=pltpu.VMEM)] * count
 
 
 def dot(a, b, dims=((1,), (0,))):
@@ -140,14 +144,13 @@
 
 
 def prepare(axes, *refs):
-    (disp, dirn, fit_disp, fit_dir, node_ref, owner_ref, slot_ref, w_in, b_in, b_mid, w_out) = refs[:11]
-    (fields, ties, w_first, w_last, b_cols, col_out, pay) = refs[11:]
+    (disp, dirn, fit_disp, fit_dir, node_ref, owner_ref, slot_ref) = refs[:7]
+    (fields, ties, col_out, pay) = refs[7:]
     tx_count, ty_count, pb_count = axes
     row_total = fields.shape[0] // COMPS
     cols = fields.shape[1]
     slots = fit_disp.shape[1]
     tie_total = ties.shape[1]
-    hid = w_in.shape[1]
     core = lax.axis_index("pb")
     across = lax.axis_index("ty")
     place = lax.axis_index("tx") * pb_count + core
@@ -165,6 +168,101 @@
             gathered = jnp.where(lane == row, value, gathered)
         col_out[side * COMPS : (side + 1) * COMPS, :] = gathered
 
+    node = as_line(node_ref)
+    slot = as_line(slot_ref)
+    owner = owner_ref[...]
+    node_row = lax.shift_right_logical(node, cols.bit_length() - 1)
+    node_col = jnp.bitwise_and(node, cols - 1)
+    hot_col = one_hot(node_col, cols)
+    wide = dot(
+        jnp.concatenate(split(fields[...], 2), axis=1), jnp.concatenate([hot_col] * 2, axis=0)
+    )
+    value = jnp.zeros((COMPS, tie_total), F32)
+    for row in range(row_total):
+        value = jnp.where(node_row == row, wide[row * COMPS : (row + 1) * COMPS], value)
+    value = jnp.where(rows_of(value.shape) == COUNT_ROW, 1.0, value)
+    ties[...] = value
+    stack = jnp.concatenate(split(value, 2), axis=0)
+    hot_slot = one_hot(slot, slots)
+    fitting = paired(fit_disp[...], fit_dir[...])
+
+    def bins(first, count):
+        lhs = [
+            stack * (owner == first + at).astype(F32).astype(BF16) for at in range(count)
+        ]
+        return dot(jnp.concatenate(lhs, axis=0), hot_slot, ((1,), (1,)))
+
+    def folded(wide_bins, at):
+        part = wide_bins[at * 2 * COMPS : (at + 1) * 2 * COMPS]
+        return part[0:COMPS] + part[COMPS : 2 * COMPS]
+
+    peers = tx_count * ty_count
+    block = math.gcd(peers, 8)
+
+    def fill(first):
+        wide_bins = bins(first, block)
+        for peer in range(block):
+            at = (first + peer) * pb_count + core
+            pay[at, 0:COMPS, :] = fitting
+            pay[at, COMPS : 2 * COMPS, :] = folded(wide_bins, peer)
+
+    if block == peers:
+        fill(0)
+    else:
+        lax.fori_loop(0, peers // block, lambda at, carry: (fill(at * block), carry)[1], 0)
+
+    for step, edge in ((-1, fields[0:COMPS, :]), (1, fields[(row_total - 1) * COMPS :, :])):
+        for side in (-1, 0, 1):
+            there, over = place + step, across + side
+            valid = (there >= 0) & (there < tx_count * pb_count) & (over >= 0) & (over < ty_count)
+
+            @pl.when(valid)
+            def _():
+                pay[block_of(there, over, ty_count, pb_count), 0:COMPS, :] = edge
+
+    for side, edge in ((-1, 0), (1, 1)):
+        over = across + side
+        packed = pack_column(col_out[edge * COMPS : (edge + 1) * COMPS, :], row_total)
+
+        @pl.when((over >= 0) & (over < ty_count))
+        def _():
+            at = block_of(place, over, ty_count, pb_count)
+            for line, row in zip(packed, SPARE_ROWS):
+                pay[at, row : row + 1, :] = line
+
+
+def pack_column(column, width):
+    each = column.shape[1] // width
+    lines = []
+    for first in range(0, 12, each):
+        line = None
+        for at in range(first, min(first + each, 12)):
+            row = at % 6 + at // 6 * 8
+            part = column[row : row + 1]
+            if at > first:
+                part = pltpu.roll(part, (at - first) * width, 1)
+            line = part if line is None else line + part
+        lines.append(line)
+    assert len(lines) <= len(SPARE_ROWS)
+    return lines
+
+
+def unpack_column(block, width):
+    shape = (COMPS, block.shape[1])
+    each = shape[1] // width
+    row = rows_of(shape)
+    column = jnp.zeros(shape, F32)
+    for at in range(12):
+        spare = SPARE_ROWS[at // each]
+        line = block[spare : spare + 1]
+        if at % each:
+            line = pltpu.roll(line, shape[1] - at % each * width, 1)
+        column = jnp.where(row == at % 6 + at // 6 * 8, line, column)
+    return jnp.where(lanes_of(shape) < width, column, 0.0)
+
+
+def build_weights(w_in, b_in, b_mid, w_out, w_first, w_last, b_cols):
+    hid = w_in.shape[1]
     bias_rows = split(b_in[...], 3)
     row = rows_of((8, hid))
     stacked = jnp.zeros((8, hid), F32)
@@ -201,126 +299,34 @@
         hit = hit | ((source >= 6) & (target == c_base + source - 6))
     w_last[...] = dot(hit.astype(F32).astype(BF16), w_out[...]).astype(BF16)
 
-    node = as_line(node_ref)
-    slot = as_line(slot_ref)
-    owner = owner_ref[...]
-    node_row = lax.shift_right_logical(node, cols.bit_length() - 1)
-    node_col = jnp.bitwise_and(node, cols - 1)
-    hot_col = one_hot(node_col, cols)
-    wide = dot(
-        jnp.concatenate(split(fields[...], 3), axis=1), jnp.concatenate([hot_col] * 3, axis=0)
-    )
-    value = jnp.zeros((COMPS, tie_total), F32)
-    for row in range(row_total):
-        value = jnp.where(node_row == row, wide[row * COMPS : (row + 1) * COMPS], value)
-    value = jnp.where(rows_of(value.shape) == COUNT_ROW, 1.0, value)
-    ties[...] = value
-    stack = jnp.concatenate(split(value, 3), axis=0)
-    hot_slot = one_hot(slot, slots)
-    fitting = paired(fit_disp[...], fit_dir[...])
-
-    def bins(first, count):
-        lhs = [
-            stack * (owner == first + at).astype(F32).astype(BF16) for at in range(count)
-        ]
-        return dot(jnp.concatenate(lhs, axis=0), hot_slot, ((1,), (1,)))
-
-    def folded(wide_bins, at):
-        part = wide_bins[at * 48 : at * 48 + 48]
-        return part[0:16] + part[16:32] + part[32:48]
-
-    peers = tx_count * ty_count
-    block = math.gcd(peers, 8)
-
-    def fill(first):
-        wide_bins = bins(first, block)
-        for peer in range(block):
-            at = (first + peer) * pb_count + core
-            pay[at, 0:COMPS, :] = fitting
-            pay[at, COMPS : 2 * COMPS, :] = folded(wide_bins, peer)
-
-    if block == peers:
-        fill(0)
-    else:
-        lax.fori_loop(0, peers // block, lambda at, carry: (fill(at * block), carry)[1], 0)
-
-    for step, edge in ((-1, fields[0:COMPS, :]), (1, fields[(row_total - 1) * COMPS :, :])):
-        for side in (-1, 0, 1):
-            there, over = place + step, across + side
-            valid = (there >= 0) & (there < tx_count * pb_count) & (over >= 0) & (over < ty_count)
-
-            @pl.when(valid)
-            def _():
-                pay[block_of(there, over, ty_count, pb_count), 0:COMPS, :] = edge
-
-    for side, edge in ((-1, 0), (1, 1)):
-        over = across + side
-        packed = pack_column(col_out[edge * COMPS : (edge + 1) * COMPS, :], row_total)
-
-        @pl.when((over >= 0) & (over < ty_count))
-        def _():
-            at = block_of(place, over, ty_count, pb_count)
-            for line, row in zip(packed, SPARE_ROWS):
-                pay[at, row : row + 1, :] = line
-
-
-def pack_column(column, width):
-    each = column.shape[1] // width
-    lines = []
-    for first in range(0, 12, each):
-        line = None
-        for at in range(first, min(first + each, 12)):
-            row = at % 6 + at // 6 * 8
-            part = column[row : row + 1]
-            if at > first:
-                part = pltpu.roll(part, (at - first) * width, 1)
-            line = part if line is None else line + part
-        lines.append(line)
-    assert len(lines) <= len(SPARE_ROWS)
-    return lines
-
-
-def unpack_column(block, width):
-    shape = (COMPS, block.shape[1])
-    each = shape[1] // width
-    row = rows_of(shape)
-    column = jnp.zeros(shape, F32)
-    for at in range(12):
-        spare = SPARE_ROWS[at // each]
-        line = block[spare : spare + 1]
-        if at % each:
-            line = pltpu.roll(line, shape[1] - at % each * width, 1)
-        column = jnp.where(row == at % 6 + at // 6 * 8, line, column)
-    return jnp.where(lanes_of(shape) < width, column, 0.0)
-
-
-def interior(fields, w_first, w_mid, b_mid, w_last, forces, strain):
+
+def interior(fields, w_in, b_in, w_mid, b_mid, w_out, forces, w_first, w_last, b_cols):
     row_total, cols = fields.shape[0] // COMPS, fields.shape[1]
     pairs = (row_total - 1) // 2
     group = next(size for size in (GROUP, 3, 2, 1) if pairs % size == 0)
     keep = lanes_of((COMPS, cols)) < cols - 1
-
-    def row_strain(row):
-        base = fields[pl.ds(row * COMPS, COMPS), :]
-        right = fields[pl.ds(row * COMPS + COMPS, COMPS), :]
-        return strain_tile(base, right, pltpu.roll(base, cols - 1, 1), pltpu.roll(right, cols - 1, 1))
-
-    def build(pair, carry):
-        strain[pair] = jnp.concatenate([row_strain(2 * pair), row_strain(2 * pair + 1)], axis=1)
-        return carry
-
-    lax.fori_loop(0, pairs, build, 0)
+    build_weights(w_in, b_in, b_mid, w_out, w_first, w_last, b_cols)
     forces[...] = jnp.zeros(forces.shape, F32)
+
+    def row_of(row):
+        base = fields[pl.ds(pl.multiple_of(row * COMPS, COMPS), COMPS), :]
+        return base, pltpu.roll(base, cols - 1, 1)
 
     def step(pair, carry):
         start = pair * group
-        sums = stress_sums([strain[start + at] for at in range(group)], w_first, w_mid, b_mid, w_last)
+        lines = [row_of(2 * start + at) for at in range(2 * group + 1)]
+        tiles = [
+            strain_tile(lines[at][0], lines[at + 1][0], lines[at][1], lines[at + 1][1])
+            for at in range(2 * group)
+        ]
+        tiles = [jnp.concatenate(tiles[at : at + 2], axis=1) for at in range(0, 2 * group, 2)]
+        sums = stress_sums(tiles, w_first, w_mid, b_cols, w_last)
         for tile, (primal, tangent) in enumerate(sums):
             for half in range(2):
                 lanes = slice(half * cols, (half + 1) * cols)
                 parts = corner_forces(primal[:, lanes], tangent[:, lanes])
                 base, right, upper, corner = (jnp.where(keep, part, 0.0) for part in parts)
-                at = (2 * (start + tile) + half) * COMPS
+                at = pl.multiple_of((2 * (start + tile) + half) * COMPS, COMPS)
                 forces[pl.ds(at, COMPS), :] += base + pltpu.roll(upper, 1, 1)
                 forces[pl.ds(at + COMPS, COMPS), :] += right + pltpu.roll(corner, 1, 1)
         return carry
@@ -442,7 +448,7 @@
     slot = as_line(ref["slot"])
     owner = ref["owner"][...]
     hot_slot = one_hot(slot, slots)
-    hot_three = jnp.concatenate([hot_slot] * 3, axis=0)
+    hot_two = jnp.concatenate([hot_slot] * 2, axis=0)
     fit_value = jnp.zeros((COMPS, tie_total), F32)
     bins = jnp.zeros((COMPS, slots), F32)
     peers = tx_count * ty_count
@@ -452,7 +458,7 @@
         fit_value, bins = carry
         parts = [got[(first + peer) * pb_count + core] for peer in range(block)]
         fit_all = jnp.concatenate([part[0:COMPS] for part in parts], axis=0)
-        wide = dot(jnp.concatenate(split(fit_all, 3), axis=1), hot_three)
+        wide = dot(jnp.concatenate(split(fit_all, 2), axis=1), hot_two)
         for peer, part in enumerate(parts):
             fit_value = jnp.where(owner == first + peer, wide[peer * COMPS : (peer + 1) * COMPS], fit_value)
             bins = bins + part[COMPS : 2 * COMPS]
@@ -533,40 +539,34 @@
     def shape(*dims, dtype=F32):
         return jax.ShapeDtypeStruct(dims, dtype)
 
-    outs = pl.pallas_call(
+    inputs = (disp2, dir2, fitting_disp, fitting_dir, node2, owner2, slot2)
+    fields, ties, cols_out, pay = pl.pallas_call(
         lambda *refs: prepare(axes, *refs),
         out_shape=[
             shape(row_total * COMPS, cols),
             shape(COMPS, tie_total),
+            shape(2 * COMPS, cols),
+            shape(peers * pb_count, 2 * COMPS, slots),
+        ],
+        in_specs=local(len(inputs)),
+        out_specs=local(4),
+        name="prepare",
+    )(*inputs)
+    got = lax.all_to_all(pay, ("tx", "ty", "pb"), split_axis=0, concat_axis=0, tiled=True)
+
+    inputs = (fields, w_in.T, b_in.reshape(1, hid), w_mid, b_mid.reshape(1, hid), w_out)
+    forces, w_first, w_last, b_cols = pl.pallas_call(
+        interior,
+        out_shape=[
+            shape(row_total * COMPS, cols),
             shape(8 * hid, 4 * COMPS, dtype=BF16),
             shape(128, hid, dtype=BF16),
             shape(hid, 128),
-            shape(2 * COMPS, cols),
-            shape(peers * pb_count, 2 * COMPS, slots),
         ],
-        name="prepare",
-    )(
-        disp2,
-        dir2,
-        fitting_disp,
-        fitting_dir,
-        node2,
-        owner2,
-        slot2,
-        w_in.T,
-        b_in.reshape(1, hid),
-        b_mid.reshape(1, hid),
-        w_out,
-    )
-    fields, ties, w_first, w_last, b_cols, cols_out, pay = outs
-    got = lax.all_to_all(pay, ("tx", "ty", "pb"), split_axis=0, concat_axis=0, tiled=True)
-
-    forces = pl.pallas_call(
-        interior,
-        out_shape=shape(row_total * COMPS, cols),
-        scratch_shapes=[pltpu.VMEM(((row_total - 1) // 2, 4 * COMPS, 2 * cols), BF16)],
+        in_specs=local(len(inputs)),
+        out_specs=local(4),
         name="interior",
-    )(fields, w_first, w_mid, b_cols, w_last)
+    )(*inputs)
 
     named = dict(
         got=got,
@@ -589,6 +589,8 @@
     res, tan, fit_res, fit_tan = pl.pallas_call(
         lambda *refs: finish(names + ["res", "tan", "fit_res", "fit_tan", "scratch"], axes, *refs),
         out_shape=[shape(*flat), shape(*flat), shape(6, slots), shape(6, slots)],
+        in_specs=local(len(names)),
+        out_specs=local(4),
         scratch_shapes=[pltpu.VMEM((row_total * COMPS, cols), F32)],
         name="finish",
     )(*named.values())

time: 32.2 us -> 29.6 us (0.919)
  Pallas kernels: 23.2 us -> 20.6 us
    pallas_call x1, Pallas kernels: 14.9 us -> 13.3 us  [per_device(): pl.pallas_call(interior, out_shape=[shape(row_total * COMPS, cols), shape...]
    pallas_call x1, Pallas kernels: 3.65 us -> 2.72 us  [per_device(): pl.pallas_call(lambda *refs: prepare(axes, *refs), out_shape=[shape(row_t...]
  transfers between devices with their start and end apart: 1 -> 1, of which waited for: 0 -> 0; matrix products, arithmetic and copies ran while one was open for 0% -> 0% of each run, Pallas kernels for 47% -> 45%
where the time goes in v1:
time: 29.6 us; the launch traced here: 29.3 us
  Pallas kernels  20.6 us (70%)
  starting transfers between devices  7.4 us (25%)
  local copies, waits for them, and re-layouts  0.68 us (2%)
  between operations  0.65 us (2%)
    pallas_call x1, Pallas kernels, per_device(): pl.pallas_call(interior, out_shape=[shape(row_total * COMPS, cols), shape...  13.3 us
    all_to_all x1, starting transfers between devices, per_device(): lax.all_to_all(pay, ('tx', 'ty', 'pb'), split_axis=0, concat_axis=0, tile...  7.4 us
    pallas_call x1, Pallas kernels, per_device(): pl.pallas_call(lambda *refs: finish(names + ['res', 'tan', 'fit_res', 'fi...  4.56 us
    pallas_call x1, Pallas kernels, per_device(): pl.pallas_call(lambda *refs: prepare(axes, *refs), out_shape=[shape(row_t...  2.72 us
    unnamed x2, local copies, waits for them, and re-layouts  0.68 us
  transfers between devices with their start and end apart: 1, of which 0 were waited for; matrix products, arithmetic and copies ran while one was open for 0% of the time, Pallas kernels for 45%

profile of v1, /device:TPU:0, one launch (start us, length us, event | category | flops | bytes accessed | tf_op | source)
XLA Modules:
  0.0 29.3 jit_solution(95194203815894605)
XLA Ops:
  0.6 2.7 %prepare.1 = (f32[512,128]{1,0:T(8,128)}, f32[16,768]{1,0:T(8,128)}, f32[32,128]{1,0:T(8,128)}, f32[16,32,128]{2,1,0:T(8,128)}) custom-call(f32[192,128]{1,0:T(8,128)} %bitcast.11, f32[192,128]{1,0:T(8,128)} %bitcast.12, f32[6,128]{1,0:T(8,128)} %refs_13_.1, f32[6,128]{1,0:T(8,128)} %refs_14_.1, s32[6,128]{1,0:T(8,128)} %bitcast.14, s32[1,768]{1,0:T(1,128)} %bitcast.18, ...), custom_call_target="tpu_custom_call" | custom-call | tf_op jit(solution)/shard_map/prepare/pallas_call | solution.py:543
  3.4 7.4 %all-to-all-start = ((f32[16,32,128]{2,1,0:T(8,128)}), f32[16,32,128]{2,1,0:T(8,128)S(1)}, u32[]{:S(2)}, u32[]{:S(2)}) async-start(f32[16,32,128]{2,1,0:T(8,128)} %get-tuple-element.16), calls=%async_computation | async-start | bytes 524288 | tf_op jit(solution)/shard_map/all_to_all | solution.py:555
  10.8 13.3 %interior.1 = (f32[512,128]{1,0:T(8,128)}, bf16[2048,64]{1,0:T(8,128)(2,1)}, bf16[128,256]{1,0:T(8,128)(2,1)}, f32[256,128]{1,0:T(8,128)}) custom-call(f32[512,128]{1,0:T(8,128)} %get-tuple-element.17.fields.refs_1_, bf16[12,256]{1,0:T(8,128)(2,1)} %bitcast.20, f32[1,256]{1,0:T(1,128)} %bitcast.21, bf16[256,256]{1,0:T(8,128)(2,1)} %refs_7_.1, ...), custom_call_target="tpu_custom_call" | custom-call | tf_op jit(solution)/shard_map/interior/pallas_call | solution.py:558
  24.1 0.0 all-to-all-done.refs_0_
  24.1 0.0 copy-start
  24.1 0.7 %copy-done = f32[16,32,128]{2,1,0:T(8,128)} copy-done((f32[16,32,128]{2,1,0:T(8,128)}, f32[16,32,128]{2,1,0:T(8,128)S(1)}, u32[]{:S(2)}) %copy-start) | copy-done | bytes 262168
  24.8 4.6 %finish.1 = (f32[192,128]{1,0:T(8,128)}, f32[192,128]{1,0:T(8,128)}, f32[6,128]{1,0:T(8,128)}, f32[6,128]{1,0:T(8,128)}) custom-call(f32[16,32,128]{2,1,0:T(8,128)} %copy-done, f32[512,128]{1,0:T(8,128)} %get-tuple-element.17.fields.refs_1_, f32[16,768]{1,0:T(8,128)} %get-tuple-element.18.refs_2_, f32[512,128]{1,0:T(8,128)} %get-tuple-element.19.refs_3_, ...), custom_call_target="tpu_custom_call" | custom-call | tf_op jit(solution)/shard_map/finish/pallas_call | solution.py:589
Async XLA Ops:
  3.4 20.7 %all-to-all-start = ((f32[16,32,128]{2,1,0:T(8,128)}), f32[16,32,128]{2,1,0:T(8,128)S(1)}, u32[]{:S(2)}, u32[]{:S(2)}) async-start(f32[16,32,128]{2,1,0:T(8,128)} %get-tuple-element.16), calls=%async_computation | async-start | bytes 524288 | tf_op jit(solution)/shard_map/all_to_all | solution.py:555
  24.1 0.7 %copy-start = (f32[16,32,128]{2,1,0:T(8,128)}, f32[16,32,128]{2,1,0:T(8,128)S(1)}, u32[]{:S(2)}) copy-start(f32[16,32,128]{2,1,0:T(8,128)S(1)} %all-to-all-done.refs_0_) | copy-start | bytes 786436

commit v2 on v1

--- a/solution.py
+++ b/solution.py
@@ -14,10 +14,15 @@
 COUNT_ROW = 6
 SPARE_ROWS = (6, 7, 14)
 GROUP = 5
+SMALL = 1 << 18
 
 
 def local(count):
     return [pl.BlockSpec(memory_space=pltpu.VMEM)] * count
+
+
+def on_chip(value):
+    return pltpu.with_memory_space_constraint(value, pltpu.VMEM)
 
 
 def dot(a, b, dims=((1,), (0,))):
@@ -543,9 +548,9 @@
     fields, ties, cols_out, pay = pl.pallas_call(
         lambda *refs: prepare(axes, *refs),
         out_shape=[
-            shape(row_total * COMPS, cols),
-            shape(COMPS, tie_total),
-            shape(2 * COMPS, cols),
+            pltpu.VMEM((row_total * COMPS, cols), F32),
+            pltpu.VMEM((COMPS, tie_total), F32),
+            pltpu.VMEM((2 * COMPS, cols), F32),
             shape(peers * pb_count, 2 * COMPS, slots),
         ],
         in_specs=local(len(inputs)),
@@ -554,14 +559,14 @@
     )(*inputs)
     got = lax.all_to_all(pay, ("tx", "ty", "pb"), split_axis=0, concat_axis=0, tiled=True)
 
-    inputs = (fields, w_in.T, b_in.reshape(1, hid), w_mid, b_mid.reshape(1, hid), w_out)
+    inputs = (on_chip(fields), w_in.T, b_in.reshape(1, hid), w_mid, b_mid.reshape(1, hid), w_out)
     forces, w_first, w_last, b_cols = pl.pallas_call(
         interior,
         out_shape=[
-            shape(row_total * COMPS, cols),
-            shape(8 * hid, 4 * COMPS, dtype=BF16),
-            shape(128, hid, dtype=BF16),
-            shape(hid, 128),
+            pltpu.VMEM((row_total * COMPS, cols), F32),
+            pltpu.VMEM((8 * hid, 4 * COMPS), BF16),
+            pltpu.VMEM((128, hid), BF16),
+            pltpu.VMEM((hid, 128), F32),
         ],
         in_specs=local(len(inputs)),
         out_specs=local(4),
@@ -569,16 +574,16 @@
     )(*inputs)
 
     named = dict(
-        got=got,
-        fields=fields,
-        ties=ties,
-        forces=forces,
+        got=on_chip(got) if got.size <= SMALL else got,
+        fields=on_chip(fields),
+        ties=on_chip(ties),
+        forces=on_chip(forces),
         load=load2,
-        cols=cols_out,
-        w_first=w_first,
+        cols=on_chip(cols_out),
+        w_first=on_chip(w_first),
         w_mid=w_mid,
-        b_mid=b_cols,
-        w_last=w_last,
+        b_mid=on_chip(b_cols),
+        w_last=on_chip(w_last),
         node=node2,
         slot=slot2,
         owner=owner2,

time: 29.6 us -> 27.5 us (0.929)
  Pallas kernels: 20.6 us -> 19.2 us
  local copies, waits for them, and re-layouts: 0.68 us -> 0 us
    pallas_call x2, Pallas kernels: 16 us -> 15.1 us  [the longest x1 12.5 us: per_device(): pl.pallas_call(interior, out_shape=[pltpu.VMEM((row_total * COMPS, cols),...]
    unnamed x2 -> x0, local copies, waits for them, and re-layouts: 0.68 us -> none
    pallas_call x1, Pallas kernels: 4.56 us -> 4.07 us  [per_device(): pl.pallas_call(lambda *refs: finish(names + ['res', 'tan', 'fit_res', 'fi...]
  transfers between devices with their start and end apart: 1 -> 1, of which waited for: 0 -> 0; matrix products, arithmetic and copies ran while one was open for 0% -> 0% of each run, Pallas kernels for 45% -> 46%
where the time goes in v2:
time: 27.5 us; the launch traced here: 27.2 us
  Pallas kernels  19.2 us (70%)
  starting transfers between devices  7.4 us (27%)
  between operations  0.65 us (2%)
    pallas_call x1, Pallas kernels, per_device(): pl.pallas_call(interior, out_shape=[pltpu.VMEM((row_total * COMPS, cols),...  12.5 us
    all_to_all x1, starting transfers between devices, per_device(): lax.all_to_all(pay, ('tx', 'ty', 'pb'), split_axis=0, concat_axis=0, tile...  7.4 us
    pallas_call x1, Pallas kernels, per_device(): pl.pallas_call(lambda *refs: finish(names + ['res', 'tan', 'fit_res', 'fi...  4.07 us
    pallas_call x1, Pallas kernels, per_device(): pl.pallas_call(lambda *refs: prepare(axes, *refs), out_shape=[pltpu.VMEM(...  2.6 us
  transfers between devices with their start and end apart: 1, of which 0 were waited for; matrix products, arithmetic and copies ran while one was open for 0% of the time, Pallas kernels for 46%

profile of v2, /device:TPU:0, one launch (start us, length us, event | category | flops | bytes accessed | tf_op | source)
XLA Modules:
  0.0 27.2 jit_solution(6656436930653723174)
XLA Ops:
  0.6 2.6 %prepare.1 = (f32[512,128]{1,0:T(8,128)S(1)}, f32[16,768]{1,0:T(8,128)S(1)}, f32[32,128]{1,0:T(8,128)S(1)}, f32[16,32,128]{2,1,0:T(8,128)}) custom-call(f32[192,128]{1,0:T(8,128)} %bitcast.11, f32[192,128]{1,0:T(8,128)} %bitcast.12, f32[6,128]{1,0:T(8,128)} %refs_13_.1, f32[6,128]{1,0:T(8,128)} %refs_14_.1, s32[6,128]{1,0:T(8,128)} %bitcast.14, ...), custom_call_target="tpu_custom_call" | custom-call | tf_op jit(solution)/shard_map/prepare/pallas_call | solution.py:548
  3.2 7.4 %all-to-all-start = ((f32[16,32,128]{2,1,0:T(8,128)}), f32[16,32,128]{2,1,0:T(8,128)S(1)}, u32[]{:S(2)}, u32[]{:S(2)}) async-start(f32[16,32,128]{2,1,0:T(8,128)} %get-tuple-element.16), calls=%async_computation | async-start | bytes 524288 | tf_op jit(solution)/shard_map/all_to_all | solution.py:560
  10.6 12.5 %interior.1 = (f32[512,128]{1,0:T(8,128)S(1)}, bf16[2048,64]{1,0:T(8,128)(2,1)S(1)}, bf16[128,256]{1,0:T(8,128)(2,1)S(1)}, f32[256,128]{1,0:T(8,128)S(1)}) custom-call(f32[512,128]{1,0:T(8,128)S(1)} %get-tuple-element.17.fields.refs_1_, bf16[12,256]{1,0:T(8,128)(2,1)} %bitcast.20, f32[1,256]{1,0:T(1,128)} %bitcast.21, bf16[256,256]{1,0:T(8,128)(2,1)} %refs_7_.1, ...), custom_call_target="tpu_custom_call" | custom-call | tf_op jit(solution)/shard_map/interior/pallas_call | solution.py:563
  23.1 0.0 all-to-all-done.refs_0_
  23.1 4.1 %finish.1 = (f32[192,128]{1,0:T(8,128)}, f32[192,128]{1,0:T(8,128)}, f32[6,128]{1,0:T(8,128)}, f32[6,128]{1,0:T(8,128)}) custom-call(f32[16,32,128]{2,1,0:T(8,128)S(1)} %all-to-all-done.refs_0_, f32[512,128]{1,0:T(8,128)S(1)} %get-tuple-element.17.fields.refs_1_, f32[16,768]{1,0:T(8,128)S(1)} %get-tuple-element.18.refs_2_, ...), custom_call_target="tpu_custom_call" | custom-call | tf_op jit(solution)/shard_map/finish/pallas_call | solution.py:594
Async XLA Ops:
  3.2 19.9 %all-to-all-start = ((f32[16,32,128]{2,1,0:T(8,128)}), f32[16,32,128]{2,1,0:T(8,128)S(1)}, u32[]{:S(2)}, u32[]{:S(2)}) async-start(f32[16,32,128]{2,1,0:T(8,128)} %get-tuple-element.16), calls=%async_computation | async-start | bytes 524288 | tf_op jit(solution)/shard_map/all_to_all | solution.py:560

commit v3 on v1

--- a/solution.py
+++ b/solution.py
@@ -13,11 +13,16 @@
 COMPS = 16
 COUNT_ROW = 6
 SPARE_ROWS = (6, 7, 14)
-GROUP = 5
+GROUP = 15
+SMALL = 1 << 18
 
 
 def local(count):
     return [pl.BlockSpec(memory_space=pltpu.VMEM)] * count
+
+
+def on_chip(value):
+    return pltpu.with_memory_space_constraint(value, pltpu.VMEM)
 
 
 def dot(a, b, dims=((1,), (0,))):
@@ -331,7 +336,10 @@
                 forces[pl.ds(at + COMPS, COMPS), :] += right + pltpu.roll(corner, 1, 1)
         return carry
 
-    lax.fori_loop(0, pairs // group, step, 0)
+    if group == pairs:
+        step(0, 0)
+    else:
+        lax.fori_loop(0, pairs // group, step, 0)
 
 
 def finish(names, axes, *refs):
@@ -543,9 +551,9 @@
     fields, ties, cols_out, pay = pl.pallas_call(
         lambda *refs: prepare(axes, *refs),
         out_shape=[
-            shape(row_total * COMPS, cols),
-            shape(COMPS, tie_total),
-            shape(2 * COMPS, cols),
+            pltpu.VMEM((row_total * COMPS, cols), F32),
+            pltpu.VMEM((COMPS, tie_total), F32),
+            pltpu.VMEM((2 * COMPS, cols), F32),
             shape(peers * pb_count, 2 * COMPS, slots),
         ],
         in_specs=local(len(inputs)),
@@ -555,13 +563,14 @@
     got = lax.all_to_all(pay, ("tx", "ty", "pb"), split_axis=0, concat_axis=0, tiled=True)
 
     inputs = (fields, w_in.T, b_in.reshape(1, hid), w_mid, b_mid.reshape(1, hid), w_out)
+    inputs = tuple(on_chip(value) for value in inputs)
     forces, w_first, w_last, b_cols = pl.pallas_call(
         interior,
         out_shape=[
-            shape(row_total * COMPS, cols),
-            shape(8 * hid, 4 * COMPS, dtype=BF16),
-            shape(128, hid, dtype=BF16),
-            shape(hid, 128),
+            pltpu.VMEM((row_total * COMPS, cols), F32),
+            pltpu.VMEM((8 * hid, 4 * COMPS), BF16),
+            pltpu.VMEM((128, hid), BF16),
+            pltpu.VMEM((hid, 128), F32),
         ],
         in_specs=local(len(inputs)),
         out_specs=local(4),
@@ -585,6 +594,7 @@
         fit_disp=fitting_disp,
         fit_dir=fitting_dir,
     )
+    named = {name: on_chip(value) if value.size <= SMALL else value for name, value in named.items()}
     names = list(named)
     res, tan, fit_res, fit_tan = pl.pallas_call(
         lambda *refs: finish(names + ["res", "tan", "fit_res", "fit_tan", "scratch"], axes, *refs),

time: 29.6 us -> 26.1 us (0.88)
  Pallas kernels: 20.6 us -> 16.2 us
  local copies, waits for them, and re-layouts: 0.68 us -> 1.33 us
    pallas_call x2, Pallas kernels: 16 us -> 13.1 us  [the longest x1 10.5 us: per_device(): pl.pallas_call(interior, out_shape=[pltpu.VMEM((row_total * COMPS, cols),...]
    pallas_call x1, Pallas kernels: 4.56 us -> 3.06 us  [per_device(): pl.pallas_call(lambda *refs: finish(names + ['res', 'tan', 'fit_res', 'fi...]
    unnamed x2 -> x22, local copies, waits for them, and re-layouts: 0.68 us -> 1.33 us
  transfers between devices with their start and end apart: 1 -> 1, of which waited for: 0 -> 0; matrix products, arithmetic and copies ran while one was open for 0% -> 0% of each run, Pallas kernels for 45% -> 41%
where the time goes in v3:
time: 26.1 us; the launch traced here: 25.8 us
  Pallas kernels  16.2 us (62%)
  starting transfers between devices  7.54 us (29%)
  local copies, waits for them, and re-layouts  1.33 us (5%)
  between operations  0.75 us (3%)
    pallas_call x1, Pallas kernels, per_device(): pl.pallas_call(interior, out_shape=[pltpu.VMEM((row_total * COMPS, cols),...  10.5 us
    all_to_all x1, starting transfers between devices, per_device(): lax.all_to_all(pay, ('tx', 'ty', 'pb'), split_axis=0, concat_axis=0, tile...  7.54 us
    pallas_call x1, Pallas kernels, per_device(): pl.pallas_call(lambda *refs: finish(names + ['res', 'tan', 'fit_res', 'fi...  3.06 us
    pallas_call x1, Pallas kernels, per_device(): pl.pallas_call(lambda *refs: prepare(axes, *refs), out_shape=[pltpu.VMEM(...  2.61 us
    unnamed x22, local copies, waits for them, and re-layouts  1.33 us
  transfers between devices with their start and end apart: 1, of which 0 were waited for; matrix products, arithmetic and copies ran while one was open for 0% of the time, Pallas kernels for 41%

profile of v3, /device:TPU:0, one launch (start us, length us, event | category | flops | bytes accessed | tf_op | source)
XLA Modules:
  0.0 25.8 jit_solution(15911229942148218065)
XLA Ops:
  0.6 2.6 %prepare.1 = (f32[512,128]{1,0:T(8,128)S(1)}, f32[16,768]{1,0:T(8,128)S(1)}, f32[32,128]{1,0:T(8,128)S(1)}, f32[16,32,128]{2,1,0:T(8,128)}) custom-call(f32[192,128]{1,0:T(8,128)} %bitcast.21, f32[192,128]{1,0:T(8,128)} %bitcast.22, f32[6,128]{1,0:T(8,128)} %refs_13_.1, f32[6,128]{1,0:T(8,128)} %refs_14_.1, s32[6,128]{1,0:T(8,128)} %bitcast.12, ...), custom_call_target="tpu_custom_call" | custom-call | tf_op jit(solution)/shard_map/prepare/pallas_call | solution.py:551
  3.2 0.0 copy-start
  3.2 0.0 copy-start.7
  3.2 0.0 copy-start.8
  3.2 0.0 copy-start.10
  3.3 7.5 %all-to-all-start = ((f32[16,32,128]{2,1,0:T(8,128)}), f32[16,32,128]{2,1,0:T(8,128)S(1)}, u32[]{:S(2)}, u32[]{:S(2)}) async-start(f32[16,32,128]{2,1,0:T(8,128)} %get-tuple-element.16), calls=%async_computation | async-start | bytes 524288 | tf_op jit(solution)/shard_map/all_to_all | solution.py:563
  10.8 0.0 copy-start.9
  10.8 0.0 copy-done
  10.8 0.0 copy-done.7
  10.8 0.0 copy-done.8
  10.8 0.0 copy-done.10
  10.9 0.6 %copy-done.9 = f32[256]{0:T(256)S(1)} copy-done((f32[256]{0:T(256)S(1)}, f32[256]{0:T(256)}, u32[]{:S(2)}) %copy-start.9) | copy-done | bytes 1048
  11.5 0.0 copy-start.1
  11.5 0.0 copy-start.5
  11.5 0.0 copy-start.6
  11.5 10.5 %interior.1 = (f32[512,128]{1,0:T(8,128)S(1)}, bf16[2048,64]{1,0:T(8,128)(2,1)S(1)}, bf16[128,256]{1,0:T(8,128)(2,1)S(1)}, f32[256,128]{1,0:T(8,128)S(1)}) custom-call(f32[512,128]{1,0:T(8,128)S(1)} %get-tuple-element.17.fields.refs_1_, bf16[12,256]{1,0:T(8,128)(2,1)S(1)} %bitcast.18, f32[1,256]{1,0:T(1,128)S(1)} %bitcast.19, bf16[256,256]{1,0:T(8,128)(2,1)S(1)} %copy-done, ...), custom_call_target="tpu_custom_call" | custom-call | tf_op jit(solution)/shard_map/interior/pallas_call | solution.py:567
  22.0 0.0 all-to-all-done.refs_0_
  22.0 0.0 copy-start.4
  22.0 0.0 copy-start.3
  22.0 0.0 copy-start.2
  22.0 0.0 copy-done.1
  22.0 0.0 copy-done.5
  22.0 0.0 copy-done.6
  22.1 0.6 %copy-done.4 = s32[768]{0:T(1024)S(1)} copy-done((s32[768]{0:T(1024)S(1)}, s32[768]{0:T(1024)}, u32[]{:S(2)}) %copy-start.4) | copy-done | bytes 3096
  22.7 0.0 copy-done.3
  22.7 0.0 copy-done.2
  22.7 3.1 %finish.1 = (f32[192,128]{1,0:T(8,128)}, f32[192,128]{1,0:T(8,128)}, f32[6,128]{1,0:T(8,128)}, f32[6,128]{1,0:T(8,128)}) custom-call(f32[16,32,128]{2,1,0:T(8,128)S(1)} %all-to-all-done.refs_0_, f32[512,128]{1,0:T(8,128)S(1)} %get-tuple-element.17.fields.refs_1_, f32[16,768]{1,0:T(8,128)S(1)} %get-tuple-element.18.refs_2_, ...), custom_call_target="tpu_custom_call" | custom-call | tf_op jit(solution)/shard_map/finish/pallas_call | solution.py:599
Async XLA Ops:
  3.2 7.6 %copy-start = (bf16[256,256]{1,0:T(8,128)(2,1)S(1)}, bf16[256,256]{1,0:T(8,128)(2,1)}, u32[]{:S(2)}) copy-start(bf16[256,256]{1,0:T(8,128)(2,1)} %refs_7_.1) | copy-start | bytes 393220
  3.2 7.6 %copy-start.7 = (bf16[256,12]{0,1:T(8,128)(2,1)S(1)}, bf16[256,12]{0,1:T(8,128)(2,1)}, u32[]{:S(2)}) copy-start(bf16[256,12]{0,1:T(8,128)(2,1)} %param.16) | copy-start | bytes 18436
  3.2 7.6 %copy-start.8 = (bf16[12,256]{1,0:T(8,128)(2,1)S(1)}, bf16[12,256]{1,0:T(8,128)(2,1)}, u32[]{:S(2)}) copy-start(bf16[12,256]{1,0:T(8,128)(2,1)} %w_out.1) | copy-start | bytes 18436
  3.2 7.6 %copy-start.10 = (f32[256]{0:T(256)S(1)}, f32[256]{0:T(256)}, u32[]{:S(2)}) copy-start(f32[256]{0:T(256)} %param.19) | copy-start | bytes 3076
  3.3 18.7 %all-to-all-start = ((f32[16,32,128]{2,1,0:T(8,128)}), f32[16,32,128]{2,1,0:T(8,128)S(1)}, u32[]{:S(2)}, u32[]{:S(2)}) async-start(f32[16,32,128]{2,1,0:T(8,128)} %get-tuple-element.16), calls=%async_computation | async-start | bytes 524288 | tf_op jit(solution)/shard_map/all_to_all | solution.py:563
  10.8 0.7 %copy-start.9 = (f32[256]{0:T(256)S(1)}, f32[256]{0:T(256)}, u32[]{:S(2)}) copy-start(f32[256]{0:T(256)} %param.17) | copy-start | bytes 3076
  11.5 10.5 %copy-start.1 = (f32[6,32,128]{2,1,0:T(8,128)S(1)}, f32[6,32,128]{2,1,0:T(8,128)}, u32[]{:S(2)}) copy-start(f32[6,32,128]{2,1,0:T(8,128)} %param.15) | copy-start | bytes 294916
  11.5 10.6 %copy-start.5 = (s32[768]{0:T(1024)S(1)}, s32[768]{0:T(1024)}, u32[]{:S(2)}) copy-start(s32[768]{0:T(1024)} %param.25) | copy-start | bytes 9220
  11.5 10.6 %copy-start.6 = (s32[768,1]{0,1:T(1,128)S(1)}, s32[768,1]{0,1:T(1,128)}, u32[]{:S(2)}) copy-start(s32[768,1]{0,1:T(1,128)} %param.24) | copy-start | bytes 9220
  22.0 0.7 %copy-start.4 = (s32[768]{0:T(1024)S(1)}, s32[768]{0:T(1024)}, u32[]{:S(2)}) copy-start(s32[768]{0:T(1024)} %param.23) | copy-start | bytes 9220
  22.0 0.7 %copy-start.3 = (f32[6,128]{1,0:T(8,128)S(1)}, f32[6,128]{1,0:T(8,128)}, u32[]{:S(2)}) copy-start(f32[6,128]{1,0:T(8,128)} %refs_14_.1) | copy-start | bytes 9220
  22.0 0.7 %copy-start.2 = (f32[6,128]{1,0:T(8,128)S(1)}, f32[6,128]{1,0:T(8,128)}, u32[]{:S(2)}) copy-start(f32[6,128]{1,0:T(8,128)} %refs_13_.1) | copy-start | bytes 9220

commit v4 on v3

--- a/solution.py
+++ b/solution.py
@@ -13,7 +13,6 @@
 COMPS = 16
 COUNT_ROW = 6
 SPARE_ROWS = (6, 7, 14)
-GROUP = 15
 SMALL = 1 << 18
 
 
@@ -149,8 +148,10 @@
 
 
 def prepare(axes, *refs):
-    (disp, dirn, fit_disp, fit_dir, node_ref, owner_ref, slot_ref) = refs[:7]
-    (fields, ties, col_out, pay) = refs[7:]
+    (disp, dirn, fit_disp, fit_dir, node_ref, owner_ref, slot_ref, b_in, b_mid) = refs[:9]
+    (fields, ties, col_out, pay) = refs[9:13]
+    for source, target in zip(refs[2:9], refs[13:]):
+        target[...] = source[...]
     tx_count, ty_count, pb_count = axes
     row_total = fields.shape[0] // COMPS
     cols = fields.shape[1]
@@ -305,48 +306,38 @@
     w_last[...] = dot(hit.astype(F32).astype(BF16), w_out[...]).astype(BF16)
 
 
-def interior(fields, w_in, b_in, w_mid, b_mid, w_out, forces, w_first, w_last, b_cols):
+def interior(pick, fields, w_in, b_in, w_mid, b_mid, w_out, forces, w_first, w_last, b_cols):
     row_total, cols = fields.shape[0] // COMPS, fields.shape[1]
-    pairs = (row_total - 1) // 2
-    group = next(size for size in (GROUP, 3, 2, 1) if pairs % size == 0)
+    half = row_total // 2
+    which = lax.axis_index("groups") if pick is None else pick
+    first = which * (row_total - 1 - half)
     keep = lanes_of((COMPS, cols)) < cols - 1
     build_weights(w_in, b_in, b_mid, w_out, w_first, w_last, b_cols)
     forces[...] = jnp.zeros(forces.shape, F32)
-
-    def row_of(row):
-        base = fields[pl.ds(pl.multiple_of(row * COMPS, COMPS), COMPS), :]
-        return base, pltpu.roll(base, cols - 1, 1)
-
-    def step(pair, carry):
-        start = pair * group
-        lines = [row_of(2 * start + at) for at in range(2 * group + 1)]
-        tiles = [
-            strain_tile(lines[at][0], lines[at + 1][0], lines[at][1], lines[at + 1][1])
-            for at in range(2 * group)
-        ]
-        tiles = [jnp.concatenate(tiles[at : at + 2], axis=1) for at in range(0, 2 * group, 2)]
-        sums = stress_sums(tiles, w_first, w_mid, b_cols, w_last)
-        for tile, (primal, tangent) in enumerate(sums):
-            for half in range(2):
-                lanes = slice(half * cols, (half + 1) * cols)
-                parts = corner_forces(primal[:, lanes], tangent[:, lanes])
-                base, right, upper, corner = (jnp.where(keep, part, 0.0) for part in parts)
-                at = pl.multiple_of((2 * (start + tile) + half) * COMPS, COMPS)
-                forces[pl.ds(at, COMPS), :] += base + pltpu.roll(upper, 1, 1)
-                forces[pl.ds(at + COMPS, COMPS), :] += right + pltpu.roll(corner, 1, 1)
-        return carry
-
-    if group == pairs:
-        step(0, 0)
-    else:
-        lax.fori_loop(0, pairs // group, step, 0)
-
-
-def finish(names, axes, *refs):
+    lines = []
+    for at in range(half + 1):
+        base = fields[pl.ds(pl.multiple_of((first + at) * COMPS, COMPS), COMPS), :]
+        lines.append((base, pltpu.roll(base, cols - 1, 1)))
+    tiles = [
+        strain_tile(lines[at][0], lines[at + 1][0], lines[at][1], lines[at + 1][1]) for at in range(half)
+    ]
+    tiles = [jnp.concatenate(tiles[at : at + 2], axis=1) for at in range(0, half, 2)]
+    sums = stress_sums(tiles, w_first, w_mid, b_cols, w_last)
+    for tile, (primal, tangent) in enumerate(sums):
+        for side in range(2):
+            lanes = slice(side * cols, (side + 1) * cols)
+            parts = corner_forces(primal[:, lanes], tangent[:, lanes])
+            mask = keep if tile + side > 0 else keep & (which == 0)
+            base, right, upper, corner = (jnp.where(mask, part, 0.0) for part in parts)
+            at = (2 * tile + side) * COMPS
+            forces[at : at + COMPS, :] += base + pltpu.roll(upper, 1, 1)
+            forces[at + COMPS : at + 2 * COMPS, :] += right + pltpu.roll(corner, 1, 1)
+
+
+def edges(names, axes, *refs):
     ref = dict(zip(names, refs))
     tx_count, ty_count, pb_count = axes
-    fields, ties, forces_in, load = ref["fields"], ref["ties"], ref["forces"], ref["load"]
-    scratch, got = ref["scratch"], ref["got"]
+    fields, ties, partial, got = ref["fields"], ref["ties"], ref["partial"], ref["got"]
     row_total, cols = fields.shape[0] // COMPS, fields.shape[1]
     slots = got.shape[2]
     tie_total = ties.shape[1]
@@ -389,11 +380,6 @@
 
     first_row = fields[0:COMPS, :]
     last_row = fields[(row_total - 1) * COMPS :, :]
-    inner_row = fields[(row_total - 2) * COMPS : (row_total - 1) * COMPS, :]
-
-    tile_inner = strain_tile(
-        inner_row, last_row, pltpu.roll(inner_row, cols - 1, 1), pltpu.roll(last_row, cols - 1, 1)
-    )
     tile_before = strain_tile(
         prev_row,
         first_row,
@@ -420,13 +406,13 @@
     tile_side = strain_tile(left_base, right_base, left_upper, right_upper)
 
     parts = []
-    edge_tiles = [jnp.concatenate(pair, axis=1) for pair in ((tile_inner, tile_before), (tile_after, tile_side))]
+    edge_tiles = [jnp.concatenate((tile_before, tile_after), axis=1), tile_side]
     edge_sums = stress_sums(edge_tiles, ref["w_first"], ref["w_mid"], ref["b_mid"], ref["w_last"])
     for primal, tangent in edge_sums:
-        for at in range(2):
-            lanes = slice(at * cols, (at + 1) * cols)
+        for start in range(0, primal.shape[1], cols):
+            lanes = slice(start, start + cols)
             parts.append(corner_forces(primal[:, lanes], tangent[:, lanes]))
-    part_inner, part_before, part_after, part_side = parts
+    part_before, part_after, part_side = parts
 
     def mask(value, keep):
         return jnp.where(keep, value, 0.0)
@@ -435,15 +421,13 @@
         return pltpu.roll(mask(value, keep), 1, 1)
 
     inside = lane < cols - 1
-    i_base, i_right, i_upper, i_corner = part_inner
     _, b_right, _, b_corner = part_before
     a_base, _, a_upper, _ = part_after
     s_base, s_right, s_upper, s_corner = part_side
     has_row = place > 0
     has_col = across > 0
     row_first = mask(mask(b_right, lane < cols) + moved(b_corner, inside), has_row)
-    row_inner = mask(i_base, inside) + moved(i_upper, inside)
-    row_last = mask(i_right, inside) + moved(i_corner, inside) + a_base + moved(a_upper, inside)
+    row_last = a_base + moved(a_upper, inside)
     first_lane = jnp.where(has_row, 0, 1)
     s_corner = mask(s_corner, (lane >= first_lane) & (lane < row_total))
     s_upper = mask(s_upper, (lane >= 1) & (lane <= row_total))
@@ -496,20 +480,31 @@
     )
 
     for row in range(row_total):
-        total = forces_in[row * COMPS : (row + 1) * COMPS, :] + tie_forces[row * COMPS : (row + 1) * COMPS]
+        total = tie_forces[row * COMPS : (row + 1) * COMPS]
         total = total + jnp.where(lane == 0, col_first[:, row : row + 1], 0.0)
         total = total + jnp.where(lane == cols - 1, col_last[:, row : row + 1], 0.0)
         if row == 0:
             total = total + row_first
-        if row == row_total - 2:
-            total = total + row_inner
         if row == row_total - 1:
             total = total + row_last
-        scratch[row * COMPS : (row + 1) * COMPS, :] = total
+        partial[row * COMPS : (row + 1) * COMPS, :] = total
+
+
+def combine(swapped, partial, own, other, load, res, tan, scratch):
+    row_total = partial.shape[0] // COMPS
+    held = own.shape[0]
+    skip = partial.shape[0] - held
+    first, second = own[...], other[...]
+    if swapped:
+        here = lax.axis_index("groups") == 0
+        first, second = jnp.where(here, first, second), jnp.where(here, second, first)
+    scratch[...] = partial[...]
+    scratch[0:held, :] += first
+    scratch[skip : skip + held, :] += second
     for comp in range(6):
         rows = slice(comp * row_total, (comp + 1) * row_total)
-        ref["res"][rows, :] = scratch[pl.ds(comp, row_total, stride=COMPS), :] - load[rows, :]
-        ref["tan"][rows, :] = scratch[pl.ds(8 + comp, row_total, stride=COMPS), :]
+        res[rows, :] = scratch[pl.ds(comp, row_total, stride=COMPS), :] - load[rows, :]
+        tan[rows, :] = scratch[pl.ds(8 + comp, row_total, stride=COMPS), :]
 
 
 def per_device(
@@ -547,63 +542,87 @@
     def shape(*dims, dtype=F32):
         return jax.ShapeDtypeStruct(dims, dtype)
 
-    inputs = (disp2, dir2, fitting_disp, fitting_dir, node2, owner2, slot2)
-    fields, ties, cols_out, pay = pl.pallas_call(
+    inputs = (
+        disp2,
+        dir2,
+        fitting_disp,
+        fitting_dir,
+        node2,
+        owner2,
+        slot2,
+        b_in.reshape(1, hid),
+        b_mid.reshape(1, hid),
+    )
+    outs = pl.pallas_call(
         lambda *refs: prepare(axes, *refs),
         out_shape=[
             pltpu.VMEM((row_total * COMPS, cols), F32),
             pltpu.VMEM((COMPS, tie_total), F32),
             pltpu.VMEM((2 * COMPS, cols), F32),
             shape(peers * pb_count, 2 * COMPS, slots),
-        ],
+        ]
+        + [pltpu.VMEM(value.shape, value.dtype) for value in inputs[2:]],
         in_specs=local(len(inputs)),
-        out_specs=local(4),
+        out_specs=local(4 + len(inputs[2:])),
         name="prepare",
     )(*inputs)
+    fields, ties, cols_out, pay, fit_disp, fit_dir, node, owner, slot, b_first, b_second = outs
     got = lax.all_to_all(pay, ("tx", "ty", "pb"), split_axis=0, concat_axis=0, tiled=True)
 
-    inputs = (fields, w_in.T, b_in.reshape(1, hid), w_mid, b_mid.reshape(1, hid), w_out)
-    inputs = tuple(on_chip(value) for value in inputs)
-    forces, w_first, w_last, b_cols = pl.pallas_call(
-        interior,
-        out_shape=[
-            pltpu.VMEM((row_total * COMPS, cols), F32),
-            pltpu.VMEM((8 * hid, 4 * COMPS), BF16),
-            pltpu.VMEM((128, hid), BF16),
-            pltpu.VMEM((hid, 128), F32),
-        ],
-        in_specs=local(len(inputs)),
-        out_specs=local(4),
-        name="interior",
-    )(*inputs)
+    inputs = tuple(on_chip(value) for value in (fields, w_in.T, b_first, w_mid, b_second, w_out))
+    groups = lax.axis_size("groups")
+    halves = []
+    for pick in (None,) if groups == 2 else (0, 1):
+        half, w_first, w_last, b_cols = pl.pallas_call(
+            lambda *refs: interior(pick, *refs),
+            out_shape=[
+                pltpu.VMEM(((row_total // 2 + 1) * COMPS, cols), F32),
+                pltpu.VMEM((8 * hid, 4 * COMPS), BF16),
+                pltpu.VMEM((128, hid), BF16),
+                pltpu.VMEM((hid, 128), F32),
+            ],
+            in_specs=local(len(inputs)),
+            out_specs=local(4),
+            name="interior",
+        )(*inputs)
+        halves.append(half)
+    if groups == 2:
+        halves.append(lax.ppermute(halves[0], "groups", [(0, 1), (1, 0)]))
 
     named = dict(
         got=got,
         fields=fields,
         ties=ties,
-        forces=forces,
-        load=load2,
         cols=cols_out,
         w_first=w_first,
         w_mid=w_mid,
         b_mid=b_cols,
         w_last=w_last,
-        node=node2,
-        slot=slot2,
-        owner=owner2,
-        fit_disp=fitting_disp,
-        fit_dir=fitting_dir,
+        node=node,
+        slot=slot,
+        owner=owner,
+        fit_disp=fit_disp,
+        fit_dir=fit_dir,
     )
     named = {name: on_chip(value) if value.size <= SMALL else value for name, value in named.items()}
     names = list(named)
-    res, tan, fit_res, fit_tan = pl.pallas_call(
-        lambda *refs: finish(names + ["res", "tan", "fit_res", "fit_tan", "scratch"], axes, *refs),
-        out_shape=[shape(*flat), shape(*flat), shape(6, slots), shape(6, slots)],
+    partial, fit_res, fit_tan = pl.pallas_call(
+        lambda *refs: edges(names + ["partial", "fit_res", "fit_tan"], axes, *refs),
+        out_shape=[pltpu.VMEM((row_total * COMPS, cols), F32), shape(6, slots), shape(6, slots)],
         in_specs=local(len(names)),
-        out_specs=local(4),
+        out_specs=local(3),
+        name="edges",
+    )(*named.values())
+
+    inputs = tuple(on_chip(value) for value in (partial, halves[0], halves[1], load2))
+    res, tan = pl.pallas_call(
+        lambda *refs: combine(groups == 2, *refs),
+        out_shape=[shape(*flat), shape(*flat)],
+        in_specs=local(len(inputs)),
+        out_specs=local(2),
         scratch_shapes=[pltpu.VMEM((row_total * COMPS, cols), F32)],
-        name="finish",
-    )(*named.values())
+        name="combine",
+    )(*inputs)
     cube = displacement.shape
     return (res.reshape(cube), tan.reshape(cube), fit_res, fit_tan)
 

time: 26.1 us -> 24.8 us (0.950)
  Pallas kernels: 16.2 us -> 12.3 us
  waiting for transfers between devices: 0.01 us -> 2.48 us
  starting transfers between devices: 7.54 us -> 9.08 us
  local copies, waits for them, and re-layouts: 1.33 us -> 0.01 us
    pallas_call x2 -> x3, Pallas kernels: 13.5 us -> 9.63 us  [the longest x1 5.96 us: per_device(): pl.pallas_call(lambda *refs: interior(pick, *refs), out_shape=[pltpu.VMEM...]
    all_to_all x1, waiting for transfers between devices: 0.01 us -> 2.48 us  [per_device(): lax.all_to_all(pay, ('tx', 'ty', 'pb'), split_axis=0, concat_axis=0, tile...]
    ppermute x0 -> x1, starting transfers between devices: none -> 1.54 us  [per_device(): halves.append(lax.ppermute(halves[0], 'groups', [(0, 1), (1, 0)]))]
    unnamed x22 -> x8, local copies, waits for them, and re-layouts: 1.33 us -> 0.01 us
  transfers between devices with their start and end apart: 1 -> 2, of which waited for: 0 -> 1; matrix products, arithmetic and copies ran while one was open for 0% -> 0% of each run, Pallas kernels for 41% -> 36%
where the time goes in v4:
time: 24.8 us; the launch traced here: 24.6 us
  Pallas kernels  12.3 us (50%)
  starting transfers between devices  9.08 us (37%)
  waiting for transfers between devices  2.48 us (10%)
  between operations  0.67 us (3%)
    all_to_all x1, starting transfers between devices, per_device(): lax.all_to_all(pay, ('tx', 'ty', 'pb'), split_axis=0, concat_axis=0, tile...  7.54 us
    pallas_call x1, Pallas kernels, per_device(): pl.pallas_call(lambda *refs: interior(pick, *refs), out_shape=[pltpu.VMEM...  5.96 us
    pallas_call x1, Pallas kernels, per_device(): pl.pallas_call(lambda *refs: edges(names + ['partial', 'fit_res', 'fit_ta...  2.87 us
    pallas_call x1, Pallas kernels, per_device(): pl.pallas_call(lambda *refs: prepare(axes, *refs), out_shape=[pltpu.VMEM(...  2.67 us
    all_to_all x1, waiting for transfers between devices, per_device(): lax.all_to_all(pay, ('tx', 'ty', 'pb'), split_axis=0, concat_axis=0, tile...  2.48 us
    ppermute x1, starting transfers between devices, per_device(): halves.append(lax.ppermute(halves[0], 'groups', [(0, 1), (1, 0)]))  1.54 us
    pallas_call x1, Pallas kernels, per_device(): pl.pallas_call(lambda *refs: combine(groups == 2, *refs), out_shape=[shap...  0.8 us
  transfers between devices with their start and end apart: 2, of which 1 were waited for; matrix products, arithmetic and copies ran while one was open for 0% of the time, Pallas kernels for 36%

profile of v4, /device:TPU:0, one launch (start us, length us, event | category | flops | bytes accessed | tf_op | source)
XLA Modules:
  0.0 24.6 jit_solution(9651218250463016526)
XLA Ops:
  0.6 2.7 %prepare.1 = (f32[512,128]{1,0:T(8,128)S(1)}, f32[16,768]{1,0:T(8,128)S(1)}, f32[32,128]{1,0:T(8,128)S(1)}, f32[16,32,128]{2,1,0:T(8,128)}, f32[6,128]{1,0:T(8,1...) custom-call(f32[192,128]{1,0:T(8,128)} %bitcast.13, ...), custom_call_target="tpu_custom_call" | custom-call | tf_op jit(solution)/shard_map/prepare/pallas_call | solution.py:556
  3.3 0.0 copy-start
  3.3 0.0 copy-start.2
  3.3 0.0 copy-start.3
  3.3 7.5 %all-to-all-start = ((f32[16,32,128]{2,1,0:T(8,128)}), f32[16,32,128]{2,1,0:T(8,128)S(1)}, u32[]{:S(2)}, u32[]{:S(2)}) async-start(f32[16,32,128]{2,1,0:T(8,128)} %get-tuple-element.24), calls=%async_computation | async-start | bytes 524288 | tf_op jit(solution)/shard_map/all_to_all | solution.py:570
  10.9 0.0 copy-done
  10.9 0.0 copy-done.2
  10.9 0.0 copy-done.3
  10.9 6.0 %interior.1 = (f32[272,128]{1,0:T(8,128)S(1)}, bf16[2048,64]{1,0:T(8,128)(2,1)S(1)}, bf16[128,256]{1,0:T(8,128)(2,1)S(1)}, f32[256,128]{1,0:T(8,128)S(1)}) custom-call(f32[512,128]{1,0:T(8,128)S(1)} %get-tuple-element.25.refs_0_.refs_1_, bf16[12,256]{1,0:T(8,128)(2,1)S(1)} %bitcast.12, f32[1,256]{1,0:T(1,128)S(1)} %get-tuple-element.28.refs_2_, ...), custom_call_target="tpu_custom_call" | custom-call | tf_op jit(solution)/shard_map/interior/pallas_call | solution.py:576
  16.9 1.5 %collective-permute-start = (f32[272,128]{1,0:T(8,128)S(1)}, f32[272,128]{1,0:T(8,128)S(1)}, u32[]{:S(2)}, u32[]{:S(2)}) collective-permute-start(f32[272,128]{1,0:T(8,128)S(1)} %get-tuple-element.39.refs_1_), channel_id=1, source_target_pairs={{0,16},{16,0},{1,17},{17,1},{2,18},{18,2},{3,19},{19,3},{4,20},{20... | collective-permute-start | bytes 417800 | tf_op jit(solution)/shard_map/ppermute | solution.py:590
  18.4 2.5 %all-to-all-done.refs_0_ = f32[16,32,128]{2,1,0:T(8,128)S(1)} async-done(((f32[16,32,128]{2,1,0:T(8,128)}), f32[16,32,128]{2,1,0:T(8,128)S(1)}, u32[]{:S(2)}, u32[]{:S(2)}) %all-to-all-start) | async-done | bytes 262176 | tf_op jit(solution)/shard_map/all_to_all | solution.py:570
  20.9 0.0 copy-start.1
  20.9 2.9 %edges.1 = (f32[512,128]{1,0:T(8,128)S(1)}, f32[6,128]{1,0:T(8,128)}, f32[6,128]{1,0:T(8,128)}) custom-call(f32[16,32,128]{2,1,0:T(8,128)S(1)} %all-to-all-done.refs_0_, f32[512,128]{1,0:T(8,128)S(1)} %get-tuple-element.25.refs_0_.refs_1_, f32[16,768]{1,0:T(8,128)S(1)} %get-tuple-element.26.refs_2_, f32[32,128]{1,0:T(8,128)S(1)} %get-tuple-element.27.refs_3_, ...), custom_call_target="tpu_custom_call" | custom-call | tf_op jit(solution)/shard_map/edges/pallas_call | solution.py:609
  23.7 0.0 collective-permute-done.refs_2_
  23.8 0.0 copy-done.1
  23.8 0.8 %combine.1 = (f32[192,128]{1,0:T(8,128)}, f32[192,128]{1,0:T(8,128)}) custom-call(f32[512,128]{1,0:T(8,128)S(1)} %get-tuple-element.38.refs_0_, f32[272,128]{1,0:T(8,128)S(1)} %get-tuple-element.39.refs_1_, f32[272,128]{1,0:T(8,128)S(1)} %collective-permute-done.refs_2_, f32[192,128]{1,0:T(8,128)S(1)} %bitcast.11), custom_call_target="tpu_custom_call" | custom-call | tf_op jit(solution)/shard_map/combine/pallas_call | solution.py:618
Async XLA Ops:
  3.3 7.6 %copy-start = (bf16[256,256]{1,0:T(8,128)(2,1)S(1)}, bf16[256,256]{1,0:T(8,128)(2,1)}, u32[]{:S(2)}) copy-start(bf16[256,256]{1,0:T(8,128)(2,1)} %refs_5_.3) | copy-start | bytes 393220
  3.3 7.6 %copy-start.2 = (bf16[256,12]{0,1:T(8,128)(2,1)S(1)}, bf16[256,12]{0,1:T(8,128)(2,1)}, u32[]{:S(2)}) copy-start(bf16[256,12]{0,1:T(8,128)(2,1)} %param.16) | copy-start | bytes 18436
  3.3 7.6 %copy-start.3 = (bf16[12,256]{1,0:T(8,128)(2,1)S(1)}, bf16[12,256]{1,0:T(8,128)(2,1)}, u32[]{:S(2)}) copy-start(bf16[12,256]{1,0:T(8,128)(2,1)} %refs_5_.2) | copy-start | bytes 18436
  3.3 17.6 %all-to-all-start = ((f32[16,32,128]{2,1,0:T(8,128)}), f32[16,32,128]{2,1,0:T(8,128)S(1)}, u32[]{:S(2)}, u32[]{:S(2)}) async-start(f32[16,32,128]{2,1,0:T(8,128)} %get-tuple-element.24), calls=%async_computation | async-start | bytes 524288 | tf_op jit(solution)/shard_map/all_to_all | solution.py:570
  16.9 6.9 %collective-permute-start = (f32[272,128]{1,0:T(8,128)S(1)}, f32[272,128]{1,0:T(8,128)S(1)}, u32[]{:S(2)}, u32[]{:S(2)}) collective-permute-start(f32[272,128]{1,0:T(8,128)S(1)} %get-tuple-element.39.refs_1_), channel_id=1, source_target_pairs={{0,16},{16,0},{1,17},{17,1},{2,18},{18,2},{3,19},{19,3},{4,20},{20... | collective-permute-start | bytes 417800 | tf_op jit(solution)/shard_map/ppermute | solution.py:590
  20.9 2.9 %copy-start.1 = (f32[6,32,128]{2,1,0:T(8,128)S(1)}, f32[6,32,128]{2,1,0:T(8,128)}, u32[]{:S(2)}) copy-start(f32[6,32,128]{2,1,0:T(8,128)} %param.15) | copy-start | bytes 294916

commit v5 on v4

--- a/solution.py
+++ b/solution.py
@@ -143,28 +143,26 @@
     )
 
 
-def block_of(row_place, across, ty_count, pb_count):
-    return (row_place // pb_count * ty_count + across) * pb_count + row_place % pb_count
-
-
-def prepare(axes, *refs):
-    (disp, dirn, fit_disp, fit_dir, node_ref, owner_ref, slot_ref, b_in, b_mid) = refs[:9]
-    (fields, ties, col_out, pay) = refs[9:13]
-    for source, target in zip(refs[2:9], refs[13:]):
+def gather_nodes(count, disp, dirn, *refs):
+    fields, rows = refs[count : count + 2]
+    for source, target in zip(refs[:count], refs[count + 2 :]):
         target[...] = source[...]
-    tx_count, ty_count, pb_count = axes
+    row_total = fields.shape[0] // COMPS
+    fields[...] = jnp.zeros(fields.shape, F32)
+    for comp in range(6):
+        part = slice(comp * row_total, (comp + 1) * row_total)
+        fields[pl.ds(comp, row_total, stride=COMPS), :] = disp[part, :]
+        fields[pl.ds(8 + comp, row_total, stride=COMPS), :] = dirn[part, :]
+    rows[0:COMPS, :] = fields[0:COMPS, :]
+    rows[COMPS : 2 * COMPS, :] = fields[(row_total - 1) * COMPS :, :]
+
+
+def sum_ties(peers, *refs):
+    (fields, fit_disp, fit_dir, node_ref, owner_ref, slot_ref, ties, col_out, pay) = refs
     row_total = fields.shape[0] // COMPS
     cols = fields.shape[1]
     slots = fit_disp.shape[1]
     tie_total = ties.shape[1]
-    core = lax.axis_index("pb")
-    across = lax.axis_index("ty")
-    place = lax.axis_index("tx") * pb_count + core
-
-    fields[...] = jnp.zeros(fields.shape, F32)
-    for comp in range(6):
-        fields[pl.ds(comp, row_total, stride=COMPS), :] = disp[comp * row_total : (comp + 1) * row_total, :]
-        fields[pl.ds(8 + comp, row_total, stride=COMPS), :] = dirn[comp * row_total : (comp + 1) * row_total, :]
 
     lane = lanes_of((COMPS, cols))
     for side, column in enumerate((0, cols - 1)):
@@ -202,37 +200,49 @@
         part = wide_bins[at * 2 * COMPS : (at + 1) * 2 * COMPS]
         return part[0:COMPS] + part[COMPS : 2 * COMPS]
 
-    peers = tx_count * ty_count
     block = math.gcd(peers, 8)
 
     def fill(first):
         wide_bins = bins(first, block)
         for peer in range(block):
-            at = (first + peer) * pb_count + core
-            pay[at, 0:COMPS, :] = fitting
-            pay[at, COMPS : 2 * COMPS, :] = folded(wide_bins, peer)
+            pay[first + peer, 0:COMPS, :] = fitting
+            pay[first + peer, COMPS : 2 * COMPS, :] = folded(wide_bins, peer)
 
     if block == peers:
         fill(0)
     else:
         lax.fori_loop(0, peers // block, lambda at, carry: (fill(at * block), carry)[1], 0)
 
-    for step, edge in ((-1, fields[0:COMPS, :]), (1, fields[(row_total - 1) * COMPS :, :])):
-        for side in (-1, 0, 1):
-            there, over = place + step, across + side
-            valid = (there >= 0) & (there < tx_count * pb_count) & (over >= 0) & (over < ty_count)
-
-            @pl.when(valid)
-            def _():
-                pay[block_of(there, over, ty_count, pb_count), 0:COMPS, :] = edge
-
-    for side, edge in ((-1, 0), (1, 1)):
+
+def mate_rows(mate):
+    upper = lax.axis_index("pb") == 0
+    first, last = mate[0:COMPS, :], mate[COMPS : 2 * COMPS, :]
+    return jnp.where(upper, first, last), jnp.where(upper, last, first)
+
+
+def fill_blocks(axes, row_total, sums, columns, mate, pay):
+    tx_count, ty_count = axes
+    along, across = lax.axis_index("tx"), lax.axis_index("ty")
+    near, far = mate_rows(mate)
+    pay[:, 0 : 2 * COMPS, :] = sums[...]
+    ahead = along + 1 - 2 * lax.axis_index("pb")
+    for side in (-1, 0, 1):
         over = across + side
-        packed = pack_column(col_out[edge * COMPS : (edge + 1) * COMPS, :], row_total)
-
-        @pl.when((over >= 0) & (over < ty_count))
+        inside = (over >= 0) & (over < ty_count)
+
+        @pl.when(inside & (ahead >= 0) & (ahead < tx_count))
         def _():
-            at = block_of(place, over, ty_count, pb_count)
+            pay[ahead * ty_count + over, 2 * COMPS : 3 * COMPS, :] = far
+
+        if side == 0:
+            continue
+        edge = 0 if side < 0 else 1
+        packed = pack_column(columns[edge * COMPS : (edge + 1) * COMPS, :], row_total)
+
+        @pl.when(inside)
+        def _():
+            at = along * ty_count + over
+            pay[at, 2 * COMPS : 3 * COMPS, :] = near
             for line, row in zip(packed, SPARE_ROWS):
                 pay[at, row : row + 1, :] = line
 
@@ -306,7 +316,7 @@
     w_last[...] = dot(hit.astype(F32).astype(BF16), w_out[...]).astype(BF16)
 
 
-def interior(pick, fields, w_in, b_in, w_mid, b_mid, w_out, forces, w_first, w_last, b_cols):
+def interior(pick, fields, w_in, b_in, w_mid, b_mid, w_out, sent, w_first, w_last, b_cols, forces):
     row_total, cols = fields.shape[0] // COMPS, fields.shape[1]
     half = row_total // 2
     which = lax.axis_index("groups") if pick is None else pick
@@ -332,6 +342,9 @@
             at = (2 * tile + side) * COMPS
             forces[at : at + COMPS, :] += base + pltpu.roll(upper, 1, 1)
             forces[at + COMPS : at + 2 * COMPS, :] += right + pltpu.roll(corner, 1, 1)
+    held = half + 1
+    for comp in range(12):
+        sent[comp * held : (comp + 1) * held, :] = forces[pl.ds(comp % 6 + comp // 6 * 8, held, stride=COMPS), :]
 
 
 def edges(names, axes, *refs):
@@ -344,23 +357,31 @@
     lane = lanes_of((COMPS, cols))
     core = lax.axis_index("pb")
     across = lax.axis_index("ty")
-    place = lax.axis_index("tx") * pb_count + core
-
-    def around(step, side):
-        there, over = place + step, across + side
-        valid = (there >= 0) & (there < tx_count * pb_count) & (over >= 0) & (over < ty_count)
-        at = jnp.where(valid, block_of(there, over, ty_count, pb_count), 0)
-        value = got[at, 0:COMPS, :]
-        if step == 0:
-            value = unpack_column(value, row_total)
+    along = lax.axis_index("tx")
+    place = along * pb_count + core
+
+    def around(step, side, packed=False):
+        there, over = along + step, across + side
+        valid = (there >= 0) & (there < tx_count) & (over >= 0) & (over < ty_count)
+        block = got.at[jnp.where(valid, there * ty_count + over, 0)]
+        if packed:
+            value = unpack_column(block[0:COMPS, :], row_total)
+        else:
+            value = block[2 * COMPS : 3 * COMPS, :]
         return jnp.where(valid, value, 0.0)
 
-    prev_row = around(-1, 0)
-    next_row = around(1, 0)
-    next_col = around(0, 1)
-    prev_col = around(0, -1)
-    next_corner = (around(-1, 1)[:, 0:1], around(1, 1)[:, 0:1])
-    prev_corner = (around(-1, -1)[:, cols - 1 : cols], around(1, -1)[:, cols - 1 : cols])
+    upper = core == 0
+    behind = 2 * core - 1
+    near, _ = mate_rows(ref["mate"])
+    rows_near = (around(0, -1), near, around(0, 1))
+    rows_far = tuple(around(behind, side) for side in (-1, 0, 1))
+    next_rows = [jnp.where(upper, one, two) for one, two in zip(rows_near, rows_far)]
+    prev_rows = [jnp.where(upper, two, one) for one, two in zip(rows_near, rows_far)]
+    prev_row, next_row = prev_rows[1], next_rows[1]
+    next_col = around(0, 1, True)
+    prev_col = around(0, -1, True)
+    next_corner = (prev_rows[2][:, 0:1], next_rows[2][:, 0:1])
+    prev_corner = (prev_rows[0][:, cols - 1 : cols], next_rows[0][:, cols - 1 : cols])
 
     def column(inner, before, after):
         line = pltpu.roll(inner, 1, 1)
@@ -448,7 +469,7 @@
 
     def collect(first, carry):
         fit_value, bins = carry
-        parts = [got[(first + peer) * pb_count + core] for peer in range(block)]
+        parts = [got[first + peer] for peer in range(block)]
         fit_all = jnp.concatenate([part[0:COMPS] for part in parts], axis=0)
         wide = dot(jnp.concatenate(split(fit_all, 2), axis=1), hot_two)
         for peer, part in enumerate(parts):
@@ -490,21 +511,24 @@
         partial[row * COMPS : (row + 1) * COMPS, :] = total
 
 
-def combine(swapped, partial, own, other, load, res, tan, scratch):
+def combine(swapped, partial, own, other, load, res, tan):
     row_total = partial.shape[0] // COMPS
-    held = own.shape[0]
-    skip = partial.shape[0] - held
+    held = own.shape[0] // 12
+    skip = row_total - held
     first, second = own[...], other[...]
     if swapped:
         here = lax.axis_index("groups") == 0
         first, second = jnp.where(here, first, second), jnp.where(here, second, first)
-    scratch[...] = partial[...]
-    scratch[0:held, :] += first
-    scratch[skip : skip + held, :] += second
-    for comp in range(6):
-        rows = slice(comp * row_total, (comp + 1) * row_total)
-        res[rows, :] = scratch[pl.ds(comp, row_total, stride=COMPS), :] - load[rows, :]
-        tan[rows, :] = scratch[pl.ds(8 + comp, row_total, stride=COMPS), :]
+    for comp in range(12):
+        target = res if comp < 6 else tan
+        start = comp % 6 * row_total
+        value = partial[pl.ds(comp % 6 + comp // 6 * 8, row_total, stride=COMPS), :]
+        if comp < 6:
+            value = value - load[start : start + row_total, :]
+        rows = slice(comp * held, (comp + 1) * held)
+        target[start : start + row_total, :] = value
+        target[start : start + held, :] += first[rows]
+        target[start + skip : start + row_total, :] += second[rows]
 
 
 def per_device(
@@ -542,9 +566,8 @@
     def shape(*dims, dtype=F32):
         return jax.ShapeDtypeStruct(dims, dtype)
 
-    inputs = (
-        disp2,
-        dir2,
+    assert pb_count == 2 and slots == cols
+    smalls = (
         fitting_disp,
         fitting_dir,
         node2,
@@ -554,20 +577,38 @@
         b_mid.reshape(1, hid),
     )
     outs = pl.pallas_call(
-        lambda *refs: prepare(axes, *refs),
+        lambda *refs: gather_nodes(len(smalls), *refs),
+        out_shape=[pltpu.VMEM((row_total * COMPS, cols), F32), pltpu.VMEM((2 * COMPS, cols), F32)]
+        + [pltpu.VMEM(value.shape, value.dtype) for value in smalls],
+        in_specs=local(2 + len(smalls)),
+        out_specs=local(2 + len(smalls)),
+        name="gather_nodes",
+    )(disp2, dir2, *smalls)
+    fields, rows, fit_disp, fit_dir, node, owner, slot, b_first, b_second = outs
+    mate = lax.ppermute(rows, "pb", [(0, 1), (1, 0)])
+
+    inputs = tuple(on_chip(value) for value in (fields, fit_disp, fit_dir, node, owner, slot))
+    small = peers * 2 * COMPS * slots <= SMALL
+    ties, cols_out, sums = pl.pallas_call(
+        lambda *refs: sum_ties(peers, *refs),
         out_shape=[
-            pltpu.VMEM((row_total * COMPS, cols), F32),
             pltpu.VMEM((COMPS, tie_total), F32),
             pltpu.VMEM((2 * COMPS, cols), F32),
-            shape(peers * pb_count, 2 * COMPS, slots),
-        ]
-        + [pltpu.VMEM(value.shape, value.dtype) for value in inputs[2:]],
+            (pltpu.VMEM if small else jax.ShapeDtypeStruct)((peers, 2 * COMPS, slots), F32),
+        ],
         in_specs=local(len(inputs)),
-        out_specs=local(4 + len(inputs[2:])),
-        name="prepare",
+        out_specs=local(3),
+        name="sum_ties",
     )(*inputs)
-    fields, ties, cols_out, pay, fit_disp, fit_dir, node, owner, slot, b_first, b_second = outs
-    got = lax.all_to_all(pay, ("tx", "ty", "pb"), split_axis=0, concat_axis=0, tiled=True)
+    inputs = [on_chip(value) if value.size <= SMALL else value for value in (sums, cols_out, mate)]
+    pay = pl.pallas_call(
+        lambda *refs: fill_blocks((tx_count, ty_count), row_total, *refs),
+        out_shape=shape(peers, 3 * COMPS, slots),
+        in_specs=local(len(inputs)),
+        out_specs=local(1)[0],
+        name="fill_blocks",
+    )(*inputs)
+    got = lax.all_to_all(pay, ("tx", "ty"), split_axis=0, concat_axis=0, tiled=True)
 
     inputs = tuple(on_chip(value) for value in (fields, w_in.T, b_first, w_mid, b_second, w_out))
     groups = lax.axis_size("groups")
@@ -576,13 +617,14 @@
         half, w_first, w_last, b_cols = pl.pallas_call(
             lambda *refs: interior(pick, *refs),
             out_shape=[
-                pltpu.VMEM(((row_total // 2 + 1) * COMPS, cols), F32),
+                pltpu.VMEM(((row_total // 2 + 1) * 12, cols), F32),
                 pltpu.VMEM((8 * hid, 4 * COMPS), BF16),
                 pltpu.VMEM((128, hid), BF16),
                 pltpu.VMEM((hid, 128), F32),
             ],
             in_specs=local(len(inputs)),
             out_specs=local(4),
+            scratch_shapes=[pltpu.VMEM(((row_total // 2 + 1) * COMPS, cols), F32)],
             name="interior",
         )(*inputs)
         halves.append(half)
@@ -591,6 +633,7 @@
 
     named = dict(
         got=got,
+        mate=mate,
         fields=fields,
         ties=ties,
         cols=cols_out,
@@ -620,7 +663,6 @@
         out_shape=[shape(*flat), shape(*flat)],
         in_specs=local(len(inputs)),
         out_specs=local(2),
-        scratch_shapes=[pltpu.VMEM((row_total * COMPS, cols), F32)],
         name="combine",
     )(*inputs)
     cube = displacement.shape

time: 24.8 us -> 23.5 us (0.948)
  waiting for transfers between devices: 2.48 us -> 0.86 us
  starting transfers between devices: 9.08 us -> 9.41 us
    all_to_all x1, waiting for transfers between devices: 2.48 us -> 0.7 us  [per_device(): lax.all_to_all(pay, ('tx', 'ty'), split_axis=0, concat_axis=0, tiled=True)]
    ppermute x0 -> x1, starting transfers between devices: none -> 0.56 us  [per_device(): mate = lax.ppermute(rows, 'pb', [(0, 1), (1, 0)])]
    all_to_all x1, starting transfers between devices: 7.54 us -> 7.26 us  [per_device(): lax.all_to_all(pay, ('tx', 'ty'), split_axis=0, concat_axis=0, tiled=True)]
    pallas_call x1 -> x3, Pallas kernels: 2.67 us -> 2.68 us  [the longest x1 1.15 us: per_device(): pl.pallas_call(lambda *refs: gather_nodes(len(smalls), *refs), out_shape=...]
  transfers between devices with their start and end apart: 2 -> 3, of which waited for: 1 -> 2; matrix products, arithmetic and copies ran while one was open for 0% -> 0% of each run, Pallas kernels for 36% -> 41%
where the time goes in v5:
time: 23.5 us; the launch traced here: 23.3 us
  Pallas kernels  12.3 us (52%)
  starting transfers between devices  9.41 us (40%)
  waiting for transfers between devices  0.86 us (4%)
  between operations  0.68 us (3%)
    all_to_all x1, starting transfers between devices, per_device(): lax.all_to_all(pay, ('tx', 'ty'), split_axis=0, concat_axis=0, tiled=True)  7.26 us
    pallas_call x1, Pallas kernels, per_device(): pl.pallas_call(lambda *refs: interior(pick, *refs), out_shape=[pltpu.VMEM...  5.96 us
    pallas_call x1, Pallas kernels, per_device(): pl.pallas_call(lambda *refs: edges(names + ['partial', 'fit_res', 'fit_ta...  2.87 us
    ppermute x1, starting transfers between devices, per_device(): halves.append(lax.ppermute(halves[0], 'groups', [(0, 1), (1, 0)]))  1.59 us
    pallas_call x1, Pallas kernels, per_device(): pl.pallas_call(lambda *refs: gather_nodes(len(smalls), *refs), out_shape=...  1.15 us
    pallas_call x1, Pallas kernels, per_device(): pl.pallas_call(lambda *refs: fill_blocks((tx_count, ty_count), row_total,...  0.85 us
    pallas_call x1, Pallas kernels, per_device(): pl.pallas_call(lambda *refs: combine(groups == 2, *refs), out_shape=[shap...  0.78 us
    all_to_all x1, waiting for transfers between devices, per_device(): lax.all_to_all(pay, ('tx', 'ty'), split_axis=0, concat_axis=0, tiled=True)  0.7 us
  transfers between devices with their start and end apart: 3, of which 2 were waited for; matrix products, arithmetic and copies ran while one was open for 0% of the time, Pallas kernels for 41%

profile of v5, /device:TPU:0, one launch (start us, length us, event | category | flops | bytes accessed | tf_op | source)
XLA Modules:
  0.0 23.3 jit_solution(3326714572020083281)
XLA Ops:
  0.6 1.1 %gather_nodes.1 = (f32[512,128]{1,0:T(8,128)S(1)}, f32[32,128]{1,0:T(8,128)S(1)}, f32[6,128]{1,0:T(8,128)S(1)}, f32[6,128]{1,0:T(8,128)S(1)}, s32[6,128]{1,0:T(8...) custom-call(f32[192,128]{1,0:T(8,128)} %bitcast.13, ...), custom_call_target="tpu_custom_call" | custom-call | tf_op jit(solution)/shard_map/gather_nodes/pallas_call | solution.py:579
  1.8 0.6 %collective-permute-start = (f32[32,128]{1,0:T(8,128)S(1)}, f32[32,128]{1,0:T(8,128)S(1)}, u32[]{:S(2)}, u32[]{:S(2)}) collective-permute-start(f32[32,128]{1,0:T(8,128)S(1)} %get-tuple-element.33), channel_id=1, source_target_pairs={{0,1},{1,0},{2,3},{3,2},{4,5},{5,4},{6,7},{7,6},{8,9},{9,8},{10,11... | collective-permute-start | bytes 49160 | tf_op jit(solution)/shard_map/ppermute | solution.py:588
  2.3 0.7 %sum_ties.1 = (f32[16,768]{1,0:T(8,128)S(1)}, f32[32,128]{1,0:T(8,128)S(1)}, f32[8,32,128]{2,1,0:T(8,128)S(1)}) custom-call(f32[512,128]{1,0:T(8,128)S(1)} %get-tuple-element.25.refs_0_.refs_2_, f32[6,128]{1,0:T(8,128)S(1)} %get-tuple-element.26.refs_1_.refs_12_, f32[6,128]{1,0:T(8,128)S(1)} %get-tuple-element.27.refs_2_.refs_13_, ...), custom_call_target="tpu_custom_call" | custom-call | tf_op jit(solution)/shard_map/sum_ties/pallas_call | solution.py:592
  3.0 0.2 collective-permute-done.refs_2_.refs_1_
  3.2 0.9 %fill_blocks.1 = f32[8,48,128]{2,1,0:T(8,128)} custom-call(f32[8,32,128]{2,1,0:T(8,128)S(1)} %get-tuple-element.31.refs_0_, f32[32,128]{1,0:T(8,128)S(1)} %get-tuple-element.32.refs_1_.refs_4_, f32[32,128]{1,0:T(8,128)S(1)} %collective-permute-done.refs_2_.refs_1_), custom_call_target="tpu_custom_call" | custom-call | tf_op jit(solution)/shard_map/fill_blocks/pallas_call | solution.py:604
  4.0 0.0 copy-start
  4.0 0.0 copy-start.2
  4.0 0.0 copy-start.3
  4.0 7.3 %all-to-all-start = ((f32[8,48,128]{2,1,0:T(8,128)}), f32[8,48,128]{2,1,0:T(8,128)S(1)}, u32[]{:S(2)}, u32[]{:S(2)}) async-start(f32[8,48,128]{2,1,0:T(8,128)} %fill_blocks.1), calls=%async_computation | async-start | bytes 393216 | tf_op jit(solution)/shard_map/all_to_all | solution.py:611
  11.3 0.0 copy-done
  11.3 0.0 copy-done.2
  11.3 0.0 copy-done.3
  11.3 6.0 %interior.1 = (f32[204,128]{1,0:T(8,128)S(1)}, bf16[2048,64]{1,0:T(8,128)(2,1)S(1)}, bf16[128,256]{1,0:T(8,128)(2,1)S(1)}, f32[256,128]{1,0:T(8,128)S(1)}) custom-call(f32[512,128]{1,0:T(8,128)S(1)} %get-tuple-element.25.refs_0_.refs_2_, bf16[12,256]{1,0:T(8,128)(2,1)S(1)} %bitcast.12, f32[1,256]{1,0:T(1,128)S(1)} %get-tuple-element.35.refs_2_, ...), custom_call_target="tpu_custom_call" | custom-call | tf_op jit(solution)/shard_map/interior/pallas_call | solution.py:617
  17.3 1.6 %collective-permute-start.1 = (f32[204,128]{1,0:T(8,128)S(1)}, f32[204,128]{1,0:T(8,128)S(1)}, u32[]{:S(2)}, u32[]{:S(2)}) collective-permute-start(f32[204,128]{1,0:T(8,128)S(1)} %get-tuple-element.41.refs_1_), channel_id=1, source_target_pairs={{0,16},{16,0},{1,17},{17,1},{2,18},{18,2},{3,19},{19,3},{4,20},{20... | collective-permute-start | bytes 313352 | tf_op jit(solution)/shard_map/ppermute | solution.py:632
  18.9 0.7 %all-to-all-done.refs_0_ = f32[8,48,128]{2,1,0:T(8,128)S(1)} async-done(((f32[8,48,128]{2,1,0:T(8,128)}), f32[8,48,128]{2,1,0:T(8,128)S(1)}, u32[]{:S(2)}, u32[]{:S(2)}) %all-to-all-start) | async-done | bytes 196640 | tf_op jit(solution)/shard_map/all_to_all | solution.py:611
  19.6 0.0 copy-start.1
  19.6 2.9 %edges.1 = (f32[512,128]{1,0:T(8,128)S(1)}, f32[6,128]{1,0:T(8,128)}, f32[6,128]{1,0:T(8,128)}) custom-call(f32[8,48,128]{2,1,0:T(8,128)S(1)} %all-to-all-done.refs_0_, f32[32,128]{1,0:T(8,128)S(1)} %collective-permute-done.refs_2_.refs_1_, f32[512,128]{1,0:T(8,128)S(1)} %get-tuple-element.25.refs_0_.refs_2_, f32[16,768]{1,0:T(8,128)S(1)} %get-tuple-element.34.refs_3_, ...), custom_call_target="tpu_custom_call" | custom-call | tf_op jit(solution)/shard_map/edges/pallas_call | solution.py:652
  22.5 0.0 collective-permute-done.1.refs_2_
  22.5 0.0 copy-done.1
  22.5 0.8 %combine.1 = (f32[192,128]{1,0:T(8,128)}, f32[192,128]{1,0:T(8,128)}) custom-call(f32[512,128]{1,0:T(8,128)S(1)} %get-tuple-element.40.refs_0_, f32[204,128]{1,0:T(8,128)S(1)} %get-tuple-element.41.refs_1_, f32[204,128]{1,0:T(8,128)S(1)} %collective-permute-done.1.refs_2_, f32[192,128]{1,0:T(8,128)S(1)} %bitcast.11), custom_call_target="tpu_custom_call" | custom-call | tf_op jit(solution)/shard_map/combine/pallas_call | solution.py:661
Async XLA Ops:
  1.8 1.4 %collective-permute-start = (f32[32,128]{1,0:T(8,128)S(1)}, f32[32,128]{1,0:T(8,128)S(1)}, u32[]{:S(2)}, u32[]{:S(2)}) collective-permute-start(f32[32,128]{1,0:T(8,128)S(1)} %get-tuple-element.33), channel_id=1, source_target_pairs={{0,1},{1,0},{2,3},{3,2},{4,5},{5,4},{6,7},{7,6},{8,9},{9,8},{10,11... | collective-permute-start | bytes 49160 | tf_op jit(solution)/shard_map/ppermute | solution.py:588
  4.0 7.3 %copy-start = (bf16[256,256]{1,0:T(8,128)(2,1)S(1)}, bf16[256,256]{1,0:T(8,128)(2,1)}, u32[]{:S(2)}) copy-start(bf16[256,256]{1,0:T(8,128)(2,1)} %refs_6_.1) | copy-start | bytes 393220
  4.0 7.3 %copy-start.2 = (bf16[256,12]{0,1:T(8,128)(2,1)S(1)}, bf16[256,12]{0,1:T(8,128)(2,1)}, u32[]{:S(2)}) copy-start(bf16[256,12]{0,1:T(8,128)(2,1)} %param.16) | copy-start | bytes 18436
  4.0 7.3 %copy-start.3 = (bf16[12,256]{1,0:T(8,128)(2,1)S(1)}, bf16[12,256]{1,0:T(8,128)(2,1)}, u32[]{:S(2)}) copy-start(bf16[12,256]{1,0:T(8,128)(2,1)} %refs_5_.1) | copy-start | bytes 18436
  4.0 15.5 %all-to-all-start = ((f32[8,48,128]{2,1,0:T(8,128)}), f32[8,48,128]{2,1,0:T(8,128)S(1)}, u32[]{:S(2)}, u32[]{:S(2)}) async-start(f32[8,48,128]{2,1,0:T(8,128)} %fill_blocks.1), calls=%async_computation | async-start | bytes 393216 | tf_op jit(solution)/shard_map/all_to_all | solution.py:611
  17.3 5.2 %collective-permute-start.1 = (f32[204,128]{1,0:T(8,128)S(1)}, f32[204,128]{1,0:T(8,128)S(1)}, u32[]{:S(2)}, u32[]{:S(2)}) collective-permute-start(f32[204,128]{1,0:T(8,128)S(1)} %get-tuple-element.41.refs_1_), channel_id=1, source_target_pairs={{0,16},{16,0},{1,17},{17,1},{2,18},{18,2},{3,19},{19,3},{4,20},{20... | collective-permute-start | bytes 313352 | tf_op jit(solution)/shard_map/ppermute | solution.py:632
  19.6 2.9 %copy-start.1 = (f32[6,32,128]{2,1,0:T(8,128)S(1)}, f32[6,32,128]{2,1,0:T(8,128)}, u32[]{:S(2)}) copy-start(f32[6,32,128]{2,1,0:T(8,128)} %param.15) | copy-start | bytes 294916

commit v6 on v5

--- a/solution.py
+++ b/solution.py
@@ -220,7 +220,7 @@
     return jnp.where(upper, first, last), jnp.where(upper, last, first)
 
 
-def fill_blocks(axes, row_total, sums, columns, mate, pay):
+def fill_blocks(axes, row_total, sums, columns, mate, w_in, b_in, b_mid, w_out, out, w_first, w_last, b_cols, pay, done):
     tx_count, ty_count = axes
     along, across = lax.axis_index("tx"), lax.axis_index("ty")
     near, far = mate_rows(mate)
@@ -245,6 +245,11 @@
             pay[at, 2 * COMPS : 3 * COMPS, :] = near
             for line, row in zip(packed, SPARE_ROWS):
                 pay[at, row : row + 1, :] = line
+
+    copy = pltpu.make_async_copy(pay, out, done)
+    copy.start()
+    build_weights(w_in, b_in, b_mid, w_out, w_first, w_last, b_cols)
+    copy.wait()
 
 
 def pack_column(column, width):
@@ -316,35 +321,46 @@
     w_last[...] = dot(hit.astype(F32).astype(BF16), w_out[...]).astype(BF16)
 
 
-def interior(pick, fields, w_in, b_in, w_mid, b_mid, w_out, sent, w_first, w_last, b_cols, forces):
+def interior(pick, fields, mate, w_first, w_mid, b_cols, w_last, sent, forces):
     row_total, cols = fields.shape[0] // COMPS, fields.shape[1]
     half = row_total // 2
-    which = lax.axis_index("groups") if pick is None else pick
-    first = which * (row_total - 1 - half)
-    keep = lanes_of((COMPS, cols)) < cols - 1
-    build_weights(w_in, b_in, b_mid, w_out, w_first, w_last, b_cols)
-    forces[...] = jnp.zeros(forces.shape, F32)
+    held = half + 1
+    group = lax.axis_index("groups") if pick is None else pick
+    core = lax.axis_index("pb")
+    first = group * half - core
+    near, _ = mate_rows(mate)
     lines = []
     for at in range(half + 1):
-        base = fields[pl.ds(pl.multiple_of((first + at) * COMPS, COMPS), COMPS), :]
+        row = first + at
+        if at == 0:
+            row = jnp.maximum(row, 0)
+        if at == half:
+            row = jnp.minimum(row, row_total - 1)
+        base = fields[pl.ds(pl.multiple_of(row * COMPS, COMPS), COMPS), :]
+        if at == 0:
+            base = jnp.where((core == 1) & (group == 0), near, base)
+        if at == half:
+            base = jnp.where((core == 0) & (group == 1), near, base)
         lines.append((base, pltpu.roll(base, cols - 1, 1)))
     tiles = [
         strain_tile(lines[at][0], lines[at + 1][0], lines[at][1], lines[at + 1][1]) for at in range(half)
     ]
     tiles = [jnp.concatenate(tiles[at : at + 2], axis=1) for at in range(0, half, 2)]
     sums = stress_sums(tiles, w_first, w_mid, b_cols, w_last)
+    keep = lanes_of((COMPS, cols)) < cols - 1
+    forces[...] = jnp.zeros(forces.shape, F32)
     for tile, (primal, tangent) in enumerate(sums):
         for side in range(2):
             lanes = slice(side * cols, (side + 1) * cols)
             parts = corner_forces(primal[:, lanes], tangent[:, lanes])
-            mask = keep if tile + side > 0 else keep & (which == 0)
-            base, right, upper, corner = (jnp.where(mask, part, 0.0) for part in parts)
-            at = (2 * tile + side) * COMPS
+            base, right, upper, corner = (jnp.where(keep, part, 0.0) for part in parts)
+            at = (2 * tile + side + 1) * COMPS
             forces[at : at + COMPS, :] += base + pltpu.roll(upper, 1, 1)
             forces[at + COMPS : at + 2 * COMPS, :] += right + pltpu.roll(corner, 1, 1)
-    held = half + 1
+    start = 1 + group * (row_total - held) - first
     for comp in range(12):
-        sent[comp * held : (comp + 1) * held, :] = forces[pl.ds(comp % 6 + comp // 6 * 8, held, stride=COMPS), :]
+        rows = pl.ds(start * COMPS + comp % 6 + comp // 6 * 8, held, stride=COMPS)
+        sent[comp * held : (comp + 1) * held, :] = forces[rows, :]
 
 
 def edges(names, axes, *refs):
@@ -401,24 +417,23 @@
 
     first_row = fields[0:COMPS, :]
     last_row = fields[(row_total - 1) * COMPS :, :]
-    tile_before = strain_tile(
-        prev_row,
-        first_row,
-        shifted(prev_row, next_corner[0]),
-        shifted(first_row, next_col[:, 0:1]),
-    )
-    tile_after = strain_tile(
-        last_row,
-        next_row,
-        shifted(last_row, next_col[:, row_total - 1 : row_total]),
-        shifted(next_row, next_corner[1]),
+    far_row = rows_far[1]
+    lower_row = jnp.where(upper, far_row, last_row)
+    upper_row = jnp.where(upper, first_row, far_row)
+    own_beyond = jnp.where(upper, next_col[:, 0:1], next_col[:, row_total - 1 : row_total])
+    far_beyond = rows_far[2][:, 0:1]
+    tile_far = strain_tile(
+        lower_row,
+        upper_row,
+        shifted(lower_row, jnp.where(upper, far_beyond, own_beyond)),
+        shifted(upper_row, jnp.where(upper, own_beyond, far_beyond)),
     )
     half = cols // 2
     low = lane < half
     back = cols - 1
 
     def two(left, right_line):
-        return jnp.where(low, left, pltpu.roll(right_line, half + back, 1))
+        return jnp.where(low, left, pltpu.roll(right_line, half, 1))
 
     left_base = two(line_prev, line_final)
     left_upper = two(line_first, line_next)
@@ -426,36 +441,29 @@
     right_upper = two(pltpu.roll(line_first, back, 1), pltpu.roll(line_next, back, 1))
     tile_side = strain_tile(left_base, right_base, left_upper, right_upper)
 
-    parts = []
-    edge_tiles = [jnp.concatenate((tile_before, tile_after), axis=1), tile_side]
-    edge_sums = stress_sums(edge_tiles, ref["w_first"], ref["w_mid"], ref["b_mid"], ref["w_last"])
-    for primal, tangent in edge_sums:
-        for start in range(0, primal.shape[1], cols):
-            lanes = slice(start, start + cols)
-            parts.append(corner_forces(primal[:, lanes], tangent[:, lanes]))
-    part_before, part_after, part_side = parts
+    edge_tile = jnp.concatenate((tile_far, tile_side), axis=1)
+    primal, tangent = stress_sums([edge_tile], ref["w_first"], ref["w_mid"], ref["b_mid"], ref["w_last"])[0]
+    f_base, f_right, f_upper, f_corner = corner_forces(primal[:, :cols], tangent[:, :cols])
+    s_base, s_right, s_upper, s_corner = corner_forces(primal[:, cols:], tangent[:, cols:])
 
     def mask(value, keep):
         return jnp.where(keep, value, 0.0)
 
-    def moved(value, keep):
-        return pltpu.roll(mask(value, keep), 1, 1)
-
-    inside = lane < cols - 1
-    _, b_right, _, b_corner = part_before
-    a_base, _, a_upper, _ = part_after
-    s_base, s_right, s_upper, s_corner = part_side
+    def moved(value):
+        return pltpu.roll(mask(value, lane < cols - 1), 1, 1)
+
     has_row = place > 0
     has_col = across > 0
-    row_first = mask(mask(b_right, lane < cols) + moved(b_corner, inside), has_row)
-    row_last = a_base + moved(a_upper, inside)
+    row_first = mask(f_right + moved(f_corner), upper & has_row)
+    row_last = mask(f_base + moved(f_upper), core == 1)
     first_lane = jnp.where(has_row, 0, 1)
     s_corner = mask(s_corner, (lane >= first_lane) & (lane < row_total))
     s_upper = mask(s_upper, (lane >= 1) & (lane <= row_total))
     col_first = mask(pltpu.roll(s_upper, back, 1) + s_corner, has_col)
-    s_base = mask(s_base, (lane >= half) & (lane < half + row_total - 1))
-    s_right = mask(s_right, (lane >= half) & (lane < half + row_total - 1))
-    col_last = pltpu.roll(s_base + pltpu.roll(s_right, 1, 1), cols - half, 1)
+    valid = (lane >= half + 1 - core) & (lane <= half + row_total - core)
+    s_base = mask(s_base, valid)
+    s_right = mask(s_right, valid)
+    col_last = pltpu.roll(pltpu.roll(s_base, back, 1) + s_right, cols - half, 1)
 
     node = as_line(ref["node"])
     slot = as_line(ref["slot"])
@@ -575,6 +583,8 @@
         slot2,
         b_in.reshape(1, hid),
         b_mid.reshape(1, hid),
+        w_in.T,
+        w_out,
     )
     outs = pl.pallas_call(
         lambda *refs: gather_nodes(len(smalls), *refs),
@@ -584,7 +594,7 @@
         out_specs=local(2 + len(smalls)),
         name="gather_nodes",
     )(disp2, dir2, *smalls)
-    fields, rows, fit_disp, fit_dir, node, owner, slot, b_first, b_second = outs
+    fields, rows, fit_disp, fit_dir, node, owner, slot, b_first, b_second, w_first_in, w_final = outs
     mate = lax.ppermute(rows, "pb", [(0, 1), (1, 0)])
 
     inputs = tuple(on_chip(value) for value in (fields, fit_disp, fit_dir, node, owner, slot))
@@ -600,31 +610,33 @@
         out_specs=local(3),
         name="sum_ties",
     )(*inputs)
-    inputs = [on_chip(value) if value.size <= SMALL else value for value in (sums, cols_out, mate)]
-    pay = pl.pallas_call(
+    inputs = (sums, cols_out, mate, w_first_in, b_first, b_second, w_final)
+    inputs = [on_chip(value) if value.size <= SMALL else value for value in inputs]
+    pay, w_first, w_last, b_cols = pl.pallas_call(
         lambda *refs: fill_blocks((tx_count, ty_count), row_total, *refs),
-        out_shape=shape(peers, 3 * COMPS, slots),
+        out_shape=[
+            shape(peers, 3 * COMPS, slots),
+            pltpu.VMEM((8 * hid, 4 * COMPS), BF16),
+            pltpu.VMEM((128, hid), BF16),
+            pltpu.VMEM((hid, 128), F32),
+        ],
         in_specs=local(len(inputs)),
-        out_specs=local(1)[0],
+        out_specs=[pl.BlockSpec(memory_space=pl.ANY)] + local(3),
+        scratch_shapes=[pltpu.VMEM((peers, 3 * COMPS, slots), F32), pltpu.SemaphoreType.DMA(())],
         name="fill_blocks",
     )(*inputs)
     got = lax.all_to_all(pay, ("tx", "ty"), split_axis=0, concat_axis=0, tiled=True)
 
-    inputs = tuple(on_chip(value) for value in (fields, w_in.T, b_first, w_mid, b_second, w_out))
+    inputs = tuple(on_chip(value) for value in (fields, mate, w_first, w_mid, b_cols, w_last))
     groups = lax.axis_size("groups")
     halves = []
     for pick in (None,) if groups == 2 else (0, 1):
-        half, w_first, w_last, b_cols = pl.pallas_call(
+        half = pl.pallas_call(
             lambda *refs: interior(pick, *refs),
-            out_shape=[
-                pltpu.VMEM(((row_total // 2 + 1) * 12, cols), F32),
-                pltpu.VMEM((8 * hid, 4 * COMPS), BF16),
-                pltpu.VMEM((128, hid), BF16),
-                pltpu.VMEM((hid, 128), F32),
-            ],
+            out_shape=pltpu.VMEM(((row_total // 2 + 1) * 12, cols), F32),
             in_specs=local(len(inputs)),
-            out_specs=local(4),
-            scratch_shapes=[pltpu.VMEM(((row_total // 2 + 1) * COMPS, cols), F32)],
+            out_specs=local(1)[0],
+            scratch_shapes=[pltpu.VMEM(((row_total // 2 + 3) * COMPS, cols), F32)],
             name="interior",
         )(*inputs)
         halves.append(half)

time: 23.5 us -> 23.1 us (0.983)
  Pallas kernels: 12.3 us -> 11.6 us
  waiting for transfers between devices: 0.86 us -> 1.13 us
    pallas_call x1, Pallas kernels: 2.87 us -> 2.45 us  [per_device(): pl.pallas_call(lambda *refs: edges(names + ['partial', 'fit_res', 'fit_ta...]
    all_to_all x1, waiting for transfers between devices: 0.7 us -> 0.97 us  [per_device(): lax.all_to_all(pay, ('tx', 'ty'), split_axis=0, concat_axis=0, tiled=True)]
    pallas_call x1, Pallas kernels: 5.96 us -> 5.7 us  [per_device(): pl.pallas_call(lambda *refs: interior(pick, *refs), out_shape=pltpu.VMEM(...]
  transfers between devices with their start and end apart: 3 -> 3, of which waited for: 2 -> 2; matrix products, arithmetic and copies ran while one was open for 0% -> 0% of each run, Pallas kernels for 41% -> 39%
where the time goes in v6:
time: 23.1 us; the launch traced here: 22.8 us
  Pallas kernels  11.6 us (50%)
  starting transfers between devices  9.43 us (41%)
  waiting for transfers between devices  1.13 us (5%)
  between operations  0.67 us (3%)
    all_to_all x1, starting transfers between devices, per_device(): lax.all_to_all(pay, ('tx', 'ty'), split_axis=0, concat_axis=0, tiled=True)  7.28 us
    pallas_call x1, Pallas kernels, per_device(): pl.pallas_call(lambda *refs: interior(pick, *refs), out_shape=pltpu.VMEM(...  5.7 us
    pallas_call x1, Pallas kernels, per_device(): pl.pallas_call(lambda *refs: edges(names + ['partial', 'fit_res', 'fit_ta...  2.45 us
    ppermute x1, starting transfers between devices, per_device(): halves.append(lax.ppermute(halves[0], 'groups', [(0, 1), (1, 0)]))  1.6 us
    pallas_call x1, Pallas kernels, per_device(): pl.pallas_call(lambda *refs: gather_nodes(len(smalls), *refs), out_shape=...  1.13 us
    all_to_all x1, waiting for transfers between devices, per_device(): lax.all_to_all(pay, ('tx', 'ty'), split_axis=0, concat_axis=0, tiled=True)  0.97 us
    pallas_call x1, Pallas kernels, per_device(): pl.pallas_call(lambda *refs: fill_blocks((tx_count, ty_count), row_total,...  0.86 us
    pallas_call x1, Pallas kernels, per_device(): pl.pallas_call(lambda *refs: combine(groups == 2, *refs), out_shape=[shap...  0.78 us
  transfers between devices with their start and end apart: 3, of which 2 were waited for; matrix products, arithmetic and copies ran while one was open for 0% of the time, Pallas kernels for 39%

profile of v6, /device:TPU:0, one launch (start us, length us, event | category | flops | bytes accessed | tf_op | source)
XLA Modules:
  0.0 22.8 jit_solution(8611959848420804551)
XLA Ops:
  0.6 1.1 %gather_nodes.1 = (f32[512,128]{1,0:T(8,128)S(1)}, f32[32,128]{1,0:T(8,128)S(1)}, f32[6,128]{1,0:T(8,128)S(1)}, f32[6,128]{1,0:T(8,128)S(1)}, s32[6,128]{1,0:T(8...) custom-call(f32[192,128]{1,0:T(8,128)} %bitcast.12, ...), custom_call_target="tpu_custom_call" | custom-call | tf_op jit(solution)/shard_map/gather_nodes/pallas_call | solution.py:589
  1.8 0.6 %collective-permute-start = (f32[32,128]{1,0:T(8,128)S(1)}, f32[32,128]{1,0:T(8,128)S(1)}, u32[]{:S(2)}, u32[]{:S(2)}) collective-permute-start(f32[32,128]{1,0:T(8,128)S(1)} %get-tuple-element.35), channel_id=1, source_target_pairs={{0,1},{1,0},{2,3},{3,2},{4,5},{5,4},{6,7},{7,6},{8,9},{9,8},{10,11... | collective-permute-start | bytes 49160 | tf_op jit(solution)/shard_map/ppermute | solution.py:598
  2.3 0.7 %sum_ties.1 = (f32[16,768]{1,0:T(8,128)S(1)}, f32[32,128]{1,0:T(8,128)S(1)}, f32[8,32,128]{2,1,0:T(8,128)S(1)}) custom-call(f32[512,128]{1,0:T(8,128)S(1)} %get-tuple-element.27.refs_0_.refs_2_, f32[6,128]{1,0:T(8,128)S(1)} %get-tuple-element.28.refs_1_.refs_12_, f32[6,128]{1,0:T(8,128)S(1)} %get-tuple-element.29.refs_2_.refs_13_, ...), custom_call_target="tpu_custom_call" | custom-call | tf_op jit(solution)/shard_map/sum_ties/pallas_call | solution.py:602
  3.0 0.2 collective-permute-done.refs_2_.refs_1_
  3.2 0.9 %fill_blocks.1 = (f32[8,48,128]{2,1,0:T(8,128)}, bf16[2048,64]{1,0:T(8,128)(2,1)S(1)}, bf16[128,256]{1,0:T(8,128)(2,1)S(1)}, f32[256,128]{1,0:T(8,128)S(1)}) custom-call(f32[8,32,128]{2,1,0:T(8,128)S(1)} %get-tuple-element.33.refs_0_, f32[32,128]{1,0:T(8,128)S(1)} %get-tuple-element.34.refs_1_.refs_4_, f32[32,128]{1,0:T(8,128)S(1)} %collective-permute-done.refs_2_.refs_1_, ...), custom_call_target="tpu_custom_call" | custom-call | tf_op jit(solution)/shard_map/fill_blocks/pallas_call | solution.py:615
  4.0 0.0 copy-start
  4.0 7.3 %all-to-all-start = ((f32[8,48,128]{2,1,0:T(8,128)}), f32[8,48,128]{2,1,0:T(8,128)S(1)}, u32[]{:S(2)}, u32[]{:S(2)}) async-start(f32[8,48,128]{2,1,0:T(8,128)} %get-tuple-element.40), calls=%async_computation | async-start | bytes 393216 | tf_op jit(solution)/shard_map/all_to_all | solution.py:628
  11.3 0.0 copy-done
  11.3 5.7 %interior.1.refs_1_ = f32[204,128]{1,0:T(8,128)S(1)} custom-call(f32[512,128]{1,0:T(8,128)S(1)} %get-tuple-element.27.refs_0_.refs_2_, f32[32,128]{1,0:T(8,128)S(1)} %collective-permute-done.refs_2_.refs_1_, bf16[2048,64]{1,0:T(8,128)(2,1)S(1)} %get-tuple-element.42.refs_5_.refs_2_, bf16[256,256]{1,0:T(8,128)(2,1)S(1)} %copy-done, ...), custom_call_target="tpu_custom_call" | custom-call | tf_op jit(solution)/shard_map/interior/pallas_call | solution.py:634
  17.0 1.6 %collective-permute-start.1 = (f32[204,128]{1,0:T(8,128)S(1)}, f32[204,128]{1,0:T(8,128)S(1)}, u32[]{:S(2)}, u32[]{:S(2)}) collective-permute-start(f32[204,128]{1,0:T(8,128)S(1)} %interior.1.refs_1_), channel_id=1, source_target_pairs={{0,16},{16,0},{1,17},{17,1},{2,18},{18,2},{3,19},{19,3},{4,20},{20... | collective-permute-start | bytes 313352 | tf_op jit(solution)/shard_map/ppermute | solution.py:644
  18.6 1.0 %all-to-all-done.refs_0_ = f32[8,48,128]{2,1,0:T(8,128)S(1)} async-done(((f32[8,48,128]{2,1,0:T(8,128)}), f32[8,48,128]{2,1,0:T(8,128)S(1)}, u32[]{:S(2)}, u32[]{:S(2)}) %all-to-all-start) | async-done | bytes 196640 | tf_op jit(solution)/shard_map/all_to_all | solution.py:628
  19.6 0.0 copy-start.1
  19.6 2.5 %edges.1 = (f32[512,128]{1,0:T(8,128)S(1)}, f32[6,128]{1,0:T(8,128)}, f32[6,128]{1,0:T(8,128)}) custom-call(f32[8,48,128]{2,1,0:T(8,128)S(1)} %all-to-all-done.refs_0_, f32[32,128]{1,0:T(8,128)S(1)} %collective-permute-done.refs_2_.refs_1_, f32[512,128]{1,0:T(8,128)S(1)} %get-tuple-element.27.refs_0_.refs_2_, f32[16,768]{1,0:T(8,128)S(1)} %get-tuple-element.41.refs_3_, ...), custom_call_target="tpu_custom_call" | custom-call | tf_op jit(solution)/shard_map/edges/pallas_call | solution.py:664
  22.1 0.0 collective-permute-done.1.refs_2_
  22.1 0.0 copy-done.1
  22.1 0.8 %combine.1 = (f32[192,128]{1,0:T(8,128)}, f32[192,128]{1,0:T(8,128)}) custom-call(f32[512,128]{1,0:T(8,128)S(1)} %get-tuple-element.45.refs_0_, f32[204,128]{1,0:T(8,128)S(1)} %interior.1.refs_1_, f32[204,128]{1,0:T(8,128)S(1)} %collective-permute-done.1.refs_2_, f32[192,128]{1,0:T(8,128)S(1)} %bitcast.11), custom_call_target="tpu_custom_call" | custom-call | tf_op jit(solution)/shard_map/combine/pallas_call | solution.py:673
Async XLA Ops:
  1.8 1.4 %collective-permute-start = (f32[32,128]{1,0:T(8,128)S(1)}, f32[32,128]{1,0:T(8,128)S(1)}, u32[]{:S(2)}, u32[]{:S(2)}) collective-permute-start(f32[32,128]{1,0:T(8,128)S(1)} %get-tuple-element.35), channel_id=1, source_target_pairs={{0,1},{1,0},{2,3},{3,2},{4,5},{5,4},{6,7},{7,6},{8,9},{9,8},{10,11... | collective-permute-start | bytes 49160 | tf_op jit(solution)/shard_map/ppermute | solution.py:598
  4.0 7.3 %copy-start = (bf16[256,256]{1,0:T(8,128)(2,1)S(1)}, bf16[256,256]{1,0:T(8,128)(2,1)}, u32[]{:S(2)}) copy-start(bf16[256,256]{1,0:T(8,128)(2,1)} %refs_3_.3) | copy-start | bytes 393220
  4.0 15.6 %all-to-all-start = ((f32[8,48,128]{2,1,0:T(8,128)}), f32[8,48,128]{2,1,0:T(8,128)S(1)}, u32[]{:S(2)}, u32[]{:S(2)}) async-start(f32[8,48,128]{2,1,0:T(8,128)} %get-tuple-element.40), calls=%async_computation | async-start | bytes 393216 | tf_op jit(solution)/shard_map/all_to_all | solution.py:628
  17.0 5.0 %collective-permute-start.1 = (f32[204,128]{1,0:T(8,128)S(1)}, f32[204,128]{1,0:T(8,128)S(1)}, u32[]{:S(2)}, u32[]{:S(2)}) collective-permute-start(f32[204,128]{1,0:T(8,128)S(1)} %interior.1.refs_1_), channel_id=1, source_target_pairs={{0,16},{16,0},{1,17},{17,1},{2,18},{18,2},{3,19},{19,3},{4,20},{20... | collective-permute-start | bytes 313352 | tf_op jit(solution)/shard_map/ppermute | solution.py:644
  19.6 2.5 %copy-start.1 = (f32[6,32,128]{2,1,0:T(8,128)S(1)}, f32[6,32,128]{2,1,0:T(8,128)}, u32[]{:S(2)}) copy-start(f32[6,32,128]{2,1,0:T(8,128)} %param.15) | copy-start | bytes 294916

commit v7 on v6

--- a/solution.py
+++ b/solution.py
@@ -157,8 +157,11 @@
     rows[COMPS : 2 * COMPS, :] = fields[(row_total - 1) * COMPS :, :]
 
 
-def sum_ties(peers, *refs):
-    (fields, fit_disp, fit_dir, node_ref, owner_ref, slot_ref, ties, col_out, pay) = refs
+def sum_ties(axes, *refs):
+    (fields, fit_disp, fit_dir, node_ref, owner_ref, slot_ref) = refs[:6]
+    (ties, col_out, hot_col_out, hot_slot_out, hot_row_out, out, pay, done) = refs[6:]
+    tx_count, ty_count = axes
+    peers = tx_count * ty_count
     row_total = fields.shape[0] // COMPS
     cols = fields.shape[1]
     slots = fit_disp.shape[1]
@@ -178,6 +181,8 @@
     node_row = lax.shift_right_logical(node, cols.bit_length() - 1)
     node_col = jnp.bitwise_and(node, cols - 1)
     hot_col = one_hot(node_col, cols)
+    hot_col_out[...] = hot_col
+    hot_row_out[...] = one_hot(node_row, row_total)
     wide = dot(
         jnp.concatenate(split(fields[...], 2), axis=1), jnp.concatenate([hot_col] * 2, axis=0)
     )
@@ -188,6 +193,7 @@
     ties[...] = value
     stack = jnp.concatenate(split(value, 2), axis=0)
     hot_slot = one_hot(slot, slots)
+    hot_slot_out[...] = hot_slot
     fitting = paired(fit_disp[...], fit_dir[...])
 
     def bins(first, count):
@@ -213,6 +219,20 @@
     else:
         lax.fori_loop(0, peers // block, lambda at, carry: (fill(at * block), carry)[1], 0)
 
+    along, across = lax.axis_index("tx"), lax.axis_index("ty")
+    for side, edge in ((-1, 0), (1, 1)):
+        over = across + side
+        packed = pack_column(col_out[edge * COMPS : (edge + 1) * COMPS, :], row_total)
+
+        @pl.when((over >= 0) & (over < ty_count))
+        def _():
+            for line, row in zip(packed, SPARE_ROWS):
+                pay[along * ty_count + over, row : row + 1, :] = line
+
+    copy = pltpu.make_async_copy(pay, out.at[:, 0 : 2 * COMPS, :], done)
+    copy.start()
+    copy.wait()
+
 
 def mate_rows(mate):
     upper = lax.axis_index("pb") == 0
@@ -220,33 +240,28 @@
     return jnp.where(upper, first, last), jnp.where(upper, last, first)
 
 
-def fill_blocks(axes, row_total, sums, columns, mate, w_in, b_in, b_mid, w_out, out, w_first, w_last, b_cols, pay, done):
+def fill_rows(axes, mate, w_in, b_in, b_mid, w_out, _, w_first, w_last, b_cols, out, rows, done):
     tx_count, ty_count = axes
     along, across = lax.axis_index("tx"), lax.axis_index("ty")
     near, far = mate_rows(mate)
-    pay[:, 0 : 2 * COMPS, :] = sums[...]
     ahead = along + 1 - 2 * lax.axis_index("pb")
+    rows[...] = jnp.zeros(rows.shape, F32)
     for side in (-1, 0, 1):
         over = across + side
         inside = (over >= 0) & (over < ty_count)
 
         @pl.when(inside & (ahead >= 0) & (ahead < tx_count))
         def _():
-            pay[ahead * ty_count + over, 2 * COMPS : 3 * COMPS, :] = far
+            rows[ahead * ty_count + over] = far
 
         if side == 0:
             continue
-        edge = 0 if side < 0 else 1
-        packed = pack_column(columns[edge * COMPS : (edge + 1) * COMPS, :], row_total)
 
         @pl.when(inside)
         def _():
-            at = along * ty_count + over
-            pay[at, 2 * COMPS : 3 * COMPS, :] = near
-            for line, row in zip(packed, SPARE_ROWS):
-                pay[at, row : row + 1, :] = line
-
-    copy = pltpu.make_async_copy(pay, out, done)
+            rows[along * ty_count + over] = near
+
+    copy = pltpu.make_async_copy(rows, out.at[:, 2 * COMPS : 3 * COMPS, :], done)
     copy.start()
     build_weights(w_in, b_in, b_mid, w_out, w_first, w_last, b_cols)
     copy.wait()
@@ -321,16 +336,18 @@
     w_last[...] = dot(hit.astype(F32).astype(BF16), w_out[...]).astype(BF16)
 
 
-def interior(pick, fields, mate, w_first, w_mid, b_cols, w_last, sent, forces):
+def interior(pick, begin, end, low, high, *refs):
+    fields, mate, w_first, w_mid, b_cols, w_last = refs[:6]
+    before = refs[6] if begin else None
+    sent, forces = refs[-2:]
     row_total, cols = fields.shape[0] // COMPS, fields.shape[1]
     half = row_total // 2
-    held = half + 1
     group = lax.axis_index("groups") if pick is None else pick
     core = lax.axis_index("pb")
     first = group * half - core
     near, _ = mate_rows(mate)
     lines = []
-    for at in range(half + 1):
+    for at in range(begin, end + 1):
         row = first + at
         if at == 0:
             row = jnp.maximum(row, 0)
@@ -343,30 +360,31 @@
             base = jnp.where((core == 0) & (group == 1), near, base)
         lines.append((base, pltpu.roll(base, cols - 1, 1)))
     tiles = [
-        strain_tile(lines[at][0], lines[at + 1][0], lines[at][1], lines[at + 1][1]) for at in range(half)
+        strain_tile(one[0], two[0], one[1], two[1]) for one, two in zip(lines[:-1], lines[1:])
     ]
-    tiles = [jnp.concatenate(tiles[at : at + 2], axis=1) for at in range(0, half, 2)]
+    tiles = [jnp.concatenate(tiles[at : at + 2], axis=1) for at in range(0, end - begin, 2)]
     sums = stress_sums(tiles, w_first, w_mid, b_cols, w_last)
     keep = lanes_of((COMPS, cols)) < cols - 1
-    forces[...] = jnp.zeros(forces.shape, F32)
+    forces[...] = jnp.zeros(forces.shape, F32) if before is None else before[...]
     for tile, (primal, tangent) in enumerate(sums):
         for side in range(2):
             lanes = slice(side * cols, (side + 1) * cols)
             parts = corner_forces(primal[:, lanes], tangent[:, lanes])
             base, right, upper, corner = (jnp.where(keep, part, 0.0) for part in parts)
-            at = (2 * tile + side + 1) * COMPS
+            at = (begin + 2 * tile + side + 1) * COMPS
             forces[at : at + COMPS, :] += base + pltpu.roll(upper, 1, 1)
             forces[at + COMPS : at + 2 * COMPS, :] += right + pltpu.roll(corner, 1, 1)
-    start = 1 + group * (row_total - held) - first
+    start = 1 + group * (row_total - half - 1) - first + low
+    count = high - low
     for comp in range(12):
-        rows = pl.ds(start * COMPS + comp % 6 + comp // 6 * 8, held, stride=COMPS)
-        sent[comp * held : (comp + 1) * held, :] = forces[rows, :]
-
-
-def edges(names, axes, *refs):
+        rows = pl.ds(start * COMPS + comp % 6 + comp // 6 * 8, count, stride=COMPS)
+        sent[comp * count : (comp + 1) * count, :] = forces[rows, :]
+
+
+def finish(names, axes, pieces, swapped, *refs):
     ref = dict(zip(names, refs))
     tx_count, ty_count, pb_count = axes
-    fields, ties, partial, got = ref["fields"], ref["ties"], ref["partial"], ref["got"]
+    fields, ties, got, load = ref["fields"], ref["ties"], ref["got"], ref["load"]
     row_total, cols = fields.shape[0] // COMPS, fields.shape[1]
     slots = got.shape[2]
     tie_total = ties.shape[1]
@@ -465,10 +483,8 @@
     s_right = mask(s_right, valid)
     col_last = pltpu.roll(pltpu.roll(s_base, back, 1) + s_right, cols - half, 1)
 
-    node = as_line(ref["node"])
-    slot = as_line(ref["slot"])
     owner = ref["owner"][...]
-    hot_slot = one_hot(slot, slots)
+    hot_slot = ref["hot_slot"][...]
     hot_two = jnp.concatenate([hot_slot] * 2, axis=0)
     fit_value = jnp.zeros((COMPS, tie_total), F32)
     bins = jnp.zeros((COMPS, slots), F32)
@@ -495,48 +511,52 @@
     for out, fit, base in (("fit_res", "fit_disp", 0), ("fit_tan", "fit_dir", 8)):
         ref[out][...] = 2.0 * (count * ref[fit][...] - bins[base : base + 6])
 
-    pulled = 2.0 * (ties[...] - fit_value)
-    node_row = lax.shift_right_logical(node, cols.bit_length() - 1)
-    node_col = jnp.bitwise_and(node, cols - 1)
-    hot_col = one_hot(node_col, cols)
-    sides = split(pulled, 2)
-    lhs = []
-    for row in range(row_total):
-        hit = (node_row == row).astype(F32).astype(BF16)
-        lhs.append(jnp.concatenate([side * hit for side in sides], axis=1))
-    tie_forces = dot(
-        jnp.concatenate(lhs, axis=0), jnp.concatenate([hot_col] * 2, axis=1), ((1,), (1,))
-    )
-
-    for row in range(row_total):
-        total = tie_forces[row * COMPS : (row + 1) * COMPS]
-        total = total + jnp.where(lane == 0, col_first[:, row : row + 1], 0.0)
-        total = total + jnp.where(lane == cols - 1, col_last[:, row : row + 1], 0.0)
-        if row == 0:
-            total = total + row_first
-        if row == row_total - 1:
-            total = total + row_last
-        partial[row * COMPS : (row + 1) * COMPS, :] = total
-
-
-def combine(swapped, partial, own, other, load, res, tan):
-    row_total = partial.shape[0] // COMPS
-    held = own.shape[0] // 12
-    skip = row_total - held
-    first, second = own[...], other[...]
-    if swapped:
-        here = lax.axis_index("groups") == 0
-        first, second = jnp.where(here, first, second), jnp.where(here, second, first)
-    for comp in range(12):
-        target = res if comp < 6 else tan
+    pulled = split(2.0 * (ties[...] - fit_value), 2)
+    hot_row = ref["hot_row"][...]
+    places = [comp % 6 + comp // 6 * 8 for comp in range(12)]
+    lhs = [
+        jnp.concatenate([hot_row * part[place_of : place_of + 1] for part in pulled], axis=1)
+        for place_of in places
+    ]
+    hot_col = ref["hot_col"][...]
+    tie_forces = dot(jnp.concatenate(lhs, axis=0), jnp.concatenate([hot_col] * 2, axis=1), ((1,), (1,)))
+
+    assert 4 * row_total <= cols
+    line = jnp.zeros((COMPS, cols), F32)
+    for at, part in enumerate(split(col_first, 2) + split(col_last, 2)):
+        part = part.astype(F32)
+        part = pltpu.roll(part, at * row_total, 1) if at else part
+        line = jnp.where((lane >= at * row_total) & (lane < (at + 1) * row_total), part, line)
+    shape = (row_total, cols)
+    eye = jnp.bitwise_and(lanes_of(shape), row_total - 1) == rows_of(shape)
+    lhs = [jnp.where(eye, line[place_of : place_of + 1], 0.0).astype(BF16) for place_of in places]
+    shape = (cols, cols)
+    in_first = (rows_of(shape) == 0) & (lanes_of(shape) < 2 * row_total)
+    in_last = (rows_of(shape) == cols - 1) & (lanes_of(shape) >= 2 * row_total)
+    ends = (in_first | (in_last & (lanes_of(shape) < 4 * row_total))).astype(F32).astype(BF16)
+    col_forces = dot(jnp.concatenate(lhs, axis=0), ends, ((1,), (1,)))
+
+    row = rows_of((row_total, cols))
+    here = lax.axis_index("groups") == 0
+    for comp, place_of in enumerate(places):
+        rows = slice(comp * row_total, (comp + 1) * row_total)
+        value = tie_forces[rows] + col_forces[rows]
+        value = value + jnp.where(row == 0, row_first[place_of : place_of + 1], 0.0)
+        value = value + jnp.where(row == row_total - 1, row_last[place_of : place_of + 1], 0.0)
+        if comp < 6:
+            value = value - load[rows, :]
+        target = ref["res"] if comp < 6 else ref["tan"]
         start = comp % 6 * row_total
-        value = partial[pl.ds(comp % 6 + comp // 6 * 8, row_total, stride=COMPS), :]
-        if comp < 6:
-            value = value - load[start : start + row_total, :]
-        rows = slice(comp * held, (comp + 1) * held)
         target[start : start + row_total, :] = value
-        target[start : start + held, :] += first[rows]
-        target[start + skip : start + row_total, :] += second[rows]
+        for piece, (low, high) in enumerate(pieces):
+            count = high - low
+            part = slice(comp * count, (comp + 1) * count)
+            first, second = ref[f"own{piece}"][part, :], ref[f"other{piece}"][part, :]
+            if swapped:
+                first, second = jnp.where(here, first, second), jnp.where(here, second, first)
+            target[start + low : start + high, :] += first
+            shift = start + row_total // 2 - 1
+            target[shift + low : shift + high, :] += second
 
 
 def per_device(
@@ -598,50 +618,64 @@
     mate = lax.ppermute(rows, "pb", [(0, 1), (1, 0)])
 
     inputs = tuple(on_chip(value) for value in (fields, fit_disp, fit_dir, node, owner, slot))
-    small = peers * 2 * COMPS * slots <= SMALL
-    ties, cols_out, sums = pl.pallas_call(
-        lambda *refs: sum_ties(peers, *refs),
+    blocks = shape(peers, 3 * COMPS, slots)
+    hbm = pl.BlockSpec(memory_space=pl.ANY)
+    ties, cols_out, hot_col, hot_slot, hot_row, pay = pl.pallas_call(
+        lambda *refs: sum_ties((tx_count, ty_count), *refs),
         out_shape=[
             pltpu.VMEM((COMPS, tie_total), F32),
             pltpu.VMEM((2 * COMPS, cols), F32),
-            (pltpu.VMEM if small else jax.ShapeDtypeStruct)((peers, 2 * COMPS, slots), F32),
+            pltpu.VMEM((cols, tie_total), BF16),
+            pltpu.VMEM((slots, tie_total), BF16),
+            pltpu.VMEM((row_total, tie_total), BF16),
+            blocks,
         ],
         in_specs=local(len(inputs)),
-        out_specs=local(3),
+        out_specs=local(5) + [hbm],
+        scratch_shapes=[pltpu.VMEM((peers, 2 * COMPS, slots), F32), pltpu.SemaphoreType.DMA(())],
         name="sum_ties",
     )(*inputs)
-    inputs = (sums, cols_out, mate, w_first_in, b_first, b_second, w_final)
-    inputs = [on_chip(value) if value.size <= SMALL else value for value in inputs]
-    pay, w_first, w_last, b_cols = pl.pallas_call(
-        lambda *refs: fill_blocks((tx_count, ty_count), row_total, *refs),
+    inputs = [on_chip(value) for value in (mate, w_first_in, b_first, b_second, w_final)] + [pay]
+    w_first, w_last, b_cols, pay = pl.pallas_call(
+        lambda *refs: fill_rows((tx_count, ty_count), *refs),
         out_shape=[
-            shape(peers, 3 * COMPS, slots),
             pltpu.VMEM((8 * hid, 4 * COMPS), BF16),
             pltpu.VMEM((128, hid), BF16),
             pltpu.VMEM((hid, 128), F32),
+            blocks,
         ],
-        in_specs=local(len(inputs)),
-        out_specs=[pl.BlockSpec(memory_space=pl.ANY)] + local(3),
-        scratch_shapes=[pltpu.VMEM((peers, 3 * COMPS, slots), F32), pltpu.SemaphoreType.DMA(())],
-        name="fill_blocks",
+        in_specs=local(5) + [hbm],
+        out_specs=local(3) + [hbm],
+        scratch_shapes=[pltpu.VMEM((peers, COMPS, slots), F32), pltpu.SemaphoreType.DMA(())],
+        input_output_aliases={5: 3},
+        name="fill_rows",
     )(*inputs)
     got = lax.all_to_all(pay, ("tx", "ty"), split_axis=0, concat_axis=0, tiled=True)
 
-    inputs = tuple(on_chip(value) for value in (fields, mate, w_first, w_mid, b_cols, w_last))
     groups = lax.axis_size("groups")
-    halves = []
-    for pick in (None,) if groups == 2 else (0, 1):
-        half = pl.pallas_call(
-            lambda *refs: interior(pick, *refs),
-            out_shape=pltpu.VMEM(((row_total // 2 + 1) * 12, cols), F32),
-            in_specs=local(len(inputs)),
-            out_specs=local(1)[0],
-            scratch_shapes=[pltpu.VMEM(((row_total // 2 + 3) * COMPS, cols), F32)],
-            name="interior",
-        )(*inputs)
-        halves.append(half)
-    if groups == 2:
-        halves.append(lax.ppermute(halves[0], "groups", [(0, 1), (1, 0)]))
+    half = row_total // 2
+    cut = half * 3 // 4 // 2 * 2
+    chunks = [(0, cut), (cut, half)]
+    pieces = [(0, cut - 1), (cut - 1, half + 1)]
+    halves = {}
+    for name, pick in (("own", None),) if groups == 2 else (("own", 0), ("other", 1)):
+        before = ()
+        for piece, (begin, end) in enumerate(chunks):
+            inputs = (fields, mate, w_first, w_mid, b_cols, w_last, *before)
+            low, high = pieces[piece]
+            results = [((high - low) * 12, cols), ((half + 3) * COMPS, cols)]
+            kept = 2 if end < half else 1
+            sent, *before = pl.pallas_call(
+                lambda *refs: interior(pick, begin, end, low, high, *refs),
+                out_shape=[pltpu.VMEM(size, F32) for size in results[:kept]],
+                in_specs=local(len(inputs)),
+                out_specs=local(kept),
+                scratch_shapes=[pltpu.VMEM(size, F32) for size in results[kept:]],
+                name="interior",
+            )(*(on_chip(value) for value in inputs))
+            halves[name + str(piece)] = sent
+            if groups == 2:
+                halves["other" + str(piece)] = lax.ppermute(sent, "groups", [(0, 1), (1, 0)])
 
     named = dict(
         got=got,
@@ -649,34 +683,28 @@
         fields=fields,
         ties=ties,
         cols=cols_out,
+        load=load2,
         w_first=w_first,
         w_mid=w_mid,
         b_mid=b_cols,
         w_last=w_last,
-        node=node,
-        slot=slot,
+        hot_col=hot_col,
+        hot_slot=hot_slot,
+        hot_row=hot_row,
         owner=owner,
         fit_disp=fit_disp,
         fit_dir=fit_dir,
+        **halves,
     )
     named = {name: on_chip(value) if value.size <= SMALL else value for name, value in named.items()}
-    names = list(named)
-    partial, fit_res, fit_tan = pl.pallas_call(
-        lambda *refs: edges(names + ["partial", "fit_res", "fit_tan"], axes, *refs),
-        out_shape=[pltpu.VMEM((row_total * COMPS, cols), F32), shape(6, slots), shape(6, slots)],
-        in_specs=local(len(names)),
-        out_specs=local(3),
-        name="edges",
+    names = list(named) + ["res", "tan", "fit_res", "fit_tan"]
+    res, tan, fit_res, fit_tan = pl.pallas_call(
+        lambda *refs: finish(names, axes, pieces, groups == 2, *refs),
+        out_shape=[shape(*flat), shape(*flat), shape(6, slots), shape(6, slots)],
+        in_specs=local(len(named)),
+        out_specs=local(4),
+        name="finish",
     )(*named.values())
-
-    inputs = tuple(on_chip(value) for value in (partial, halves[0], halves[1], load2))
-    res, tan = pl.pallas_call(
-        lambda *refs: combine(groups == 2, *refs),
-        out_shape=[shape(*flat), shape(*flat)],
-        in_specs=local(len(inputs)),
-        out_specs=local(2),
-        name="combine",
-    )(*inputs)
     cube = displacement.shape
     return (res.reshape(cube), tan.reshape(cube), fit_res, fit_tan)
 

time: 23.1 us -> 26.3 us (1.14)
  waiting for transfers between devices: 1.13 us -> 3.49 us
  Pallas kernels: 11.6 us -> 12.2 us
    ppermute x1 -> x2, waiting for transfers between devices: 0.01 us -> 3.48 us  [per_device(): lax.ppermute(sent, 'groups', [(0, 1), (1, 0)])]
    all_to_all x1, waiting for transfers between devices: 0.97 us -> 0.01 us  [per_device(): lax.all_to_all(pay, ('tx', 'ty'), split_axis=0, concat_axis=0, tiled=True)]
    pallas_call x5, Pallas kernels: 10.5 us -> 11.1 us  [the longest x2 6.25 us: per_device(): pl.pallas_call(lambda *refs: interior(pick, begin, end, low, high, *refs)...]
    ppermute x1 -> x2, starting transfers between devices: 1.6 us -> 2.15 us  [per_device(): lax.ppermute(sent, 'groups', [(0, 1), (1, 0)])]
    all_to_all x1, starting transfers between devices: 7.28 us -> 6.95 us  [per_device(): lax.all_to_all(pay, ('tx', 'ty'), split_axis=0, concat_axis=0, tiled=True)]
  transfers between devices with their start and end apart: 3 -> 4, of which waited for: 2 -> 1; matrix products, arithmetic and copies ran while one was open for 0% -> 0% of each run, Pallas kernels for 39% -> 30%
where the time goes in v7:
time: 26.3 us; the launch traced here: 26.1 us
  Pallas kernels  12.2 us (46%)
  starting transfers between devices  9.66 us (37%)
  waiting for transfers between devices  3.49 us (13%)
  between operations  0.7 us (3%)
    all_to_all x1, starting transfers between devices, per_device(): lax.all_to_all(pay, ('tx', 'ty'), split_axis=0, concat_axis=0, tiled=True)  6.95 us
    pallas_call x2, Pallas kernels, per_device(): pl.pallas_call(lambda *refs: interior(pick, begin, end, low, high, *refs)...  6.25 us
    ppermute x2, waiting for transfers between devices, per_device(): lax.ppermute(sent, 'groups', [(0, 1), (1, 0)])  3.48 us
    pallas_call x1, Pallas kernels, per_device(): pl.pallas_call(lambda *refs: finish(names, axes, pieces, groups == 2, *re...  2.66 us
    ppermute x2, starting transfers between devices, per_device(): lax.ppermute(sent, 'groups', [(0, 1), (1, 0)])  2.15 us
    pallas_call x1, Pallas kernels, per_device(): pl.pallas_call(lambda *refs: sum_ties((tx_count, ty_count), *refs), out_s...  1.47 us
    pallas_call x1, Pallas kernels, per_device(): pl.pallas_call(lambda *refs: gather_nodes(len(smalls), *refs), out_shape=...  1.13 us
    pallas_call x1, Pallas kernels, per_device(): pl.pallas_call(lambda *refs: fill_rows((tx_count, ty_count), *refs), out_...  0.68 us
  transfers between devices with their start and end apart: 4, of which 1 were waited for; matrix products, arithmetic and copies ran while one was open for 0% of the time, Pallas kernels for 30%

profile of v7, /device:TPU:0, one launch (start us, length us, event | category | flops | bytes accessed | tf_op | source)
XLA Modules:
  0.0 26.1 jit_solution(5438675985691802939)
XLA Ops:
  0.6 1.1 %gather_nodes.1 = (f32[512,128]{1,0:T(8,128)S(1)}, f32[32,128]{1,0:T(8,128)S(1)}, f32[6,128]{1,0:T(8,128)S(1)}, f32[6,128]{1,0:T(8,128)S(1)}, s32[6,128]{1,0:T(8...) custom-call(f32[192,128]{1,0:T(8,128)} %bitcast.12, ...), custom_call_target="tpu_custom_call" | custom-call | tf_op jit(solution)/shard_map/gather_nodes/pallas_call | solution.py:609
  1.8 0.6 %collective-permute-start = (f32[32,128]{1,0:T(8,128)S(1)}, f32[32,128]{1,0:T(8,128)S(1)}, u32[]{:S(2)}, u32[]{:S(2)}) collective-permute-start(f32[32,128]{1,0:T(8,128)S(1)} %get-tuple-element.31), channel_id=1, source_target_pairs={{0,1},{1,0},{2,3},{3,2},{4,5},{5,4},{6,7},{7,6},{8,9},{9,8},{10,11... | collective-permute-start | bytes 49160 | tf_op jit(solution)/shard_map/ppermute | solution.py:618
  2.3 1.5 %sum_ties.1 = (f32[16,768]{1,0:T(8,128)S(1)}, f32[32,128]{1,0:T(8,128)S(1)}, bf16[128,768]{1,0:T(8,128)(2,1)S(1)}, bf16[128,768]{1,0:T(8,128)(2,1)S(1)}, bf16[32...) custom-call(f32[512,128]{1,0:T(8,128)S(1)} %get-tuple-element.36.refs_0_.refs_2_, ...), custom_call_target="tpu_custom_call" | custom-call | tf_op jit(solution)/shard_map/sum_ties/pallas_call | solution.py:623
  3.8 0.0 collective-permute-done.refs_0_.refs_1_
  3.8 0.7 %fill_rows.1 = (bf16[2048,64]{1,0:T(8,128)(2,1)S(1)}, bf16[128,256]{1,0:T(8,128)(2,1)S(1)}, f32[256,128]{1,0:T(8,128)S(1)}, f32[8,48,128]{2,1,0:T(8,128)}) custom-call(f32[32,128]{1,0:T(8,128)S(1)} %collective-permute-done.refs_0_.refs_1_, bf16[12,256]{1,0:T(8,128)(2,1)S(1)} %get-tuple-element.32.refs_1_, ...), custom_call_target="tpu_custom_call", output_to_operand_aliasing={{3}: (5, {})} | custom-call | tf_op jit(solution)/shard_map/fill_rows/pallas_call | solution.py:639
  4.5 0.0 copy-start
  4.5 7.0 %all-to-all-start = ((f32[8,48,128]{2,1,0:T(8,128)}), f32[8,48,128]{2,1,0:T(8,128)S(1)}, u32[]{:S(2)}, u32[]{:S(2)}) async-start(f32[8,48,128]{2,1,0:T(8,128)} %get-tuple-element.43), calls=%async_computation | async-start | bytes 393216 | tf_op jit(solution)/shard_map/all_to_all | solution.py:653
  11.5 0.0 copy-done
  11.5 4.4 %interior.2 = (f32[132,128]{1,0:T(8,128)S(1)}, f32[304,128]{1,0:T(8,128)S(1)}) custom-call(f32[512,128]{1,0:T(8,128)S(1)} %get-tuple-element.36.refs_0_.refs_2_, f32[32,128]{1,0:T(8,128)S(1)} %collective-permute-done.refs_0_.refs_1_, bf16[2048,64]{1,0:T(8,128)(2,1)S(1)} %get-tuple-element.46.refs_2_.refs_6_, bf16[256,256]{1,0:T(8,128)(2,1)S(1)} %copy-done, ...), custom_call_target="tpu_custom_call" | custom-call | tf_op jit(solution)/shard_map/interior/pallas_call | solution.py:668
  15.9 1.6 %collective-permute-start.1 = (f32[132,128]{1,0:T(8,128)S(1)}, f32[132,128]{1,0:T(8,128)S(1)}, u32[]{:S(2)}, u32[]{:S(2)}) collective-permute-start(f32[132,128]{1,0:T(8,128)S(1)} %get-tuple-element.52.refs_16_), channel_id=1, source_target_pairs={{0,16},{16,0},{1,17},{17,1},{2,18},{18,2},{3,19},{19,3},{4,20},{20... | collective-permute-start | bytes 202760 | tf_op jit(solution)/shard_map/ppermute | solution.py:678
  17.5 0.0 copy-start.1
  17.5 1.8 %interior.3.refs_18_ = f32[72,128]{1,0:T(8,128)S(1)} custom-call(f32[512,128]{1,0:T(8,128)S(1)} %get-tuple-element.36.refs_0_.refs_2_, f32[32,128]{1,0:T(8,128)S(1)} %collective-permute-done.refs_0_.refs_1_, bf16[2048,64]{1,0:T(8,128)(2,1)S(1)} %get-tuple-element.46.refs_2_.refs_6_, bf16[256,256]{1,0:T(8,128)(2,1)S(1)} %copy-done, ...), custom_call_target="tpu_custom_call" | custom-call | tf_op jit(solution)/shard_map/interior/pallas_call | solution.py:668
  19.4 0.5 %collective-permute-start.2 = (f32[72,128]{1,0:T(8,128)S(1)}, f32[72,128]{1,0:T(8,128)S(1)}, u32[]{:S(2)}, u32[]{:S(2)}) collective-permute-start(f32[72,128]{1,0:T(8,128)S(1)} %interior.3.refs_18_), channel_id=1, source_target_pairs={{0,16},{16,0},{1,17},{17,1},{2,18},{18,2},{3,19},{19,3},{4,20},{20... | collective-permute-start | bytes 110600 | tf_op jit(solution)/shard_map/ppermute | solution.py:678
  19.9 3.5 %collective-permute-done.2.refs_19_ = f32[72,128]{1,0:T(8,128)S(1)} collective-permute-done((f32[72,128]{1,0:T(8,128)S(1)}, f32[72,128]{1,0:T(8,128)S(1)}, u32[]{:S(2)}, u32[]{:S(2)}) %collective-permute-start.2) | collective-permute-done | bytes 36896 | tf_op jit(solution)/shard_map/ppermute | solution.py:678
  23.4 0.0 collective-permute-done.1.refs_17_
  23.4 0.0 all-to-all-done.refs_0_
  23.4 0.0 copy-done.1
  23.4 2.7 %finish.1 = (f32[192,128]{1,0:T(8,128)}, f32[192,128]{1,0:T(8,128)}, f32[6,128]{1,0:T(8,128)}, f32[6,128]{1,0:T(8,128)}) custom-call(f32[8,48,128]{2,1,0:T(8,128)S(1)} %all-to-all-done.refs_0_, f32[32,128]{1,0:T(8,128)S(1)} %collective-permute-done.refs_0_.refs_1_, f32[512,128]{1,0:T(8,128)S(1)} %get-tuple-element.36.refs_0_.refs_2_, ...), custom_call_target="tpu_custom_call" | custom-call | tf_op jit(solution)/shard_map/finish/pallas_call | solution.py:701
Async XLA Ops:
  1.8 2.0 %collective-permute-start = (f32[32,128]{1,0:T(8,128)S(1)}, f32[32,128]{1,0:T(8,128)S(1)}, u32[]{:S(2)}, u32[]{:S(2)}) collective-permute-start(f32[32,128]{1,0:T(8,128)S(1)} %get-tuple-element.31), channel_id=1, source_target_pairs={{0,1},{1,0},{2,3},{3,2},{4,5},{5,4},{6,7},{7,6},{8,9},{9,8},{10,11... | collective-permute-start | bytes 49160 | tf_op jit(solution)/shard_map/ppermute | solution.py:618
  4.5 7.0 %copy-start = (bf16[256,256]{1,0:T(8,128)(2,1)S(1)}, bf16[256,256]{1,0:T(8,128)(2,1)}, u32[]{:S(2)}) copy-start(bf16[256,256]{1,0:T(8,128)(2,1)} %refs_7_.1) | copy-start | bytes 393220
  4.5 18.9 %all-to-all-start = ((f32[8,48,128]{2,1,0:T(8,128)}), f32[8,48,128]{2,1,0:T(8,128)S(1)}, u32[]{:S(2)}, u32[]{:S(2)}) async-start(f32[8,48,128]{2,1,0:T(8,128)} %get-tuple-element.43), calls=%async_computation | async-start | bytes 393216 | tf_op jit(solution)/shard_map/all_to_all | solution.py:653
  15.9 7.5 %collective-permute-start.1 = (f32[132,128]{1,0:T(8,128)S(1)}, f32[132,128]{1,0:T(8,128)S(1)}, u32[]{:S(2)}, u32[]{:S(2)}) collective-permute-start(f32[132,128]{1,0:T(8,128)S(1)} %get-tuple-element.52.refs_16_), channel_id=1, source_target_pairs={{0,16},{16,0},{1,17},{17,1},{2,18},{18,2},{3,19},{19,3},{4,20},{20... | collective-permute-start | bytes 202760 | tf_op jit(solution)/shard_map/ppermute | solution.py:678
  17.5 5.9 %copy-start.1 = (f32[6,32,128]{2,1,0:T(8,128)S(1)}, f32[6,32,128]{2,1,0:T(8,128)}, u32[]{:S(2)}) copy-start(f32[6,32,128]{2,1,0:T(8,128)} %param.15) | copy-start | bytes 294916
  19.4 4.0 %collective-permute-start.2 = (f32[72,128]{1,0:T(8,128)S(1)}, f32[72,128]{1,0:T(8,128)S(1)}, u32[]{:S(2)}, u32[]{:S(2)}) collective-permute-start(f32[72,128]{1,0:T(8,128)S(1)} %interior.3.refs_18_), channel_id=1, source_target_pairs={{0,16},{16,0},{1,17},{17,1},{2,18},{18,2},{3,19},{19,3},{4,20},{20... | collective-permute-start | bytes 110600 | tf_op jit(solution)/shard_map/ppermute | solution.py:678

commit v8 on v6

--- a/solution.py
+++ b/solution.py
@@ -158,7 +158,8 @@
 
 
 def sum_ties(peers, *refs):
-    (fields, fit_disp, fit_dir, node_ref, owner_ref, slot_ref, ties, col_out, pay) = refs
+    (fields, fit_disp, fit_dir, node_ref, owner_ref, slot_ref) = refs[:6]
+    (ties, col_out, hot_col_out, hot_slot_out, hot_row_out, pay) = refs[6:]
     row_total = fields.shape[0] // COMPS
     cols = fields.shape[1]
     slots = fit_disp.shape[1]
@@ -178,6 +179,8 @@
     node_row = lax.shift_right_logical(node, cols.bit_length() - 1)
     node_col = jnp.bitwise_and(node, cols - 1)
     hot_col = one_hot(node_col, cols)
+    hot_col_out[...] = hot_col
+    hot_row_out[...] = one_hot(node_row, row_total)
     wide = dot(
         jnp.concatenate(split(fields[...], 2), axis=1), jnp.concatenate([hot_col] * 2, axis=0)
     )
@@ -188,6 +191,7 @@
     ties[...] = value
     stack = jnp.concatenate(split(value, 2), axis=0)
     hot_slot = one_hot(slot, slots)
+    hot_slot_out[...] = hot_slot
     fitting = paired(fit_disp[...], fit_dir[...])
 
     def bins(first, count):
@@ -465,10 +469,8 @@
     s_right = mask(s_right, valid)
     col_last = pltpu.roll(pltpu.roll(s_base, back, 1) + s_right, cols - half, 1)
 
-    node = as_line(ref["node"])
-    slot = as_line(ref["slot"])
     owner = ref["owner"][...]
-    hot_slot = one_hot(slot, slots)
+    hot_slot = ref["hot_slot"][...]
     hot_two = jnp.concatenate([hot_slot] * 2, axis=0)
     fit_value = jnp.zeros((COMPS, tie_total), F32)
     bins = jnp.zeros((COMPS, slots), F32)
@@ -495,48 +497,55 @@
     for out, fit, base in (("fit_res", "fit_disp", 0), ("fit_tan", "fit_dir", 8)):
         ref[out][...] = 2.0 * (count * ref[fit][...] - bins[base : base + 6])
 
-    pulled = 2.0 * (ties[...] - fit_value)
-    node_row = lax.shift_right_logical(node, cols.bit_length() - 1)
-    node_col = jnp.bitwise_and(node, cols - 1)
-    hot_col = one_hot(node_col, cols)
-    sides = split(pulled, 2)
-    lhs = []
-    for row in range(row_total):
-        hit = (node_row == row).astype(F32).astype(BF16)
-        lhs.append(jnp.concatenate([side * hit for side in sides], axis=1))
-    tie_forces = dot(
-        jnp.concatenate(lhs, axis=0), jnp.concatenate([hot_col] * 2, axis=1), ((1,), (1,))
-    )
-
-    for row in range(row_total):
-        total = tie_forces[row * COMPS : (row + 1) * COMPS]
-        total = total + jnp.where(lane == 0, col_first[:, row : row + 1], 0.0)
-        total = total + jnp.where(lane == cols - 1, col_last[:, row : row + 1], 0.0)
-        if row == 0:
-            total = total + row_first
-        if row == row_total - 1:
-            total = total + row_last
-        partial[row * COMPS : (row + 1) * COMPS, :] = total
-
-
-def combine(swapped, partial, own, other, load, res, tan):
-    row_total = partial.shape[0] // COMPS
+    pulled = split(2.0 * (ties[...] - fit_value), 2)
+    hot_row = ref["hot_row"][...]
+    places = [comp % 6 + comp // 6 * 8 for comp in range(12)]
+    lhs = [
+        jnp.concatenate([hot_row * part[place_of : place_of + 1] for part in pulled], axis=1)
+        for place_of in places
+    ]
+    hot_col = ref["hot_col"][...]
+    tie_forces = dot(jnp.concatenate(lhs, axis=0), jnp.concatenate([hot_col] * 2, axis=1), ((1,), (1,)))
+
+    assert 4 * row_total <= cols
+    line = jnp.zeros((COMPS, cols), F32)
+    for at, part in enumerate(split(col_first, 2) + split(col_last, 2)):
+        part = part.astype(F32)
+        part = pltpu.roll(part, at * row_total, 1) if at else part
+        line = jnp.where((lane >= at * row_total) & (lane < (at + 1) * row_total), part, line)
+    shape = (row_total, cols)
+    eye = jnp.bitwise_and(lanes_of(shape), row_total - 1) == rows_of(shape)
+    lhs = [jnp.where(eye, line[place_of : place_of + 1], 0.0).astype(BF16) for place_of in places]
+    shape = (cols, cols)
+    in_first = (rows_of(shape) == 0) & (lanes_of(shape) < 2 * row_total)
+    in_last = (rows_of(shape) == cols - 1) & (lanes_of(shape) >= 2 * row_total)
+    ends = (in_first | (in_last & (lanes_of(shape) < 4 * row_total))).astype(F32).astype(BF16)
+    col_forces = dot(jnp.concatenate(lhs, axis=0), ends, ((1,), (1,)))
+
+    row = rows_of((row_total, cols))
+    for comp, place_of in enumerate(places):
+        rows = slice(comp * row_total, (comp + 1) * row_total)
+        value = tie_forces[rows] + col_forces[rows]
+        value = value + jnp.where(row == 0, row_first[place_of : place_of + 1], 0.0)
+        value = value + jnp.where(row == row_total - 1, row_last[place_of : place_of + 1], 0.0)
+        partial[rows, :] = value - ref["load"][rows, :] if comp < 6 else value
+
+
+def combine(swapped, partial, own, other, res, tan):
+    row_total = partial.shape[0] // 12
     held = own.shape[0] // 12
     skip = row_total - held
-    first, second = own[...], other[...]
-    if swapped:
-        here = lax.axis_index("groups") == 0
-        first, second = jnp.where(here, first, second), jnp.where(here, second, first)
+    here = lax.axis_index("groups") == 0
     for comp in range(12):
         target = res if comp < 6 else tan
         start = comp % 6 * row_total
-        value = partial[pl.ds(comp % 6 + comp // 6 * 8, row_total, stride=COMPS), :]
-        if comp < 6:
-            value = value - load[start : start + row_total, :]
         rows = slice(comp * held, (comp + 1) * held)
-        target[start : start + row_total, :] = value
-        target[start : start + held, :] += first[rows]
-        target[start + skip : start + row_total, :] += second[rows]
+        first, second = own[rows, :], other[rows, :]
+        if swapped:
+            first, second = jnp.where(here, first, second), jnp.where(here, second, first)
+        target[start : start + row_total, :] = partial[comp * row_total : (comp + 1) * row_total, :]
+        target[start : start + held, :] += first
+        target[start + skip : start + row_total, :] += second
 
 
 def per_device(
@@ -599,15 +608,18 @@
 
     inputs = tuple(on_chip(value) for value in (fields, fit_disp, fit_dir, node, owner, slot))
     small = peers * 2 * COMPS * slots <= SMALL
-    ties, cols_out, sums = pl.pallas_call(
+    ties, cols_out, hot_col, hot_slot, hot_row, sums = pl.pallas_call(
         lambda *refs: sum_ties(peers, *refs),
         out_shape=[
             pltpu.VMEM((COMPS, tie_total), F32),
             pltpu.VMEM((2 * COMPS, cols), F32),
+            pltpu.VMEM((cols, tie_total), BF16),
+            pltpu.VMEM((slots, tie_total), BF16),
+            pltpu.VMEM((row_total, tie_total), BF16),
             (pltpu.VMEM if small else jax.ShapeDtypeStruct)((peers, 2 * COMPS, slots), F32),
         ],
         in_specs=local(len(inputs)),
-        out_specs=local(3),
+        out_specs=local(6),
         name="sum_ties",
     )(*inputs)
     inputs = (sums, cols_out, mate, w_first_in, b_first, b_second, w_final)
@@ -653,8 +665,10 @@
         w_mid=w_mid,
         b_mid=b_cols,
         w_last=w_last,
-        node=node,
-        slot=slot,
+        hot_col=hot_col,
+        hot_slot=hot_slot,
+        hot_row=hot_row,
+        load=load2,
         owner=owner,
         fit_disp=fit_disp,
         fit_dir=fit_dir,
@@ -663,13 +677,13 @@
     names = list(named)
     partial, fit_res, fit_tan = pl.pallas_call(
         lambda *refs: edges(names + ["partial", "fit_res", "fit_tan"], axes, *refs),
-        out_shape=[pltpu.VMEM((row_total * COMPS, cols), F32), shape(6, slots), shape(6, slots)],
+        out_shape=[pltpu.VMEM((12 * row_total, cols), F32), shape(6, slots), shape(6, slots)],
         in_specs=local(len(names)),
         out_specs=local(3),
         name="edges",
     )(*named.values())
 
-    inputs = tuple(on_chip(value) for value in (partial, halves[0], halves[1], load2))
+    inputs = tuple(on_chip(value) for value in (partial, halves[0], halves[1]))
     res, tan = pl.pallas_call(
         lambda *refs: combine(groups == 2, *refs),
         out_shape=[shape(*flat), shape(*flat)],

time: 23.1 us -> 23.1 us (level)
  no operation moved by 1% of the time
where the time goes in v8:
time: 23.1 us; the launch traced here: 22.8 us
  Pallas kernels  11.6 us (50%)
  starting transfers between devices  9.41 us (41%)
  waiting for transfers between devices  1.12 us (5%)
  between operations  0.68 us (3%)
    all_to_all x1, starting transfers between devices, per_device(): lax.all_to_all(pay, ('tx', 'ty'), split_axis=0, concat_axis=0, tiled=True)  7.28 us
    pallas_call x1, Pallas kernels, per_device(): pl.pallas_call(lambda *refs: interior(pick, *refs), out_shape=pltpu.VMEM(...  5.71 us
    pallas_call x1, Pallas kernels, per_device(): pl.pallas_call(lambda *refs: edges(names + ['partial', 'fit_res', 'fit_ta...  2.49 us
    ppermute x1, starting transfers between devices, per_device(): halves.append(lax.ppermute(halves[0], 'groups', [(0, 1), (1, 0)]))  1.58 us
    pallas_call x1, Pallas kernels, per_device(): pl.pallas_call(lambda *refs: gather_nodes(len(smalls), *refs), out_shape=...  1.13 us
    all_to_all x1, waiting for transfers between devices, per_device(): lax.all_to_all(pay, ('tx', 'ty'), split_axis=0, concat_axis=0, tiled=True)  0.97 us
    pallas_call x1, Pallas kernels, per_device(): pl.pallas_call(lambda *refs: fill_blocks((tx_count, ty_count), row_total,...  0.86 us
    pallas_call x1, Pallas kernels, per_device(): pl.pallas_call(lambda *refs: combine(groups == 2, *refs), out_shape=[shap...  0.72 us
  transfers between devices with their start and end apart: 3, of which 2 were waited for; matrix products, arithmetic and copies ran while one was open for 0% of the time, Pallas kernels for 39%

profile of v8, /device:TPU:0, one launch (start us, length us, event | category | flops | bytes accessed | tf_op | source)
XLA Modules:
  0.0 22.8 jit_solution(2678081561944199399)
XLA Ops:
  0.6 1.1 %gather_nodes.1 = (f32[512,128]{1,0:T(8,128)S(1)}, f32[32,128]{1,0:T(8,128)S(1)}, f32[6,128]{1,0:T(8,128)S(1)}, f32[6,128]{1,0:T(8,128)S(1)}, s32[6,128]{1,0:T(8...) custom-call(f32[192,128]{1,0:T(8,128)} %bitcast.12, ...), custom_call_target="tpu_custom_call" | custom-call | tf_op jit(solution)/shard_map/gather_nodes/pallas_call | solution.py:598
  1.8 0.6 %collective-permute-start = (f32[32,128]{1,0:T(8,128)S(1)}, f32[32,128]{1,0:T(8,128)S(1)}, u32[]{:S(2)}, u32[]{:S(2)}) collective-permute-start(f32[32,128]{1,0:T(8,128)S(1)} %get-tuple-element.38), channel_id=1, source_target_pairs={{0,1},{1,0},{2,3},{3,2},{4,5},{5,4},{6,7},{7,6},{8,9},{9,8},{10,11... | collective-permute-start | bytes 49160 | tf_op jit(solution)/shard_map/ppermute | solution.py:607
  2.3 0.7 %sum_ties.1 = (f32[16,768]{1,0:T(8,128)S(1)}, f32[32,128]{1,0:T(8,128)S(1)}, bf16[128,768]{1,0:T(8,128)(2,1)S(1)}, bf16[128,768]{1,0:T(8,128)(2,1)S(1)}, bf16[32...) custom-call(f32[512,128]{1,0:T(8,128)S(1)} %get-tuple-element.30.refs_0_.refs_2_, ...), custom_call_target="tpu_custom_call" | custom-call | tf_op jit(solution)/shard_map/sum_ties/pallas_call | solution.py:611
  3.0 0.1 collective-permute-done.refs_2_.refs_1_
  3.2 0.9 %fill_blocks.1 = (f32[8,48,128]{2,1,0:T(8,128)}, bf16[2048,64]{1,0:T(8,128)(2,1)S(1)}, bf16[128,256]{1,0:T(8,128)(2,1)S(1)}, f32[256,128]{1,0:T(8,128)S(1)}) custom-call(f32[8,32,128]{2,1,0:T(8,128)S(1)} %get-tuple-element.36.refs_0_, f32[32,128]{1,0:T(8,128)S(1)} %get-tuple-element.37.refs_1_.refs_4_, f32[32,128]{1,0:T(8,128)S(1)} %collective-permute-done.refs_2_.refs_1_, ...), custom_call_target="tpu_custom_call" | custom-call | tf_op jit(solution)/shard_map/fill_blocks/pallas_call | solution.py:627
  4.0 0.0 copy-start
  4.0 7.3 %all-to-all-start = ((f32[8,48,128]{2,1,0:T(8,128)}), f32[8,48,128]{2,1,0:T(8,128)S(1)}, u32[]{:S(2)}, u32[]{:S(2)}) async-start(f32[8,48,128]{2,1,0:T(8,128)} %get-tuple-element.43), calls=%async_computation | async-start | bytes 393216 | tf_op jit(solution)/shard_map/all_to_all | solution.py:640
  11.3 0.0 copy-done
  11.3 0.0 copy-start.1
  11.3 5.7 %interior.1.refs_1_ = f32[204,128]{1,0:T(8,128)S(1)} custom-call(f32[512,128]{1,0:T(8,128)S(1)} %get-tuple-element.30.refs_0_.refs_2_, f32[32,128]{1,0:T(8,128)S(1)} %collective-permute-done.refs_2_.refs_1_, bf16[2048,64]{1,0:T(8,128)(2,1)S(1)} %get-tuple-element.45.refs_5_.refs_2_, bf16[256,256]{1,0:T(8,128)(2,1)S(1)} %copy-done, ...), custom_call_target="tpu_custom_call" | custom-call | tf_op jit(solution)/shard_map/interior/pallas_call | solution.py:646
  17.1 1.6 %collective-permute-start.1 = (f32[204,128]{1,0:T(8,128)S(1)}, f32[204,128]{1,0:T(8,128)S(1)}, u32[]{:S(2)}, u32[]{:S(2)}) collective-permute-start(f32[204,128]{1,0:T(8,128)S(1)} %interior.1.refs_1_), channel_id=1, source_target_pairs={{0,16},{16,0},{1,17},{17,1},{2,18},{18,2},{3,19},{19,3},{4,20},{20... | collective-permute-start | bytes 313352 | tf_op jit(solution)/shard_map/ppermute | solution.py:656
  18.6 1.0 %all-to-all-done.refs_0_ = f32[8,48,128]{2,1,0:T(8,128)S(1)} async-done(((f32[8,48,128]{2,1,0:T(8,128)}), f32[8,48,128]{2,1,0:T(8,128)S(1)}, u32[]{:S(2)}, u32[]{:S(2)}) %all-to-all-start) | async-done | bytes 196640 | tf_op jit(solution)/shard_map/all_to_all | solution.py:640
  19.6 0.0 copy-done.1
  19.6 2.5 %edges.1 = (f32[384,128]{1,0:T(8,128)S(1)}, f32[6,128]{1,0:T(8,128)}, f32[6,128]{1,0:T(8,128)}) custom-call(f32[8,48,128]{2,1,0:T(8,128)S(1)} %all-to-all-done.refs_0_, f32[32,128]{1,0:T(8,128)S(1)} %collective-permute-done.refs_2_.refs_1_, f32[512,128]{1,0:T(8,128)S(1)} %get-tuple-element.30.refs_0_.refs_2_, f32[16,768]{1,0:T(8,128)S(1)} %get-tuple-element.44.refs_3_, ...), custom_call_target="tpu_custom_call" | custom-call | tf_op jit(solution)/shard_map/edges/pallas_call | solution.py:678
  22.1 0.0 collective-permute-done.1.refs_2_
  22.1 0.7 %combine.1 = (f32[192,128]{1,0:T(8,128)}, f32[192,128]{1,0:T(8,128)}) custom-call(f32[384,128]{1,0:T(8,128)S(1)} %get-tuple-element.51.refs_0_, f32[204,128]{1,0:T(8,128)S(1)} %interior.1.refs_1_, f32[204,128]{1,0:T(8,128)S(1)} %collective-permute-done.1.refs_2_), custom_call_target="tpu_custom_call" | custom-call | tf_op jit(solution)/shard_map/combine/pallas_call | solution.py:687
Async XLA Ops:
  1.8 1.4 %collective-permute-start = (f32[32,128]{1,0:T(8,128)S(1)}, f32[32,128]{1,0:T(8,128)S(1)}, u32[]{:S(2)}, u32[]{:S(2)}) collective-permute-start(f32[32,128]{1,0:T(8,128)S(1)} %get-tuple-element.38), channel_id=1, source_target_pairs={{0,1},{1,0},{2,3},{3,2},{4,5},{5,4},{6,7},{7,6},{8,9},{9,8},{10,11... | collective-permute-start | bytes 49160 | tf_op jit(solution)/shard_map/ppermute | solution.py:607
  4.0 7.3 %copy-start = (bf16[256,256]{1,0:T(8,128)(2,1)S(1)}, bf16[256,256]{1,0:T(8,128)(2,1)}, u32[]{:S(2)}) copy-start(bf16[256,256]{1,0:T(8,128)(2,1)} %refs_3_.3) | copy-start | bytes 393220
  4.0 15.6 %all-to-all-start = ((f32[8,48,128]{2,1,0:T(8,128)}), f32[8,48,128]{2,1,0:T(8,128)S(1)}, u32[]{:S(2)}, u32[]{:S(2)}) async-start(f32[8,48,128]{2,1,0:T(8,128)} %get-tuple-element.43), calls=%async_computation | async-start | bytes 393216 | tf_op jit(solution)/shard_map/all_to_all | solution.py:640
  11.3 8.3 %copy-start.1 = (f32[6,32,128]{2,1,0:T(8,128)S(1)}, f32[6,32,128]{2,1,0:T(8,128)}, u32[]{:S(2)}) copy-start(f32[6,32,128]{2,1,0:T(8,128)} %param.15) | copy-start | bytes 294916
  17.1 5.0 %collective-permute-start.1 = (f32[204,128]{1,0:T(8,128)S(1)}, f32[204,128]{1,0:T(8,128)S(1)}, u32[]{:S(2)}, u32[]{:S(2)}) collective-permute-start(f32[204,128]{1,0:T(8,128)S(1)} %interior.1.refs_1_), channel_id=1, source_target_pairs={{0,16},{16,0},{1,17},{17,1},{2,18},{18,2},{3,19},{19,3},{4,20},{20... | collective-permute-start | bytes 313352 | tf_op jit(solution)/shard_map/ppermute | solution.py:656

commit v9 on v8

--- a/solution.py
+++ b/solution.py
@@ -531,7 +531,9 @@
         partial[rows, :] = value - ref["load"][rows, :] if comp < 6 else value
 
 
-def combine(swapped, partial, own, other, res, tan):
+def combine(swapped, partial, own, other, fit_one, fit_two, res, tan, fit_res, fit_tan):
+    fit_res[...] = fit_one[...]
+    fit_tan[...] = fit_two[...]
     row_total = partial.shape[0] // 12
     held = own.shape[0] // 12
     skip = row_total - held
@@ -675,20 +677,20 @@
     )
     named = {name: on_chip(value) if value.size <= SMALL else value for name, value in named.items()}
     names = list(named)
-    partial, fit_res, fit_tan = pl.pallas_call(
+    partial, fit_one, fit_two = pl.pallas_call(
         lambda *refs: edges(names + ["partial", "fit_res", "fit_tan"], axes, *refs),
-        out_shape=[pltpu.VMEM((12 * row_total, cols), F32), shape(6, slots), shape(6, slots)],
+        out_shape=[pltpu.VMEM(size, F32) for size in ((12 * row_total, cols), (6, slots), (6, slots))],
         in_specs=local(len(names)),
         out_specs=local(3),
         name="edges",
     )(*named.values())
 
-    inputs = tuple(on_chip(value) for value in (partial, halves[0], halves[1]))
-    res, tan = pl.pallas_call(
+    inputs = tuple(on_chip(value) for value in (partial, halves[0], halves[1], fit_one, fit_two))
+    res, tan, fit_res, fit_tan = pl.pallas_call(
         lambda *refs: combine(groups == 2, *refs),
-        out_shape=[shape(*flat), shape(*flat)],
+        out_shape=[shape(*flat), shape(*flat), shape(6, slots), shape(6, slots)],
         in_specs=local(len(inputs)),
-        out_specs=local(2),
+        out_specs=local(4),
         name="combine",
     )(*inputs)
     cube = displacement.shape

time: 23.1 us -> 22.9 us (level)
  Pallas kernels: 11.6 us -> 11.1 us
  waiting for transfers between devices: 1.12 us -> 1.43 us
    pallas_call x1, Pallas kernels: 2.49 us -> 1.95 us  [per_device(): pl.pallas_call(lambda *refs: edges(names + ['partial', 'fit_res', 'fit_ta...]
    ppermute x1, waiting for transfers between devices: 0.01 us -> 0.31 us  [per_device(): halves.append(lax.ppermute(halves[0], 'groups', [(0, 1), (1, 0)]))]
  transfers between devices with their start and end apart: 3 -> 3, of which waited for: 2 -> 3; matrix products, arithmetic and copies ran while one was open for 0% -> 0% of each run, Pallas kernels for 39% -> 37%
where the time goes in v9:
time: 22.9 us; the launch traced here: 22.6 us
  Pallas kernels  11.1 us (48%)
  starting transfers between devices  9.41 us (41%)
  waiting for transfers between devices  1.43 us (6%)
  between operations  0.69 us (3%)
    all_to_all x1, starting transfers between devices, per_device(): lax.all_to_all(pay, ('tx', 'ty'), split_axis=0, concat_axis=0, tiled=True)  7.28 us
    pallas_call x1, Pallas kernels, per_device(): pl.pallas_call(lambda *refs: interior(pick, *refs), out_shape=pltpu.VMEM(...  5.71 us
    pallas_call x1, Pallas kernels, per_device(): pl.pallas_call(lambda *refs: edges(names + ['partial', 'fit_res', 'fit_ta...  1.95 us
    ppermute x1, starting transfers between devices, per_device(): halves.append(lax.ppermute(halves[0], 'groups', [(0, 1), (1, 0)]))  1.57 us
    pallas_call x1, Pallas kernels, per_device(): pl.pallas_call(lambda *refs: gather_nodes(len(smalls), *refs), out_shape=...  1.13 us
    all_to_all x1, waiting for transfers between devices, per_device(): lax.all_to_all(pay, ('tx', 'ty'), split_axis=0, concat_axis=0, tiled=True)  0.98 us
    pallas_call x1, Pallas kernels, per_device(): pl.pallas_call(lambda *refs: fill_blocks((tx_count, ty_count), row_total,...  0.86 us
    pallas_call x1, Pallas kernels, per_device(): pl.pallas_call(lambda *refs: combine(groups == 2, *refs), out_shape=[shap...  0.73 us
  transfers between devices with their start and end apart: 3, of which 3 were waited for; matrix products, arithmetic and copies ran while one was open for 0% of the time, Pallas kernels for 37%

profile of v9, /device:TPU:0, one launch (start us, length us, event | category | flops | bytes accessed | tf_op | source)
XLA Modules:
  0.0 22.6 jit_solution(11851207521752751636)
XLA Ops:
  0.6 1.1 %gather_nodes.1 = (f32[512,128]{1,0:T(8,128)S(1)}, f32[32,128]{1,0:T(8,128)S(1)}, f32[6,128]{1,0:T(8,128)S(1)}, f32[6,128]{1,0:T(8,128)S(1)}, s32[6,128]{1,0:T(8...) custom-call(f32[192,128]{1,0:T(8,128)} %bitcast.12, ...), custom_call_target="tpu_custom_call" | custom-call | tf_op jit(solution)/shard_map/gather_nodes/pallas_call | solution.py:600
  1.8 0.6 %collective-permute-start = (f32[32,128]{1,0:T(8,128)S(1)}, f32[32,128]{1,0:T(8,128)S(1)}, u32[]{:S(2)}, u32[]{:S(2)}) collective-permute-start(f32[32,128]{1,0:T(8,128)S(1)} %get-tuple-element.40), channel_id=1, source_target_pairs={{0,1},{1,0},{2,3},{3,2},{4,5},{5,4},{6,7},{7,6},{8,9},{9,8},{10,11... | collective-permute-start | bytes 49160 | tf_op jit(solution)/shard_map/ppermute | solution.py:609
  2.3 0.7 %sum_ties.1 = (f32[16,768]{1,0:T(8,128)S(1)}, f32[32,128]{1,0:T(8,128)S(1)}, bf16[128,768]{1,0:T(8,128)(2,1)S(1)}, bf16[128,768]{1,0:T(8,128)(2,1)S(1)}, bf16[32...) custom-call(f32[512,128]{1,0:T(8,128)S(1)} %get-tuple-element.32.refs_0_.refs_2_, ...), custom_call_target="tpu_custom_call" | custom-call | tf_op jit(solution)/shard_map/sum_ties/pallas_call | solution.py:613
  3.0 0.1 collective-permute-done.refs_2_.refs_1_
  3.2 0.9 %fill_blocks.1 = (f32[8,48,128]{2,1,0:T(8,128)}, bf16[2048,64]{1,0:T(8,128)(2,1)S(1)}, bf16[128,256]{1,0:T(8,128)(2,1)S(1)}, f32[256,128]{1,0:T(8,128)S(1)}) custom-call(f32[8,32,128]{2,1,0:T(8,128)S(1)} %get-tuple-element.38.refs_0_, f32[32,128]{1,0:T(8,128)S(1)} %get-tuple-element.39.refs_1_.refs_4_, f32[32,128]{1,0:T(8,128)S(1)} %collective-permute-done.refs_2_.refs_1_, ...), custom_call_target="tpu_custom_call" | custom-call | tf_op jit(solution)/shard_map/fill_blocks/pallas_call | solution.py:629
  4.0 0.0 copy-start
  4.0 7.3 %all-to-all-start = ((f32[8,48,128]{2,1,0:T(8,128)}), f32[8,48,128]{2,1,0:T(8,128)S(1)}, u32[]{:S(2)}, u32[]{:S(2)}) async-start(f32[8,48,128]{2,1,0:T(8,128)} %get-tuple-element.45), calls=%async_computation | async-start | bytes 393216 | tf_op jit(solution)/shard_map/all_to_all | solution.py:642
  11.3 0.0 copy-done
  11.3 0.0 copy-start.1
  11.3 5.7 %interior.1.refs_1_ = f32[204,128]{1,0:T(8,128)S(1)} custom-call(f32[512,128]{1,0:T(8,128)S(1)} %get-tuple-element.32.refs_0_.refs_2_, f32[32,128]{1,0:T(8,128)S(1)} %collective-permute-done.refs_2_.refs_1_, bf16[2048,64]{1,0:T(8,128)(2,1)S(1)} %get-tuple-element.47.refs_5_.refs_2_, bf16[256,256]{1,0:T(8,128)(2,1)S(1)} %copy-done, ...), custom_call_target="tpu_custom_call" | custom-call | tf_op jit(solution)/shard_map/interior/pallas_call | solution.py:648
  17.1 1.6 %collective-permute-start.1 = (f32[204,128]{1,0:T(8,128)S(1)}, f32[204,128]{1,0:T(8,128)S(1)}, u32[]{:S(2)}, u32[]{:S(2)}) collective-permute-start(f32[204,128]{1,0:T(8,128)S(1)} %interior.1.refs_1_), channel_id=1, source_target_pairs={{0,16},{16,0},{1,17},{17,1},{2,18},{18,2},{3,19},{19,3},{4,20},{20... | collective-permute-start | bytes 313352 | tf_op jit(solution)/shard_map/ppermute | solution.py:658
  18.6 1.0 %all-to-all-done.refs_0_ = f32[8,48,128]{2,1,0:T(8,128)S(1)} async-done(((f32[8,48,128]{2,1,0:T(8,128)}), f32[8,48,128]{2,1,0:T(8,128)S(1)}, u32[]{:S(2)}, u32[]{:S(2)}) %all-to-all-start) | async-done | bytes 196640 | tf_op jit(solution)/shard_map/all_to_all | solution.py:642
  19.6 0.0 copy-done.1
  19.6 2.0 %edges.1 = (f32[384,128]{1,0:T(8,128)S(1)}, f32[6,128]{1,0:T(8,128)S(1)}, f32[6,128]{1,0:T(8,128)S(1)}) custom-call(f32[8,48,128]{2,1,0:T(8,128)S(1)} %all-to-all-done.refs_0_, f32[32,128]{1,0:T(8,128)S(1)} %collective-permute-done.refs_2_.refs_1_, f32[512,128]{1,0:T(8,128)S(1)} %get-tuple-element.32.refs_0_.refs_2_, ...), custom_call_target="tpu_custom_call" | custom-call | tf_op jit(solution)/shard_map/edges/pallas_call | solution.py:680
  21.6 0.3 %collective-permute-done.1.refs_2_ = f32[204,128]{1,0:T(8,128)S(1)} collective-permute-done((f32[204,128]{1,0:T(8,128)S(1)}, f32[204,128]{1,0:T(8,128)S(1)}, u32[]{:S(2)}, u32[]{:S(2)}) %collective-permute-start.1) | collective-permute-done | bytes 104480 | tf_op jit(solution)/shard_map/ppermute | solution.py:658
  21.9 0.7 %combine.1 = (f32[192,128]{1,0:T(8,128)}, f32[192,128]{1,0:T(8,128)}, f32[6,128]{1,0:T(8,128)}, f32[6,128]{1,0:T(8,128)}) custom-call(f32[384,128]{1,0:T(8,128)S(1)} %get-tuple-element.53.refs_0_, f32[204,128]{1,0:T(8,128)S(1)} %interior.1.refs_1_, f32[204,128]{1,0:T(8,128)S(1)} %collective-permute-done.1.refs_2_, f32[6,128]{1,0:T(8,128)S(1)} %get-tuple-element.54.refs_3_, ...), custom_call_target="tpu_custom_call" | custom-call | tf_op jit(solution)/shard_map/combine/pallas_call | solution.py:689
Async XLA Ops:
  1.8 1.4 %collective-permute-start = (f32[32,128]{1,0:T(8,128)S(1)}, f32[32,128]{1,0:T(8,128)S(1)}, u32[]{:S(2)}, u32[]{:S(2)}) collective-permute-start(f32[32,128]{1,0:T(8,128)S(1)} %get-tuple-element.40), channel_id=1, source_target_pairs={{0,1},{1,0},{2,3},{3,2},{4,5},{5,4},{6,7},{7,6},{8,9},{9,8},{10,11... | collective-permute-start | bytes 49160 | tf_op jit(solution)/shard_map/ppermute | solution.py:609
  4.0 7.3 %copy-start = (bf16[256,256]{1,0:T(8,128)(2,1)S(1)}, bf16[256,256]{1,0:T(8,128)(2,1)}, u32[]{:S(2)}) copy-start(bf16[256,256]{1,0:T(8,128)(2,1)} %refs_3_.3) | copy-start | bytes 393220
  4.0 15.6 %all-to-all-start = ((f32[8,48,128]{2,1,0:T(8,128)}), f32[8,48,128]{2,1,0:T(8,128)S(1)}, u32[]{:S(2)}, u32[]{:S(2)}) async-start(f32[8,48,128]{2,1,0:T(8,128)} %get-tuple-element.45), calls=%async_computation | async-start | bytes 393216 | tf_op jit(solution)/shard_map/all_to_all | solution.py:642
  11.3 8.3 %copy-start.1 = (f32[6,32,128]{2,1,0:T(8,128)S(1)}, f32[6,32,128]{2,1,0:T(8,128)}, u32[]{:S(2)}) copy-start(f32[6,32,128]{2,1,0:T(8,128)} %param.15) | copy-start | bytes 294916
  17.1 4.8 %collective-permute-start.1 = (f32[204,128]{1,0:T(8,128)S(1)}, f32[204,128]{1,0:T(8,128)S(1)}, u32[]{:S(2)}, u32[]{:S(2)}) collective-permute-start(f32[204,128]{1,0:T(8,128)S(1)} %interior.1.refs_1_), channel_id=1, source_target_pairs={{0,16},{16,0},{1,17},{17,1},{2,18},{18,2},{3,19},{19,3},{4,20},{20... | collective-permute-start | bytes 313352 | tf_op jit(solution)/shard_map/ppermute | solution.py:658

commit v10 on v9

--- a/solution.py
+++ b/solution.py
@@ -14,6 +14,7 @@
 COUNT_ROW = 6
 SPARE_ROWS = (6, 7, 14)
 SMALL = 1 << 18
+SHARED_ROWS = 4
 
 
 def local(count):
@@ -159,7 +160,8 @@
 
 def sum_ties(peers, *refs):
     (fields, fit_disp, fit_dir, node_ref, owner_ref, slot_ref) = refs[:6]
-    (ties, col_out, hot_col_out, hot_slot_out, hot_row_out, pay) = refs[6:]
+    (ties, col_out, hot_col_out, hot_slot_out, hot_row_out, pay) = refs[10:16]
+    build_weights(*refs[6:10], *refs[16:])
     row_total = fields.shape[0] // COMPS
     cols = fields.shape[1]
     slots = fit_disp.shape[1]
@@ -224,7 +226,7 @@
     return jnp.where(upper, first, last), jnp.where(upper, last, first)
 
 
-def fill_blocks(axes, row_total, sums, columns, mate, w_in, b_in, b_mid, w_out, out, w_first, w_last, b_cols, pay, done):
+def fill_blocks(axes, row_total, sums, columns, mate, pay):
     tx_count, ty_count = axes
     along, across = lax.axis_index("tx"), lax.axis_index("ty")
     near, far = mate_rows(mate)
@@ -249,11 +251,6 @@
             pay[at, 2 * COMPS : 3 * COMPS, :] = near
             for line, row in zip(packed, SPARE_ROWS):
                 pay[at, row : row + 1, :] = line
-
-    copy = pltpu.make_async_copy(pay, out, done)
-    copy.start()
-    build_weights(w_in, b_in, b_mid, w_out, w_first, w_last, b_cols)
-    copy.wait()
 
 
 def pack_column(column, width):
@@ -325,32 +322,14 @@
     w_last[...] = dot(hit.astype(F32).astype(BF16), w_out[...]).astype(BF16)
 
 
-def interior(pick, fields, mate, w_first, w_mid, b_cols, w_last, sent, forces):
-    row_total, cols = fields.shape[0] // COMPS, fields.shape[1]
-    half = row_total // 2
-    held = half + 1
-    group = lax.axis_index("groups") if pick is None else pick
-    core = lax.axis_index("pb")
-    first = group * half - core
-    near, _ = mate_rows(mate)
-    lines = []
-    for at in range(half + 1):
-        row = first + at
-        if at == 0:
-            row = jnp.maximum(row, 0)
-        if at == half:
-            row = jnp.minimum(row, row_total - 1)
-        base = fields[pl.ds(pl.multiple_of(row * COMPS, COMPS), COMPS), :]
-        if at == 0:
-            base = jnp.where((core == 1) & (group == 0), near, base)
-        if at == half:
-            base = jnp.where((core == 0) & (group == 1), near, base)
-        lines.append((base, pltpu.roll(base, cols - 1, 1)))
+def row_forces(fields, lines, first, weights, forces):
+    cols = fields.shape[1]
+    lines = [(line, pltpu.roll(line, cols - 1, 1)) for line in lines]
     tiles = [
-        strain_tile(lines[at][0], lines[at + 1][0], lines[at][1], lines[at + 1][1]) for at in range(half)
+        strain_tile(one[0], two[0], one[1], two[1]) for one, two in zip(lines[:-1], lines[1:])
     ]
-    tiles = [jnp.concatenate(tiles[at : at + 2], axis=1) for at in range(0, half, 2)]
-    sums = stress_sums(tiles, w_first, w_mid, b_cols, w_last)
+    tiles = [jnp.concatenate(tiles[at : at + 2], axis=1) for at in range(0, len(tiles), 2)]
+    sums = stress_sums(tiles, *weights)
     keep = lanes_of((COMPS, cols)) < cols - 1
     forces[...] = jnp.zeros(forces.shape, F32)
     for tile, (primal, tangent) in enumerate(sums):
@@ -361,10 +340,40 @@
             at = (2 * tile + side + 1) * COMPS
             forces[at : at + COMPS, :] += base + pltpu.roll(upper, 1, 1)
             forces[at + COMPS : at + 2 * COMPS, :] += right + pltpu.roll(corner, 1, 1)
-    start = 1 + group * (row_total - held) - first
+
+
+def component_rows(forces, start, sent):
+    held = sent.shape[0] // 12
     for comp in range(12):
         rows = pl.ds(start * COMPS + comp % 6 + comp // 6 * 8, held, stride=COMPS)
         sent[comp * held : (comp + 1) * held, :] = forces[rows, :]
+
+
+def node_row(fields, row):
+    return fields[pl.ds(pl.multiple_of(row * COMPS, COMPS), COMPS), :]
+
+
+def interior(pick, count, fields, mate, w_first, w_mid, b_cols, w_last, sent, forces):
+    row_total = fields.shape[0] // COMPS
+    group = lax.axis_index("groups") if pick is None else pick
+    core = lax.axis_index("pb")
+    first = group * (row_total - count) - core
+    near, _ = mate_rows(mate)
+    lines = [jnp.where((core == 1) & (group == 0), near, node_row(fields, jnp.maximum(first, 0)))]
+    lines += [node_row(fields, first + at) for at in range(1, count)]
+    last = node_row(fields, jnp.minimum(first + count, row_total - 1))
+    lines.append(jnp.where((core == 0) & (group == 1), near, last))
+    row_forces(fields, lines, first, (w_first, w_mid, b_cols, w_last), forces)
+    component_rows(forces, 1 + group * (row_total - count - 1) - first, sent)
+
+
+def middle(count, fields, w_first, w_mid, b_cols, w_last, kept, forces):
+    row_total = fields.shape[0] // COMPS
+    core = lax.axis_index("pb")
+    first = count - core
+    lines = [node_row(fields, first + at) for at in range(row_total - 2 * count + 1)]
+    row_forces(fields, lines, first, (w_first, w_mid, b_cols, w_last), forces)
+    component_rows(forces, core, kept)
 
 
 def edges(names, axes, *refs):
@@ -531,7 +540,7 @@
         partial[rows, :] = value - ref["load"][rows, :] if comp < 6 else value
 
 
-def combine(swapped, partial, own, other, fit_one, fit_two, res, tan, fit_res, fit_tan):
+def combine(swapped, partial, own, other, between, fit_one, fit_two, res, tan, fit_res, fit_tan):
     fit_res[...] = fit_one[...]
     fit_tan[...] = fit_two[...]
     row_total = partial.shape[0] // 12
@@ -548,6 +557,9 @@
         target[start : start + row_total, :] = partial[comp * row_total : (comp + 1) * row_total, :]
         target[start : start + held, :] += first
         target[start + skip : start + row_total, :] += second
+        count = between.shape[0] // 12
+        low = start + held - 2
+        target[low : low + count, :] += between[comp * count : (comp + 1) * count, :]
 
 
 def per_device(
@@ -608,9 +620,10 @@
     fields, rows, fit_disp, fit_dir, node, owner, slot, b_first, b_second, w_first_in, w_final = outs
     mate = lax.ppermute(rows, "pb", [(0, 1), (1, 0)])
 
-    inputs = tuple(on_chip(value) for value in (fields, fit_disp, fit_dir, node, owner, slot))
+    inputs = (fields, fit_disp, fit_dir, node, owner, slot, w_first_in, b_first, b_second, w_final)
+    inputs = tuple(on_chip(value) for value in inputs)
     small = peers * 2 * COMPS * slots <= SMALL
-    ties, cols_out, hot_col, hot_slot, hot_row, sums = pl.pallas_call(
+    ties, cols_out, hot_col, hot_slot, hot_row, sums, w_first, w_last, b_cols = pl.pallas_call(
         lambda *refs: sum_ties(peers, *refs),
         out_shape=[
             pltpu.VMEM((COMPS, tie_total), F32),
@@ -619,43 +632,50 @@
             pltpu.VMEM((slots, tie_total), BF16),
             pltpu.VMEM((row_total, tie_total), BF16),
             (pltpu.VMEM if small else jax.ShapeDtypeStruct)((peers, 2 * COMPS, slots), F32),
-        ],
-        in_specs=local(len(inputs)),
-        out_specs=local(6),
-        name="sum_ties",
-    )(*inputs)
-    inputs = (sums, cols_out, mate, w_first_in, b_first, b_second, w_final)
-    inputs = [on_chip(value) if value.size <= SMALL else value for value in inputs]
-    pay, w_first, w_last, b_cols = pl.pallas_call(
-        lambda *refs: fill_blocks((tx_count, ty_count), row_total, *refs),
-        out_shape=[
-            shape(peers, 3 * COMPS, slots),
             pltpu.VMEM((8 * hid, 4 * COMPS), BF16),
             pltpu.VMEM((128, hid), BF16),
             pltpu.VMEM((hid, 128), F32),
         ],
         in_specs=local(len(inputs)),
-        out_specs=[pl.BlockSpec(memory_space=pl.ANY)] + local(3),
-        scratch_shapes=[pltpu.VMEM((peers, 3 * COMPS, slots), F32), pltpu.SemaphoreType.DMA(())],
+        out_specs=local(9),
+        name="sum_ties",
+    )(*inputs)
+    inputs = [on_chip(value) if value.size <= SMALL else value for value in (sums, cols_out, mate)]
+    pay = pl.pallas_call(
+        lambda *refs: fill_blocks((tx_count, ty_count), row_total, *refs),
+        out_shape=shape(peers, 3 * COMPS, slots),
+        in_specs=local(len(inputs)),
+        out_specs=local(1)[0],
         name="fill_blocks",
     )(*inputs)
     got = lax.all_to_all(pay, ("tx", "ty"), split_axis=0, concat_axis=0, tiled=True)
 
     inputs = tuple(on_chip(value) for value in (fields, mate, w_first, w_mid, b_cols, w_last))
     groups = lax.axis_size("groups")
+    count = (row_total - SHARED_ROWS) // 2
     halves = []
     for pick in (None,) if groups == 2 else (0, 1):
         half = pl.pallas_call(
-            lambda *refs: interior(pick, *refs),
-            out_shape=pltpu.VMEM(((row_total // 2 + 1) * 12, cols), F32),
+            lambda *refs: interior(pick, count, *refs),
+            out_shape=pltpu.VMEM(((count + 1) * 12, cols), F32),
             in_specs=local(len(inputs)),
             out_specs=local(1)[0],
-            scratch_shapes=[pltpu.VMEM(((row_total // 2 + 3) * COMPS, cols), F32)],
+            scratch_shapes=[pltpu.VMEM(((count + 3) * COMPS, cols), F32)],
             name="interior",
         )(*inputs)
         halves.append(half)
     if groups == 2:
         halves.append(lax.ppermute(halves[0], "groups", [(0, 1), (1, 0)]))
+    fields_late, _ = lax.optimization_barrier((fields, halves[0]))
+    inputs = tuple(on_chip(value) for value in (fields_late, w_first, w_mid, b_cols, w_last))
+    between = pl.pallas_call(
+        lambda *refs: middle(count, *refs),
+        out_shape=pltpu.VMEM(((SHARED_ROWS + 2) * 12, cols), F32),
+        in_specs=local(len(inputs)),
+        out_specs=local(1)[0],
+        scratch_shapes=[pltpu.VMEM(((SHARED_ROWS + 3) * COMPS, cols), F32)],
+        name="middle",
+    )(*inputs)
 
     named = dict(
         got=got,
@@ -685,7 +705,7 @@
         name="edges",
     )(*named.values())
 
-    inputs = tuple(on_chip(value) for value in (partial, halves[0], halves[1], fit_one, fit_two))
+    inputs = tuple(on_chip(value) for value in (partial, halves[0], halves[1], between, fit_one, fit_two))
     res, tan, fit_res, fit_tan = pl.pallas_call(
         lambda *refs: combine(groups == 2, *refs),
         out_shape=[shape(*flat), shape(*flat), shape(6, slots), shape(6, slots)],

time: 22.9 us -> 22.8 us (level)
  Pallas kernels: 11.1 us -> 12.6 us
  waiting for transfers between devices: 1.43 us -> 0.03 us
  starting transfers between devices: 9.41 us -> 9.16 us
    pallas_call x1 -> x2, Pallas kernels: 5.71 us -> 6.89 us  [the longest x1 5.08 us: per_device(): pl.pallas_call(lambda *refs: interior(pick, count, *refs), out_shape=pltp...]
    all_to_all x1, waiting for transfers between devices: 0.98 us -> 0.03 us  [per_device(): lax.all_to_all(pay, ('tx', 'ty'), split_axis=0, concat_axis=0, tiled=True)]
    pallas_call x1, Pallas kernels: 0.69 us -> 1.05 us  [per_device(): pl.pallas_call(lambda *refs: sum_ties(peers, *refs), out_shape=[pltpu.VME...]
    ppermute x1, waiting for transfers between devices: 0.31 us -> 0.01 us  [per_device(): halves.append(lax.ppermute(halves[0], 'groups', [(0, 1), (1, 0)]))]
    all_to_all x1, starting transfers between devices: 7.28 us -> 7.03 us  [per_device(): lax.all_to_all(pay, ('tx', 'ty'), split_axis=0, concat_axis=0, tiled=True)]
  transfers between devices with their start and end apart: 3 -> 3, of which waited for: 3 -> 0; matrix products, arithmetic and copies ran while one was open for 0% -> 0% of each run, Pallas kernels for 37% -> 44%
where the time goes in v10:
time: 22.8 us; the launch traced here: 22.5 us
  Pallas kernels  12.6 us (55%)
  starting transfers between devices  9.16 us (40%)
  between operations  0.69 us (3%)
    all_to_all x1, starting transfers between devices, per_device(): lax.all_to_all(pay, ('tx', 'ty'), split_axis=0, concat_axis=0, tiled=True)  7.03 us
    pallas_call x1, Pallas kernels, per_device(): pl.pallas_call(lambda *refs: interior(pick, count, *refs), out_shape=pltp...  5.08 us
    pallas_call x1, Pallas kernels, per_device(): pl.pallas_call(lambda *refs: edges(names + ['partial', 'fit_res', 'fit_ta...  1.96 us
    pallas_call x1, Pallas kernels, per_device(): pl.pallas_call(lambda *refs: middle(count, *refs), out_shape=pltpu.VMEM((...  1.81 us
    ppermute x1, starting transfers between devices, per_device(): halves.append(lax.ppermute(halves[0], 'groups', [(0, 1), (1, 0)]))  1.57 us
    pallas_call x1, Pallas kernels, per_device(): pl.pallas_call(lambda *refs: gather_nodes(len(smalls), *refs), out_shape=...  1.13 us
    pallas_call x1, Pallas kernels, per_device(): pl.pallas_call(lambda *refs: sum_ties(peers, *refs), out_shape=[pltpu.VME...  1.05 us
    pallas_call x1, Pallas kernels, per_device(): pl.pallas_call(lambda *refs: fill_blocks((tx_count, ty_count), row_total,...  0.87 us
  transfers between devices with their start and end apart: 3, of which 0 were waited for; matrix products, arithmetic and copies ran while one was open for 0% of the time, Pallas kernels for 44%

profile of v10, /device:TPU:0, one launch (start us, length us, event | category | flops | bytes accessed | tf_op | source)
XLA Modules:
  0.0 22.5 jit_solution(13390792682074831236)
XLA Ops:
  0.6 1.1 %gather_nodes.1 = (f32[512,128]{1,0:T(8,128)S(1)}, f32[32,128]{1,0:T(8,128)S(1)}, f32[6,128]{1,0:T(8,128)S(1)}, f32[6,128]{1,0:T(8,128)S(1)}, s32[6,128]{1,0:T(8...) custom-call(f32[192,128]{1,0:T(8,128)} %bitcast.12, ...), custom_call_target="tpu_custom_call" | custom-call | tf_op jit(solution)/shard_map/gather_nodes/pallas_call | solution.py:612
  1.8 0.6 %collective-permute-start = (f32[32,128]{1,0:T(8,128)S(1)}, f32[32,128]{1,0:T(8,128)S(1)}, u32[]{:S(2)}, u32[]{:S(2)}) collective-permute-start(f32[32,128]{1,0:T(8,128)S(1)} %get-tuple-element.44), channel_id=1, source_target_pairs={{0,1},{1,0},{2,3},{3,2},{4,5},{5,4},{6,7},{7,6},{8,9},{9,8},{10,11... | collective-permute-start | bytes 49160 | tf_op jit(solution)/shard_map/ppermute | solution.py:621
  2.3 1.1 %sum_ties.1 = (f32[16,768]{1,0:T(8,128)S(1)}, f32[32,128]{1,0:T(8,128)S(1)}, bf16[128,768]{1,0:T(8,128)(2,1)S(1)}, bf16[128,768]{1,0:T(8,128)(2,1)S(1)}, bf16[32...) custom-call(f32[512,128]{1,0:T(8,128)S(1)} %get-tuple-element.53.ref, ...), custom_call_target="tpu_custom_call" | custom-call | tf_op jit(solution)/shard_map/sum_ties/pallas_call | solution.py:626
  3.4 0.0 collective-permute-done.refs_2_.refs_1_
  3.4 0.9 %fill_blocks.1 = f32[8,48,128]{2,1,0:T(8,128)} custom-call(f32[8,32,128]{2,1,0:T(8,128)S(1)} %get-tuple-element.42.refs_0_, f32[32,128]{1,0:T(8,128)S(1)} %get-tuple-element.43.refs_1_.refs_4_, f32[32,128]{1,0:T(8,128)S(1)} %collective-permute-done.refs_2_.refs_1_), custom_call_target="tpu_custom_call" | custom-call | tf_op jit(solution)/shard_map/fill_blocks/pallas_call | solution.py:644
  4.3 0.0 copy-start
  4.3 7.0 %all-to-all-start = ((f32[8,48,128]{2,1,0:T(8,128)}), f32[8,48,128]{2,1,0:T(8,128)S(1)}, u32[]{:S(2)}, u32[]{:S(2)}) async-start(f32[8,48,128]{2,1,0:T(8,128)} %fill_blocks.1), calls=%async_computation | async-start | bytes 393216 | tf_op jit(solution)/shard_map/all_to_all | solution.py:651
  11.3 0.0 copy-done
  11.3 5.1 %interior.1.refs_1_ = f32[180,128]{1,0:T(8,128)S(1)} custom-call(f32[512,128]{1,0:T(8,128)S(1)} %get-tuple-element.53.refs_0_.refs_2_, f32[32,128]{1,0:T(8,128)S(1)} %collective-permute-done.refs_2_.refs_1_, bf16[2048,64]{1,0:T(8,128)(2,1)S(1)} %get-tuple-element.46.refs_5_.refs_2_.refs_1_, bf16[256,256]{1,0:T(8,128)(2,1)S(1)} %copy-done, ...), custom_call_target="tpu_custom_call" | custom-call | tf_op jit(solution)/shard_map/interior/pallas_call | solution.py:658
  16.4 0.0 copy-start.1
  16.4 1.6 %collective-permute-start.1 = (f32[180,128]{1,0:T(8,128)S(1)}, f32[180,128]{1,0:T(8,128)S(1)}, u32[]{:S(2)}, u32[]{:S(2)}) collective-permute-start(f32[180,128]{1,0:T(8,128)S(1)} %interior.1.refs_1_), channel_id=1, source_target_pairs={{0,16},{16,0},{1,17},{17,1},{2,18},{18,2},{3,19},{19,3},{4,20},{20... | collective-permute-start | bytes 276488 | tf_op jit(solution)/shard_map/ppermute | solution.py:668
  18.0 1.8 %middle.1.refs_3_ = f32[72,128]{1,0:T(8,128)S(1)} custom-call(f32[512,128]{1,0:T(8,128)S(1)} %get-tuple-element.53.refs_0_.refs_2_, bf16[2048,64]{1,0:T(8,128)(2,1)S(1)} %get-tuple-element.46.refs_5_.refs_2_.refs_1_, bf16[256,256]{1,0:T(8,128)(2,1)S(1)} %copy-done, f32[256,128]{1,0:T(8,128)S(1)} %get-tuple-element.47.refs_7_.refs_4_.refs_3_, ...), custom_call_target="tpu_custom_call" | custom-call | tf_op jit(solution)/shard_map/middle/pallas_call | solution.py:671
  19.8 0.0 all-to-all-done.refs_0_
  19.8 0.0 copy-done.1
  19.8 2.0 %edges.1 = (f32[384,128]{1,0:T(8,128)S(1)}, f32[6,128]{1,0:T(8,128)S(1)}, f32[6,128]{1,0:T(8,128)S(1)}) custom-call(f32[8,48,128]{2,1,0:T(8,128)S(1)} %all-to-all-done.refs_0_, f32[32,128]{1,0:T(8,128)S(1)} %collective-permute-done.refs_2_.refs_1_, f32[512,128]{1,0:T(8,128)S(1)} %get-tuple-element.53.refs_0_.refs_2_, ...), custom_call_target="tpu_custom_call" | custom-call | tf_op jit(solution)/shard_map/edges/pallas_call | solution.py:700
  21.8 0.0 collective-permute-done.1.refs_2_
  21.8 0.7 %combine.1 = (f32[192,128]{1,0:T(8,128)}, f32[192,128]{1,0:T(8,128)}, f32[6,128]{1,0:T(8,128)}, f32[6,128]{1,0:T(8,128)}) custom-call(f32[384,128]{1,0:T(8,128)S(1)} %get-tuple-element.52.refs_0_, f32[180,128]{1,0:T(8,128)S(1)} %interior.1.refs_1_, f32[180,128]{1,0:T(8,128)S(1)} %collective-permute-done.1.refs_2_, f32[72,128]{1,0:T(8,128)S(1)} %middle.1.refs_3_, ...), custom_call_target="tpu_custom_call" | custom-call | tf_op jit(solution)/shard_map/combine/pallas_call | solution.py:709
Async XLA Ops:
  1.8 1.6 %collective-permute-start = (f32[32,128]{1,0:T(8,128)S(1)}, f32[32,128]{1,0:T(8,128)S(1)}, u32[]{:S(2)}, u32[]{:S(2)}) collective-permute-start(f32[32,128]{1,0:T(8,128)S(1)} %get-tuple-element.44), channel_id=1, source_target_pairs={{0,1},{1,0},{2,3},{3,2},{4,5},{5,4},{6,7},{7,6},{8,9},{9,8},{10,11... | collective-permute-start | bytes 49160 | tf_op jit(solution)/shard_map/ppermute | solution.py:621
  4.3 7.0 %copy-start = (bf16[256,256]{1,0:T(8,128)(2,1)S(1)}, bf16[256,256]{1,0:T(8,128)(2,1)}, u32[]{:S(2)}) copy-start(bf16[256,256]{1,0:T(8,128)(2,1)} %refs_2_.3) | copy-start | bytes 393220
  4.3 15.5 %all-to-all-start = ((f32[8,48,128]{2,1,0:T(8,128)}), f32[8,48,128]{2,1,0:T(8,128)S(1)}, u32[]{:S(2)}, u32[]{:S(2)}) async-start(f32[8,48,128]{2,1,0:T(8,128)} %fill_blocks.1), calls=%async_computation | async-start | bytes 393216 | tf_op jit(solution)/shard_map/all_to_all | solution.py:651
  16.4 3.4 %copy-start.1 = (f32[6,32,128]{2,1,0:T(8,128)S(1)}, f32[6,32,128]{2,1,0:T(8,128)}, u32[]{:S(2)}) copy-start(f32[6,32,128]{2,1,0:T(8,128)} %param.15) | copy-start | bytes 294916
  16.4 5.4 %collective-permute-start.1 = (f32[180,128]{1,0:T(8,128)S(1)}, f32[180,128]{1,0:T(8,128)S(1)}, u32[]{:S(2)}, u32[]{:S(2)}) collective-permute-start(f32[180,128]{1,0:T(8,128)S(1)} %interior.1.refs_1_), channel_id=1, source_target_pairs={{0,16},{16,0},{1,17},{17,1},{2,18},{18,2},{3,19},{19,3},{4,20},{20... | collective-permute-start | bytes 276488 | tf_op jit(solution)/shard_map/ppermute | solution.py:668

commit v11 on v10

--- a/solution.py
+++ b/solution.py
@@ -389,6 +389,44 @@
     along = lax.axis_index("tx")
     place = along * pb_count + core
 
+    owner = ref["owner"][...]
+    hot_slot = ref["hot_slot"][...]
+    hot_two = jnp.concatenate([hot_slot] * 2, axis=0)
+    fit_value = jnp.zeros((COMPS, tie_total), F32)
+    bins = jnp.zeros((COMPS, slots), F32)
+    peers = tx_count * ty_count
+    block = math.gcd(peers, 8)
+
+    def collect(first, carry):
+        fit_value, bins = carry
+        parts = [got[first + peer] for peer in range(block)]
+        fit_all = jnp.concatenate([part[0:COMPS] for part in parts], axis=0)
+        wide = dot(jnp.concatenate(split(fit_all, 2), axis=1), hot_two)
+        for peer, part in enumerate(parts):
+            fit_value = jnp.where(owner == first + peer, wide[peer * COMPS : (peer + 1) * COMPS], fit_value)
+            bins = bins + part[COMPS : 2 * COMPS]
+        return fit_value, bins
+
+    if block == peers:
+        fit_value, bins = collect(0, (fit_value, bins))
+    else:
+        fit_value, bins = lax.fori_loop(
+            0, peers // block, lambda at, carry: collect(at * block, carry), (fit_value, bins)
+        )
+    count = bins[COUNT_ROW : COUNT_ROW + 1]
+    for out, fit, base in (("fit_res", "fit_disp", 0), ("fit_tan", "fit_dir", 8)):
+        ref[out][...] = 2.0 * (count * ref[fit][...] - bins[base : base + 6])
+
+    pulled = split(2.0 * (ties[...] - fit_value), 2)
+    hot_row = ref["hot_row"][...]
+    places = [comp % 6 + comp // 6 * 8 for comp in range(12)]
+    lhs = [
+        jnp.concatenate([hot_row * part[place_of : place_of + 1] for part in pulled], axis=1)
+        for place_of in places
+    ]
+    hot_col = ref["hot_col"][...]
+    tie_forces = dot(jnp.concatenate(lhs, axis=0), jnp.concatenate([hot_col] * 2, axis=1), ((1,), (1,)))
+
     def around(step, side, packed=False):
         there, over = along + step, across + side
         valid = (there >= 0) & (there < tx_count) & (over >= 0) & (over < ty_count)
@@ -477,44 +515,6 @@
     s_base = mask(s_base, valid)
     s_right = mask(s_right, valid)
     col_last = pltpu.roll(pltpu.roll(s_base, back, 1) + s_right, cols - half, 1)
-
-    owner = ref["owner"][...]
-    hot_slot = ref["hot_slot"][...]
-    hot_two = jnp.concatenate([hot_slot] * 2, axis=0)
-    fit_value = jnp.zeros((COMPS, tie_total), F32)
-    bins = jnp.zeros((COMPS, slots), F32)
-    peers = tx_count * ty_count
-    block = math.gcd(peers, 8)
-
-    def collect(first, carry):
-        fit_value, bins = carry
-        parts = [got[first + peer] for peer in range(block)]
-        fit_all = jnp.concatenate([part[0:COMPS] for part in parts], axis=0)
-        wide = dot(jnp.concatenate(split(fit_all, 2), axis=1), hot_two)
-        for peer, part in enumerate(parts):
-            fit_value = jnp.where(owner == first + peer, wide[peer * COMPS : (peer + 1) * COMPS], fit_value)
-            bins = bins + part[COMPS : 2 * COMPS]
-        return fit_value, bins
-
-    if block == peers:
-        fit_value, bins = collect(0, (fit_value, bins))
-    else:
-        fit_value, bins = lax.fori_loop(
-            0, peers // block, lambda at, carry: collect(at * block, carry), (fit_value, bins)
-        )
-    count = bins[COUNT_ROW : COUNT_ROW + 1]
-    for out, fit, base in (("fit_res", "fit_disp", 0), ("fit_tan", "fit_dir", 8)):
-        ref[out][...] = 2.0 * (count * ref[fit][...] - bins[base : base + 6])
-
-    pulled = split(2.0 * (ties[...] - fit_value), 2)
-    hot_row = ref["hot_row"][...]
-    places = [comp % 6 + comp // 6 * 8 for comp in range(12)]
-    lhs = [
-        jnp.concatenate([hot_row * part[place_of : place_of + 1] for part in pulled], axis=1)
-        for place_of in places
-    ]
-    hot_col = ref["hot_col"][...]
-    tie_forces = dot(jnp.concatenate(lhs, axis=0), jnp.concatenate([hot_col] * 2, axis=1), ((1,), (1,)))
 
     assert 4 * row_total <= cols
     line = jnp.zeros((COMPS, cols), F32)

time: 22.8 us -> 22.7 us (level)
  no operation moved by 1% of the time
where the time goes in v11:
time: 22.7 us; the launch traced here: 22.5 us
  Pallas kernels  12.6 us (56%)
  starting transfers between devices  9.16 us (40%)
  between operations  0.69 us (3%)
    all_to_all x1, starting transfers between devices, per_device(): lax.all_to_all(pay, ('tx', 'ty'), split_axis=0, concat_axis=0, tiled=True)  7.03 us
    pallas_call x1, Pallas kernels, per_device(): pl.pallas_call(lambda *refs: interior(pick, count, *refs), out_shape=pltp...  5.08 us
    pallas_call x1, Pallas kernels, per_device(): pl.pallas_call(lambda *refs: edges(names + ['partial', 'fit_res', 'fit_ta...  1.9 us
    pallas_call x1, Pallas kernels, per_device(): pl.pallas_call(lambda *refs: middle(count, *refs), out_shape=pltpu.VMEM((...  1.81 us
    ppermute x1, starting transfers between devices, per_device(): halves.append(lax.ppermute(halves[0], 'groups', [(0, 1), (1, 0)]))  1.57 us
    pallas_call x1, Pallas kernels, per_device(): pl.pallas_call(lambda *refs: gather_nodes(len(smalls), *refs), out_shape=...  1.13 us
    pallas_call x1, Pallas kernels, per_device(): pl.pallas_call(lambda *refs: sum_ties(peers, *refs), out_shape=[pltpu.VME...  1.05 us
    pallas_call x1, Pallas kernels, per_device(): pl.pallas_call(lambda *refs: fill_blocks((tx_count, ty_count), row_total,...  0.87 us
  transfers between devices with their start and end apart: 3, of which 0 were waited for; matrix products, arithmetic and copies ran while one was open for 0% of the time, Pallas kernels for 44%

profile of v11, /device:TPU:0, one launch (start us, length us, event | category | flops | bytes accessed | tf_op | source)
XLA Modules:
  0.0 22.5 jit_solution(9509008523315897711)
XLA Ops:
  0.6 1.1 %gather_nodes.1 = (f32[512,128]{1,0:T(8,128)S(1)}, f32[32,128]{1,0:T(8,128)S(1)}, f32[6,128]{1,0:T(8,128)S(1)}, f32[6,128]{1,0:T(8,128)S(1)}, s32[6,128]{1,0:T(8...) custom-call(f32[192,128]{1,0:T(8,128)} %bitcast.12, ...), custom_call_target="tpu_custom_call" | custom-call | tf_op jit(solution)/shard_map/gather_nodes/pallas_call | solution.py:612
  1.8 0.6 %collective-permute-start = (f32[32,128]{1,0:T(8,128)S(1)}, f32[32,128]{1,0:T(8,128)S(1)}, u32[]{:S(2)}, u32[]{:S(2)}) collective-permute-start(f32[32,128]{1,0:T(8,128)S(1)} %get-tuple-element.44), channel_id=1, source_target_pairs={{0,1},{1,0},{2,3},{3,2},{4,5},{5,4},{6,7},{7,6},{8,9},{9,8},{10,11... | collective-permute-start | bytes 49160 | tf_op jit(solution)/shard_map/ppermute | solution.py:621
  2.3 1.1 %sum_ties.1 = (f32[16,768]{1,0:T(8,128)S(1)}, f32[32,128]{1,0:T(8,128)S(1)}, bf16[128,768]{1,0:T(8,128)(2,1)S(1)}, bf16[128,768]{1,0:T(8,128)(2,1)S(1)}, bf16[32...) custom-call(f32[512,128]{1,0:T(8,128)S(1)} %get-tuple-element.53.ref, ...), custom_call_target="tpu_custom_call" | custom-call | tf_op jit(solution)/shard_map/sum_ties/pallas_call | solution.py:626
  3.4 0.0 collective-permute-done.refs_2_.refs_1_
  3.4 0.9 %fill_blocks.1 = f32[8,48,128]{2,1,0:T(8,128)} custom-call(f32[8,32,128]{2,1,0:T(8,128)S(1)} %get-tuple-element.42.refs_0_, f32[32,128]{1,0:T(8,128)S(1)} %get-tuple-element.43.refs_1_.refs_4_, f32[32,128]{1,0:T(8,128)S(1)} %collective-permute-done.refs_2_.refs_1_), custom_call_target="tpu_custom_call" | custom-call | tf_op jit(solution)/shard_map/fill_blocks/pallas_call | solution.py:644
  4.3 0.0 copy-start
  4.3 7.0 %all-to-all-start = ((f32[8,48,128]{2,1,0:T(8,128)}), f32[8,48,128]{2,1,0:T(8,128)S(1)}, u32[]{:S(2)}, u32[]{:S(2)}) async-start(f32[8,48,128]{2,1,0:T(8,128)} %fill_blocks.1), calls=%async_computation | async-start | bytes 393216 | tf_op jit(solution)/shard_map/all_to_all | solution.py:651
  11.3 0.0 copy-done
  11.3 5.1 %interior.1.refs_1_ = f32[180,128]{1,0:T(8,128)S(1)} custom-call(f32[512,128]{1,0:T(8,128)S(1)} %get-tuple-element.53.refs_0_.refs_2_, f32[32,128]{1,0:T(8,128)S(1)} %collective-permute-done.refs_2_.refs_1_, bf16[2048,64]{1,0:T(8,128)(2,1)S(1)} %get-tuple-element.46.refs_5_.refs_2_.refs_1_, bf16[256,256]{1,0:T(8,128)(2,1)S(1)} %copy-done, ...), custom_call_target="tpu_custom_call" | custom-call | tf_op jit(solution)/shard_map/interior/pallas_call | solution.py:658
  16.4 0.0 copy-start.1
  16.4 1.6 %collective-permute-start.1 = (f32[180,128]{1,0:T(8,128)S(1)}, f32[180,128]{1,0:T(8,128)S(1)}, u32[]{:S(2)}, u32[]{:S(2)}) collective-permute-start(f32[180,128]{1,0:T(8,128)S(1)} %interior.1.refs_1_), channel_id=1, source_target_pairs={{0,16},{16,0},{1,17},{17,1},{2,18},{18,2},{3,19},{19,3},{4,20},{20... | collective-permute-start | bytes 276488 | tf_op jit(solution)/shard_map/ppermute | solution.py:668
  18.0 1.8 %middle.1.refs_3_ = f32[72,128]{1,0:T(8,128)S(1)} custom-call(f32[512,128]{1,0:T(8,128)S(1)} %get-tuple-element.53.refs_0_.refs_2_, bf16[2048,64]{1,0:T(8,128)(2,1)S(1)} %get-tuple-element.46.refs_5_.refs_2_.refs_1_, bf16[256,256]{1,0:T(8,128)(2,1)S(1)} %copy-done, f32[256,128]{1,0:T(8,128)S(1)} %get-tuple-element.47.refs_7_.refs_4_.refs_3_, ...), custom_call_target="tpu_custom_call" | custom-call | tf_op jit(solution)/shard_map/middle/pallas_call | solution.py:671
  19.8 0.0 all-to-all-done.refs_0_
  19.8 0.0 copy-done.1
  19.8 1.9 %edges.1 = (f32[384,128]{1,0:T(8,128)S(1)}, f32[6,128]{1,0:T(8,128)S(1)}, f32[6,128]{1,0:T(8,128)S(1)}) custom-call(f32[8,48,128]{2,1,0:T(8,128)S(1)} %all-to-all-done.refs_0_, f32[32,128]{1,0:T(8,128)S(1)} %collective-permute-done.refs_2_.refs_1_, f32[512,128]{1,0:T(8,128)S(1)} %get-tuple-element.53.refs_0_.refs_2_, ...), custom_call_target="tpu_custom_call" | custom-call | tf_op jit(solution)/shard_map/edges/pallas_call | solution.py:700
  21.7 0.0 collective-permute-done.1.refs_2_
  21.7 0.7 %combine.1 = (f32[192,128]{1,0:T(8,128)}, f32[192,128]{1,0:T(8,128)}, f32[6,128]{1,0:T(8,128)}, f32[6,128]{1,0:T(8,128)}) custom-call(f32[384,128]{1,0:T(8,128)S(1)} %get-tuple-element.52.refs_0_, f32[180,128]{1,0:T(8,128)S(1)} %interior.1.refs_1_, f32[180,128]{1,0:T(8,128)S(1)} %collective-permute-done.1.refs_2_, f32[72,128]{1,0:T(8,128)S(1)} %middle.1.refs_3_, ...), custom_call_target="tpu_custom_call" | custom-call | tf_op jit(solution)/shard_map/combine/pallas_call | solution.py:709
Async XLA Ops:
  1.8 1.6 %collective-permute-start = (f32[32,128]{1,0:T(8,128)S(1)}, f32[32,128]{1,0:T(8,128)S(1)}, u32[]{:S(2)}, u32[]{:S(2)}) collective-permute-start(f32[32,128]{1,0:T(8,128)S(1)} %get-tuple-element.44), channel_id=1, source_target_pairs={{0,1},{1,0},{2,3},{3,2},{4,5},{5,4},{6,7},{7,6},{8,9},{9,8},{10,11... | collective-permute-start | bytes 49160 | tf_op jit(solution)/shard_map/ppermute | solution.py:621
  4.3 7.0 %copy-start = (bf16[256,256]{1,0:T(8,128)(2,1)S(1)}, bf16[256,256]{1,0:T(8,128)(2,1)}, u32[]{:S(2)}) copy-start(bf16[256,256]{1,0:T(8,128)(2,1)} %refs_2_.3) | copy-start | bytes 393220
  4.3 15.5 %all-to-all-start = ((f32[8,48,128]{2,1,0:T(8,128)}), f32[8,48,128]{2,1,0:T(8,128)S(1)}, u32[]{:S(2)}, u32[]{:S(2)}) async-start(f32[8,48,128]{2,1,0:T(8,128)} %fill_blocks.1), calls=%async_computation | async-start | bytes 393216 | tf_op jit(solution)/shard_map/all_to_all | solution.py:651
  16.4 3.4 %copy-start.1 = (f32[6,32,128]{2,1,0:T(8,128)S(1)}, f32[6,32,128]{2,1,0:T(8,128)}, u32[]{:S(2)}) copy-start(f32[6,32,128]{2,1,0:T(8,128)} %param.15) | copy-start | bytes 294916
  16.4 5.3 %collective-permute-start.1 = (f32[180,128]{1,0:T(8,128)S(1)}, f32[180,128]{1,0:T(8,128)S(1)}, u32[]{:S(2)}, u32[]{:S(2)}) collective-permute-start(f32[180,128]{1,0:T(8,128)S(1)} %interior.1.refs_1_), channel_id=1, source_target_pairs={{0,16},{16,0},{1,17},{17,1},{2,18},{18,2},{3,19},{19,3},{4,20},{20... | collective-permute-start | bytes 276488 | tf_op jit(solution)/shard_map/ppermute | solution.py:668

commit v12 on v11

--- a/solution.py
+++ b/solution.py
@@ -15,6 +15,7 @@
 SPARE_ROWS = (6, 7, 14)
 SMALL = 1 << 18
 SHARED_ROWS = 4
+PAD = 8
 
 
 def local(count):
@@ -52,7 +53,8 @@
 
 
 def as_line(ref):
-    return jnp.concatenate([ref[row : row + 1, :] for row in range(ref.shape[0])], axis=1)
+    value = ref[...]
+    return jnp.concatenate([value[row : row + 1] for row in range(value.shape[0])], axis=1)
 
 
 def paired(top, bottom):
@@ -343,7 +345,7 @@
 
 
 def component_rows(forces, start, sent):
-    held = sent.shape[0] // 12
+    held = (sent.shape[0] - PAD) // 12
     for comp in range(12):
         rows = pl.ds(start * COMPS + comp % 6 + comp // 6 * 8, held, stride=COMPS)
         sent[comp * held : (comp + 1) * held, :] = forces[rows, :]
@@ -540,26 +542,26 @@
         partial[rows, :] = value - ref["load"][rows, :] if comp < 6 else value
 
 
-def combine(swapped, partial, own, other, between, fit_one, fit_two, res, tan, fit_res, fit_tan):
+def combine(swapped, partial, own, other, between, fit_one, fit_two, res, tan, fit_res, fit_tan, total):
     fit_res[...] = fit_one[...]
     fit_tan[...] = fit_two[...]
     row_total = partial.shape[0] // 12
-    held = own.shape[0] // 12
-    skip = row_total - held
+    held = (own.shape[0] - PAD) // 12
+    count = (between.shape[0] - PAD) // 12
     here = lax.axis_index("groups") == 0
     for comp in range(12):
-        target = res if comp < 6 else tan
-        start = comp % 6 * row_total
+        start = comp * row_total
         rows = slice(comp * held, (comp + 1) * held)
         first, second = own[rows, :], other[rows, :]
         if swapped:
             first, second = jnp.where(here, first, second), jnp.where(here, second, first)
-        target[start : start + row_total, :] = partial[comp * row_total : (comp + 1) * row_total, :]
-        target[start : start + held, :] += first
-        target[start + skip : start + row_total, :] += second
-        count = between.shape[0] // 12
+        total[start : start + row_total, :] = partial[start : start + row_total, :]
+        total[start : start + held, :] += first
+        total[start + row_total - held : start + row_total, :] += second
         low = start + held - 2
-        target[low : low + count, :] += between[comp * count : (comp + 1) * count, :]
+        total[low : low + count, :] += between[comp * count : (comp + 1) * count, :]
+    res[...] = total[0 : 6 * row_total, :]
+    tan[...] = total[6 * row_total : 12 * row_total, :]
 
 
 def per_device(
@@ -657,10 +659,10 @@
     for pick in (None,) if groups == 2 else (0, 1):
         half = pl.pallas_call(
             lambda *refs: interior(pick, count, *refs),
-            out_shape=pltpu.VMEM(((count + 1) * 12, cols), F32),
+            out_shape=pltpu.VMEM(((count + 1) * 12 + PAD, cols), F32),
             in_specs=local(len(inputs)),
             out_specs=local(1)[0],
-            scratch_shapes=[pltpu.VMEM(((count + 3) * COMPS, cols), F32)],
+            scratch_shapes=[pltpu.VMEM(((count + 3 + PAD) * COMPS, cols), F32)],
             name="interior",
         )(*inputs)
         halves.append(half)
@@ -670,10 +672,10 @@
     inputs = tuple(on_chip(value) for value in (fields_late, w_first, w_mid, b_cols, w_last))
     between = pl.pallas_call(
         lambda *refs: middle(count, *refs),
-        out_shape=pltpu.VMEM(((SHARED_ROWS + 2) * 12, cols), F32),
+        out_shape=pltpu.VMEM(((SHARED_ROWS + 2) * 12 + PAD, cols), F32),
         in_specs=local(len(inputs)),
         out_specs=local(1)[0],
-        scratch_shapes=[pltpu.VMEM(((SHARED_ROWS + 3) * COMPS, cols), F32)],
+        scratch_shapes=[pltpu.VMEM(((SHARED_ROWS + 3 + PAD) * COMPS, cols), F32)],
         name="middle",
     )(*inputs)
 
@@ -711,6 +713,7 @@
         out_shape=[shape(*flat), shape(*flat), shape(6, slots), shape(6, slots)],
         in_specs=local(len(inputs)),
         out_specs=local(4),
+        scratch_shapes=[pltpu.VMEM((12 * row_total + PAD, cols), F32)],
         name="combine",
     )(*inputs)
     cube = displacement.shape

time: 22.7 us -> 22.7 us (level)
  no operation moved by 1% of the time
where the time goes in v12:
time: 22.7 us; the launch traced here: 22.5 us
  Pallas kernels  12.6 us (56%)
  starting transfers between devices  9.16 us (40%)
  between operations  0.69 us (3%)
    all_to_all x1, starting transfers between devices, per_device(): lax.all_to_all(pay, ('tx', 'ty'), split_axis=0, concat_axis=0, tiled=True)  7.02 us
    pallas_call x1, Pallas kernels, per_device(): pl.pallas_call(lambda *refs: interior(pick, count, *refs), out_shape=pltp...  5.07 us
    pallas_call x1, Pallas kernels, per_device(): pl.pallas_call(lambda *refs: edges(names + ['partial', 'fit_res', 'fit_ta...  1.9 us
    pallas_call x1, Pallas kernels, per_device(): pl.pallas_call(lambda *refs: middle(count, *refs), out_shape=pltpu.VMEM((...  1.82 us
    ppermute x1, starting transfers between devices, per_device(): halves.append(lax.ppermute(halves[0], 'groups', [(0, 1), (1, 0)]))  1.58 us
    pallas_call x1, Pallas kernels, per_device(): pl.pallas_call(lambda *refs: gather_nodes(len(smalls), *refs), out_shape=...  1.13 us
    pallas_call x1, Pallas kernels, per_device(): pl.pallas_call(lambda *refs: sum_ties(peers, *refs), out_shape=[pltpu.VME...  1.05 us
    pallas_call x1, Pallas kernels, per_device(): pl.pallas_call(lambda *refs: fill_blocks((tx_count, ty_count), row_total,...  0.87 us
  transfers between devices with their start and end apart: 3, of which 0 were waited for; matrix products, arithmetic and copies ran while one was open for 0% of the time, Pallas kernels for 44%

profile of v12, /device:TPU:0, one launch (start us, length us, event | category | flops | bytes accessed | tf_op | source)
XLA Modules:
  0.0 22.5 jit_solution(11939026229152845271)
XLA Ops:
  0.6 1.1 %gather_nodes.1 = (f32[512,128]{1,0:T(8,128)S(1)}, f32[32,128]{1,0:T(8,128)S(1)}, f32[6,128]{1,0:T(8,128)S(1)}, f32[6,128]{1,0:T(8,128)S(1)}, s32[6,128]{1,0:T(8...) custom-call(f32[192,128]{1,0:T(8,128)} %bitcast.12, ...), custom_call_target="tpu_custom_call" | custom-call | tf_op jit(solution)/shard_map/gather_nodes/pallas_call | solution.py:614
  1.8 0.6 %collective-permute-start = (f32[32,128]{1,0:T(8,128)S(1)}, f32[32,128]{1,0:T(8,128)S(1)}, u32[]{:S(2)}, u32[]{:S(2)}) collective-permute-start(f32[32,128]{1,0:T(8,128)S(1)} %get-tuple-element.44), channel_id=1, source_target_pairs={{0,1},{1,0},{2,3},{3,2},{4,5},{5,4},{6,7},{7,6},{8,9},{9,8},{10,11... | collective-permute-start | bytes 49160 | tf_op jit(solution)/shard_map/ppermute | solution.py:623
  2.3 1.1 %sum_ties.1 = (f32[16,768]{1,0:T(8,128)S(1)}, f32[32,128]{1,0:T(8,128)S(1)}, bf16[128,768]{1,0:T(8,128)(2,1)S(1)}, bf16[128,768]{1,0:T(8,128)(2,1)S(1)}, bf16[32...) custom-call(f32[512,128]{1,0:T(8,128)S(1)} %get-tuple-element.53.ref, ...), custom_call_target="tpu_custom_call" | custom-call | tf_op jit(solution)/shard_map/sum_ties/pallas_call | solution.py:628
  3.4 0.0 collective-permute-done.refs_2_.refs_1_
  3.4 0.9 %fill_blocks.1 = f32[8,48,128]{2,1,0:T(8,128)} custom-call(f32[8,32,128]{2,1,0:T(8,128)S(1)} %get-tuple-element.42.refs_0_, f32[32,128]{1,0:T(8,128)S(1)} %get-tuple-element.43.refs_1_.refs_4_, f32[32,128]{1,0:T(8,128)S(1)} %collective-permute-done.refs_2_.refs_1_), custom_call_target="tpu_custom_call" | custom-call | tf_op jit(solution)/shard_map/fill_blocks/pallas_call | solution.py:646
  4.3 0.0 copy-start
  4.3 7.0 %all-to-all-start = ((f32[8,48,128]{2,1,0:T(8,128)}), f32[8,48,128]{2,1,0:T(8,128)S(1)}, u32[]{:S(2)}, u32[]{:S(2)}) async-start(f32[8,48,128]{2,1,0:T(8,128)} %fill_blocks.1), calls=%async_computation | async-start | bytes 393216 | tf_op jit(solution)/shard_map/all_to_all | solution.py:653
  11.3 0.0 copy-done
  11.3 5.1 %interior.1.refs_1_ = f32[188,128]{1,0:T(8,128)S(1)} custom-call(f32[512,128]{1,0:T(8,128)S(1)} %get-tuple-element.53.refs_0_.refs_2_, f32[32,128]{1,0:T(8,128)S(1)} %collective-permute-done.refs_2_.refs_1_, bf16[2048,64]{1,0:T(8,128)(2,1)S(1)} %get-tuple-element.46.refs_5_.refs_2_.refs_1_, bf16[256,256]{1,0:T(8,128)(2,1)S(1)} %copy-done, ...), custom_call_target="tpu_custom_call" | custom-call | tf_op jit(solution)/shard_map/interior/pallas_call | solution.py:660
  16.4 0.0 copy-start.1
  16.4 1.6 %collective-permute-start.1 = (f32[188,128]{1,0:T(8,128)S(1)}, f32[188,128]{1,0:T(8,128)S(1)}, u32[]{:S(2)}, u32[]{:S(2)}) collective-permute-start(f32[188,128]{1,0:T(8,128)S(1)} %interior.1.refs_1_), channel_id=1, source_target_pairs={{0,16},{16,0},{1,17},{17,1},{2,18},{18,2},{3,19},{19,3},{4,20},{20... | collective-permute-start | bytes 288776 | tf_op jit(solution)/shard_map/ppermute | solution.py:670
  17.9 1.8 %middle.1.refs_3_ = f32[80,128]{1,0:T(8,128)S(1)} custom-call(f32[512,128]{1,0:T(8,128)S(1)} %get-tuple-element.53.refs_0_.refs_2_, bf16[2048,64]{1,0:T(8,128)(2,1)S(1)} %get-tuple-element.46.refs_5_.refs_2_.refs_1_, bf16[256,256]{1,0:T(8,128)(2,1)S(1)} %copy-done, f32[256,128]{1,0:T(8,128)S(1)} %get-tuple-element.47.refs_7_.refs_4_.refs_3_, ...), custom_call_target="tpu_custom_call" | custom-call | tf_op jit(solution)/shard_map/middle/pallas_call | solution.py:673
  19.8 0.0 all-to-all-done.refs_0_
  19.8 0.0 copy-done.1
  19.8 1.9 %edges.1 = (f32[384,128]{1,0:T(8,128)S(1)}, f32[6,128]{1,0:T(8,128)S(1)}, f32[6,128]{1,0:T(8,128)S(1)}) custom-call(f32[8,48,128]{2,1,0:T(8,128)S(1)} %all-to-all-done.refs_0_, f32[32,128]{1,0:T(8,128)S(1)} %collective-permute-done.refs_2_.refs_1_, f32[512,128]{1,0:T(8,128)S(1)} %get-tuple-element.53.refs_0_.refs_2_, ...), custom_call_target="tpu_custom_call" | custom-call | tf_op jit(solution)/shard_map/edges/pallas_call | solution.py:702
  21.7 0.0 collective-permute-done.1.refs_2_
  21.7 0.7 %combine.1 = (f32[192,128]{1,0:T(8,128)}, f32[192,128]{1,0:T(8,128)}, f32[6,128]{1,0:T(8,128)}, f32[6,128]{1,0:T(8,128)}) custom-call(f32[384,128]{1,0:T(8,128)S(1)} %get-tuple-element.52.refs_0_, f32[188,128]{1,0:T(8,128)S(1)} %interior.1.refs_1_, f32[188,128]{1,0:T(8,128)S(1)} %collective-permute-done.1.refs_2_, f32[80,128]{1,0:T(8,128)S(1)} %middle.1.refs_3_, ...), custom_call_target="tpu_custom_call" | custom-call | tf_op jit(solution)/shard_map/combine/pallas_call | solution.py:711
Async XLA Ops:
  1.8 1.6 %collective-permute-start = (f32[32,128]{1,0:T(8,128)S(1)}, f32[32,128]{1,0:T(8,128)S(1)}, u32[]{:S(2)}, u32[]{:S(2)}) collective-permute-start(f32[32,128]{1,0:T(8,128)S(1)} %get-tuple-element.44), channel_id=1, source_target_pairs={{0,1},{1,0},{2,3},{3,2},{4,5},{5,4},{6,7},{7,6},{8,9},{9,8},{10,11... | collective-permute-start | bytes 49160 | tf_op jit(solution)/shard_map/ppermute | solution.py:623
  4.3 7.0 %copy-start = (bf16[256,256]{1,0:T(8,128)(2,1)S(1)}, bf16[256,256]{1,0:T(8,128)(2,1)}, u32[]{:S(2)}) copy-start(bf16[256,256]{1,0:T(8,128)(2,1)} %refs_2_.3) | copy-start | bytes 393220
  4.3 15.5 %all-to-all-start = ((f32[8,48,128]{2,1,0:T(8,128)}), f32[8,48,128]{2,1,0:T(8,128)S(1)}, u32[]{:S(2)}, u32[]{:S(2)}) async-start(f32[8,48,128]{2,1,0:T(8,128)} %fill_blocks.1), calls=%async_computation | async-start | bytes 393216 | tf_op jit(solution)/shard_map/all_to_all | solution.py:653
  16.4 3.4 %copy-start.1 = (f32[6,32,128]{2,1,0:T(8,128)S(1)}, f32[6,32,128]{2,1,0:T(8,128)}, u32[]{:S(2)}) copy-start(f32[6,32,128]{2,1,0:T(8,128)} %param.15) | copy-start | bytes 294916
  16.4 5.4 %collective-permute-start.1 = (f32[188,128]{1,0:T(8,128)S(1)}, f32[188,128]{1,0:T(8,128)S(1)}, u32[]{:S(2)}, u32[]{:S(2)}) collective-permute-start(f32[188,128]{1,0:T(8,128)S(1)} %interior.1.refs_1_), channel_id=1, source_target_pairs={{0,16},{16,0},{1,17},{17,1},{2,18},{18,2},{3,19},{19,3},{4,20},{20... | collective-permute-start | bytes 288776 | tf_op jit(solution)/shard_map/ppermute | solution.py:670
